TPU v7x, 128 devices: a whole 4x4x4 slice. The times are simulated.
128 devices in a mesh: pencil: 128 (over x, y, z, core).
Axes of the slice: x: 4, y: 4, z: 4, core: 2. Of those that a mesh axis runs over, the one named last changes fastest.
Arguments:
- coefficients: float32 [2, 8, 16384, 128], P(None, None, 'pencil'), may hold values from -6 to 6
- potential: float32 [256, 256, 256], P('pencil'), may hold values from -5 to 5
- slot_atom: int32 [8192], P('pencil'), may hold values from 0 to 2047, as said below
- slot_count: int32 [128], P('pencil'), may hold values from 8 to 64, as said below
- point_offset: int32 [8192, 256], P('pencil'), may hold values from 0 to 131071
- proj_value: float32 [8192, 8, 256], P('pencil'), may hold values from -0.7 to 0.7
- proj_strength: float32 [2048, 8], replicated, may hold values from 0.5 to 4
- proj_count: int32 [2048], replicated, may hold values from 1 to 8
Outputs:
- applied_coefficients: float32 [2, 8, 16384, 128], P(None, None, 'pencil')
- projections: float32 [2048, 128], P('pencil')
Inputs may be any that keep to these rules, and one draw needn't show every extreme that they name: `slot_atom`: the home block of atom a is a // 16; the atom of every slot of block d has its home block within 2 of d modulo the number of blocks, so (a // 16 - d) modulo the number of blocks is at most 2 or at least the number of blocks minus 2. `slot_count`: some block uses all 64 slots.
All inputs are finite; a program needn't handle non-finite values.
Results may differ from a plain program's by a relative error of at most 0.00011.
Values sent between devices are 32-bit elements; how exact they have to be, the bound alone decides.
No kernel may reach another device: no remote copies, remote signals or barrier semaphores. Data moves between devices by JAX's collectives and lax.ppermute only.
A program may use at most 256 MiB of HBM per device.

v0:
```python
import math

import jax
import jax.numpy as jnp
from jax import lax
from jax.sharding import PartitionSpec as P

GRID_SIDE = 256
WAVE_CUTOFF = 128
NPROJ = 8
REACH = 2


def passed_along(block, axis, distance):
    devices = range(lax.axis_size(axis))
    route = [((i - distance) % len(devices), i) for i in devices]
    return lax.ppermute(block, axis, route)


def phase_tables():
    frequency = jnp.arange(WAVE_CUTOFF, dtype=jnp.int32) - WAVE_CUTOFF // 2
    points = jnp.arange(GRID_SIDE, dtype=jnp.int32)
    turn_count = frequency[:, None] * points[None, :] % GRID_SIDE
    phase_angles = 2.0 * math.pi / GRID_SIDE * turn_count.astype(jnp.float32)
    return (jnp.cos(phase_angles), jnp.sin(phase_angles))


def complex_step(real_part, imag_part, full_pattern, table, factor):
    stacked = jnp.stack([real_part, imag_part])
    result = jnp.einsum(full_pattern, stacked, table, precision=lax.Precision.HIGHEST)
    return (factor * result[0], factor * result[1])


def forward_dim(real_part, imag_part, full_pattern, cosine_lookup, sine_lookup, factor):
    table = jnp.stack(
        [jnp.stack([cosine_lookup, sine_lookup]), jnp.stack([-sine_lookup, cosine_lookup])]
    )
    return complex_step(real_part, imag_part, full_pattern, table, factor)


def backward_dim(real_part, imag_part, full_pattern, cosine_lookup, sine_lookup, factor):
    table = jnp.stack(
        [jnp.stack([cosine_lookup, -sine_lookup]), jnp.stack([sine_lookup, cosine_lookup])]
    )
    return complex_step(real_part, imag_part, full_pattern, table, factor)


def columns_to_planes(band_amplitudes, cosine_lookup, sine_lookup):
    real_part, imag_part = forward_dim(
        band_amplitudes[0],
        band_amplitudes[1],
        "rchw,rowa->ocah",
        cosine_lookup,
        sine_lookup,
        WAVE_CUTOFF ** (-0.5),
    )
    return jnp.stack([real_part, imag_part])


def planes_to_grid(incoming_pieces, cosine_lookup, sine_lookup):
    shape_now = incoming_pieces.shape
    real_part = incoming_pieces[0].reshape(shape_now[1], shape_now[2], WAVE_CUTOFF, WAVE_CUTOFF)
    imag_part = incoming_pieces[1].reshape(shape_now[1], shape_now[2], WAVE_CUTOFF, WAVE_CUTOFF)
    real_part, imag_part = forward_dim(
        real_part, imag_part, "rbzkj,rojy->obzky", cosine_lookup, sine_lookup, WAVE_CUTOFF ** (-0.5)
    )
    return forward_dim(
        real_part, imag_part, "rbzky,rokx->obzyx", cosine_lookup, sine_lookup, WAVE_CUTOFF ** (-0.5)
    )


def grid_to_planes(real_part, imag_part, cosine_lookup, sine_lookup):
    real_part, imag_part = backward_dim(
        real_part, imag_part, "rbzyx,rokx->obzyk", cosine_lookup, sine_lookup, GRID_SIDE ** (-0.5)
    )
    real_part, imag_part = backward_dim(
        real_part, imag_part, "rbzyk,rojy->obzkj", cosine_lookup, sine_lookup, GRID_SIDE ** (-0.5)
    )
    shape_now = real_part.shape
    return jnp.stack(
        [
            real_part.reshape(shape_now[0], shape_now[1], WAVE_CUTOFF * WAVE_CUTOFF),
            imag_part.reshape(shape_now[0], shape_now[1], WAVE_CUTOFF * WAVE_CUTOFF),
        ]
    )


def planes_to_columns(incoming_pieces, cosine_lookup, sine_lookup):
    real_part, imag_part = backward_dim(
        incoming_pieces[0],
        incoming_pieces[1],
        "runv,rotn->ouvt",
        cosine_lookup,
        sine_lookup,
        GRID_SIDE ** (-0.5),
    )
    return jnp.stack([real_part, imag_part])


def per_device(
    coefficients,
    potential,
    slot_atom,
    slot_count,
    point_offset,
    proj_value,
    proj_strength,
    proj_count,
):
    highest = lax.Precision.HIGHEST
    cosine_lookup, sine_lookup = phase_tables()
    device = lax.axis_index("pencil")
    devices_all = lax.axis_size("pencil")
    band_total = coefficients.shape[1]
    column_local = coefficients.shape[2]
    incoming_pieces = lax.all_to_all(
        columns_to_planes(coefficients, cosine_lookup, sine_lookup),
        "pencil",
        split_axis=2,
        concat_axis=3,
        tiled=True,
    )
    real_field, imag_field = planes_to_grid(incoming_pieces, cosine_lookup, sine_lookup)
    plane_local = real_field.shape[1]
    field_row_values = 2 * band_total
    fields = jnp.stack([real_field, imag_field]).reshape(
        field_row_values, plane_local * GRID_SIDE * GRID_SIDE
    )
    coeff_width = field_row_values * NPROJ
    slot_local = slot_atom.shape[0]
    used_total = slot_count[0]
    groups_live = (used_total + 7) // 8

    def gather_group(group_index, coeffs):
        first_slot = group_index * 8
        offsets = lax.dynamic_slice_in_dim(point_offset, first_slot, 8, 0)
        values = lax.dynamic_slice_in_dim(proj_value, first_slot, 8, 0)
        live_slot = first_slot + jnp.arange(8, dtype=jnp.int32) < used_total
        picked = fields[:, offsets]
        slot_terms = jnp.einsum("mst,spt->smp", picked, values, precision=highest)
        slot_terms = jnp.where(live_slot[:, None, None], slot_terms, 0.0).reshape(8, coeff_width)
        return lax.dynamic_update_slice_in_dim(coeffs, slot_terms, first_slot, 0)

    coeffs = lax.fori_loop(
        0, groups_live, gather_group, jnp.zeros((slot_local, coeff_width), jnp.float32)
    )
    atom_total = proj_strength.shape[0]
    atom_dev = atom_total // devices_all
    column_proj = jnp.arange(coeff_width, dtype=jnp.int32) % NPROJ
    proj_mask_all = column_proj[None, :] < proj_count[:, None]
    strength_all = jnp.tile(proj_strength, (1, field_row_values))
    window_size = 2 * REACH + 1
    home_block = slot_atom // atom_dev
    relative = (home_block - device + REACH) % devices_all
    window_index = relative * atom_dev + slot_atom % atom_dev
    onehot = (
        window_index[:, None] == jnp.arange(window_size * atom_dev, dtype=jnp.int32)[None, :]
    ).astype(jnp.float32)
    partial_sum = jnp.dot(onehot.T, coeffs, precision=highest).reshape(
        window_size, atom_dev, coeff_width
    )
    mask_home = lax.dynamic_slice_in_dim(proj_mask_all, device * atom_dev, atom_dev, 0)
    strength_home = lax.dynamic_slice_in_dim(strength_all, device * atom_dev, atom_dev, 0)
    totals = partial_sum[REACH]
    for offset in range(-REACH, REACH + 1):
        if offset != 0:
            totals = totals + passed_along(partial_sum[REACH + offset], "pencil", offset)
    becp_home = jnp.where(mask_home, totals, 0.0)
    energy_home = becp_home * strength_home
    pieces = []
    for offset in range(-REACH, REACH + 1):
        if offset == 0:
            pieces.append(energy_home)
        else:
            pieces.append(passed_along(energy_home, "pencil", -offset))
    window = jnp.concatenate(pieces, 0)
    slot_energy = jnp.dot(onehot, window, precision=highest)

    def apply_group(group_index, projected):
        first_slot = group_index * 8
        offsets = lax.dynamic_slice_in_dim(point_offset, first_slot, 8, 0)
        values = lax.dynamic_slice_in_dim(proj_value, first_slot, 8, 0)
        live_slot = first_slot + jnp.arange(8, dtype=jnp.int32) < used_total
        energy = lax.dynamic_slice_in_dim(slot_energy, first_slot, 8, 0).reshape(
            8, field_row_values, NPROJ
        )
        energy = jnp.where(live_slot[:, None, None], energy, 0.0)
        slot_terms = jnp.einsum("smp,spt->mst", energy, values, precision=highest)
        return projected.at[:, offsets].add(slot_terms)

    projected = lax.fori_loop(0, groups_live, apply_group, jnp.zeros_like(fields))
    applied = potential.reshape(1, -1) * fields + projected
    applied = applied.reshape(2, band_total, plane_local, GRID_SIDE, GRID_SIDE)
    incoming_pieces = lax.all_to_all(
        grid_to_planes(applied[0], applied[1], cosine_lookup, sine_lookup),
        "pencil",
        split_axis=3,
        concat_axis=2,
        tiled=True,
    )
    transformed = planes_to_columns(incoming_pieces, cosine_lookup, sine_lookup)
    columns = device * column_local + jnp.arange(column_local, dtype=jnp.int32)
    freq_x = columns // WAVE_CUTOFF - WAVE_CUTOFF // 2
    freq_y = columns % WAVE_CUTOFF - WAVE_CUTOFF // 2
    freq_z = jnp.arange(WAVE_CUTOFF, dtype=jnp.int32) - WAVE_CUTOFF // 2
    squared = (freq_x * freq_x + freq_y * freq_y)[:, None] + (freq_z * freq_z)[None, :]
    kinetic = 6.0 / (WAVE_CUTOFF * WAVE_CUTOFF) * squared.astype(jnp.float32)
    applied_coefficients = transformed + kinetic[None, None] * coefficients
    return (applied_coefficients, becp_home)


def solution(mesh):
    in_specs = (
        P(None, None, "pencil", None),
        P("pencil", None, None),
        P("pencil"),
        P("pencil"),
        P("pencil", None),
        P("pencil", None, None),
        P(),
        P(),
    )
    out_specs = (P(None, None, "pencil", None), P("pencil", None))
    return jax.shard_map(
        per_device, mesh=mesh, in_specs=in_specs, out_specs=out_specs, check_vma=False
    )
```

profile of v0, /device:TPU:1, one launch (start us, length us, event | category | flops | bytes accessed | tf_op | source)
XLA Modules:
  0.0 1233.9 jit_solution(4582404144399266949)
XLA Ops:
  1.3 3.1 convolution_bitcast_fusion.1
  4.8 2.6 copy.101
  7.4 11.7 all-to-all-start
  20.0 29.4 %all-to-all-done = f32[2,8,256,128]{3,1,0,2:T(8,128)S(1)} async-done(((f32[2,8,256,128]{3,1,0,2:T(8,128)}), f32[2,8,256,128]{3,1,0,2:T(8,128)S(1)}, u32[]{:S(2)}, u32[]{:S(2)}) %all-to-all-start) | async-done | bytes 2097184 | tf_op jit(solution)/shard_map/all_to_all | solution.py:116
  49.4 4.5 convolution_bitcast_fusion
  54.5 8.1 fusion.25
  62.6 1.2 slice_multiply_fusion.1
  63.8 3.8 pad_maximum_fusion
  67.6 8.7 copy.105
  76.3 6.2 reshape.280
  82.5 31.4 %copy.106 = f32[16,131072]{0,1:T(8,128)} copy(f32[16,131072]{1,0:T(8,128)} %reshape.280) | data formatting | bytes 16777216 | tf_op jit(solution)/shard_map/while | solution.py:144
  113.9 70.6 %while.20 = (s32[]{:T(128)}, f32[64,128]{1,0:T(8,128)S(1)}, s32[]{:T(128)}, s32[]{:T(128)}, s32[64,256]{1,0:T(8,128)}, /*index=5*/f32[16,131072]{0,1:T(8,128)}, ...) while((s32[]{:T(128)}, f32[64,128]{1,0:T(8,128)S(1)}, s32[]{:T(128)}, ...), condition=%wide.region_1.2_spmd, body=%wide.region_0.1_spmd.sunk | while | flops 3154966 | bytes 807103 | solution.py:144
  113.9 0.8 fusion.97
  114.7 20.5 %gather_fusion = f32[2048,16]{1,0:T(8,128)S(1)} fusion(f32[16,131072]{0,1:T(8,128)} %get-tuple-element.302, s32[2048]{0:T(1024)S(1)} %broadcast_clamp_fusion.4), kind=kCustom, calls=%fused_computation.clone.1 | custom fusion | bytes 270336 | tf_op jit(solution)/shard_map/while/body/gather | solution.py:139
  136.2 1.1 convolution_select_fusion.2
  137.5 0.7 fusion.97
  138.2 20.5 %gather_fusion = f32[2048,16]{1,0:T(8,128)S(1)} fusion(f32[16,131072]{0,1:T(8,128)} %get-tuple-element.302, s32[2048]{0:T(1024)S(1)} %broadcast_clamp_fusion.4), kind=kCustom, calls=%fused_computation.clone.1 | custom fusion | bytes 270336 | tf_op jit(solution)/shard_map/while/body/gather | solution.py:139
  159.7 1.1 convolution_select_fusion.2
  161.0 0.7 fusion.97
  161.8 20.5 %gather_fusion = f32[2048,16]{1,0:T(8,128)S(1)} fusion(f32[16,131072]{0,1:T(8,128)} %get-tuple-element.302, s32[2048]{0:T(1024)S(1)} %broadcast_clamp_fusion.4), kind=kCustom, calls=%fused_computation.clone.1 | custom fusion | bytes 270336 | tf_op jit(solution)/shard_map/while/body/gather | solution.py:139
  183.2 1.1 convolution_select_fusion.2
  184.8 1.4 collective-permute-start
  186.3 24.9 %collective-permute-start.1 = (f32[16,128]{1,0:T(8,128)S(1)}, f32[16,128]{1,0:T(8,128)S(1)}, u32[]{:S(2)}, u32[]{:S(2)}) collective-permute-start(f32[16,128]{1,0:T(8,128)S(1)} %get-tuple-element.177), channel_id=1, source_target_pairs={{1,0},{2,1},{3,2},{4,3},{5,4},{6,5},{7,6},{8,7},{9,8},{10,9},{11,1... | collective-permute-start | bytes 24584 | tf_op jit(solution)/shard_map/ppermute | solution.py:17
  211.3 0.8 dynamic-slice
  212.4 6.9 collective-permute-done.3
  220.0 1.0 fusion.45
  221.4 1.5 collective-permute-start.6
  222.9 7.2 collective-permute-start.7
  230.2 0.7 collective-permute-done.7
  231.1 21.0 %broadcast_in_dim.47 = f32[16,131072]{0,1:T(8,128)} broadcast(f32[]{:T(128)} %constant.136.clone.1), dimensions={} | broadcast | bytes 8388612 | tf_op jit(solution)/shard_map/broadcast_in_dim | solution.py:191
  252.2 220.1 %while.21 = (s32[]{:T(128)}, f32[16,131072]{0,1:T(8,128)}, s32[]{:T(128)}, s32[64,256]{1,0:T(8,128)}, f32[64,8,256]{2,1,0:T(8,128)}, /*index=5*/s32[]{:T(128)}, ...) while((s32[]{:T(128)}, f32[16,131072]{0,1:T(8,128)}, s32[]{:T(128)}, ...), condition=%wide.region_4.5_spmd, body=%wide.region_2.4_spmd.sunk | while | flops 3210262 | bytes 8695999 | solution.py:191
  252.9 2.8 fusion.103
  255.7 0.7 fusion.102
  256.4 4.4 sort.2
  260.9 64.6 %scatter_custom_fusion.5 = f32[16,131072]{0,1:T(8,128)} fusion(f32[16,131072]{0,1:T(8,128)} %get-tuple-element.320, s32[2048]{0:T(1024)S(1)} %get-tuple-element.273, f32[2048,16]{1,0:T(8,128)S(1)} %bitcast.143, s32[2048]{0:T(1024)S(1)} %broadcast_clamp_fusion.5), kind=kCustom, calls=%fused_computation.12.clone.1 | custom fusion | flops 32768 | bytes 8388608 | tf_op jit(solution)/shard_map/while/body/scatter-add | solution.py:189
  326.2 2.8 fusion.103
  329.0 0.7 fusion.102
  329.7 4.4 sort.2
  334.2 64.6 %scatter_custom_fusion.5 = f32[16,131072]{0,1:T(8,128)} fusion(f32[16,131072]{0,1:T(8,128)} %get-tuple-element.320, s32[2048]{0:T(1024)S(1)} %get-tuple-element.273, f32[2048,16]{1,0:T(8,128)S(1)} %bitcast.143, s32[2048]{0:T(1024)S(1)} %broadcast_clamp_fusion.5), kind=kCustom, calls=%fused_computation.12.clone.1 | custom fusion | flops 32768 | bytes 8388608 | tf_op jit(solution)/shard_map/while/body/scatter-add | solution.py:189
  399.5 2.8 fusion.103
  402.3 0.7 fusion.102
  403.1 4.4 sort.2
  407.5 64.6 %scatter_custom_fusion.5 = f32[16,131072]{0,1:T(8,128)} fusion(f32[16,131072]{0,1:T(8,128)} %get-tuple-element.320, s32[2048]{0:T(1024)S(1)} %get-tuple-element.273, f32[2048,16]{1,0:T(8,128)S(1)} %bitcast.143, s32[2048]{0:T(1024)S(1)} %broadcast_clamp_fusion.5), kind=kCustom, calls=%fused_computation.12.clone.1 | custom fusion | flops 32768 | bytes 8388608 | tf_op jit(solution)/shard_map/while/body/scatter-add | solution.py:189
  472.3 36.3 %copy.108 = f32[16,131072]{1,0:T(8,128)} copy(f32[16,131072]{0,1:T(8,128)} %get-tuple-element.79) | data formatting | bytes 16777216 | tf_op jit(solution)/shard_map/while | solution.py:191
  508.6 10.1 multiply_add_fusion
  518.7 4.0 fusion.81
  522.7 1.4 copy.151
  524.0 1.4 copy.152
  525.4 13.6 %fusion.26 = f32[2,8,2,256,128]{3,4,2,1,0:T(8,128)S(1)} fusion(f32[1,8,2,256,256]{4,3,0,2,1:T(8,128)S(1)} %bitcast.145, f32[1,8,2,256,256]{4,3,0,2,1:T(8,128)S(1)} %bitcast.144, f32[2,2,128,256,1,1]{2,3,1,0,5,4:T(8,128)S(1)} %copy-done.3), kind=kOutput, calls=%fused_computation.42 | convolution fusion | flops 6444548096 | bytes 13107200 | tf_op jit(solution)/shard_map/rbzyx,rokx->obzyk/dot_general | solution.py:30
  539.5 7.2 fusion.32
  547.2 1.3 copy.113
  548.5 3.1 pad_maximum_fusion.2
  551.6 33.0 %copy.114 = f32[2,8,2,16384]{1,2,0,3:T(2,128)} copy(f32[2,8,2,16384]{3,0,2,1:T(2,128)S(1)} %pad_maximum_fusion.2) | data formatting | bytes 4194304 | tf_op jit(solution)/shard_map/stack | solution.py:80
  584.6 55.7 %reshape.320 = f32[128,1,4096]{2,1,0:T(1,128)} reshape(f32[16384,2,2,8]{3,2,1,0:T(2,128)} %bitcast.140) | data formatting | bytes 4194304
  640.3 461.3 %all-to-all-start.1 = ((f32[128,1,4096]{2,1,0:T(1,128)}), f32[128,1,4096]{2,1,0:T(1,128)S(1)}, u32[]{:S(2)}, u32[]{:S(2)}) async-start(f32[128,1,4096]{2,1,0:T(1,128)} %reshape.320), calls=%async_computation.1 | async-start | bytes 4194304 | tf_op jit(solution)/shard_map/all_to_all | solution.py:194
  1101.6 1.3 copy.117
  1103.0 29.0 %all-to-all-done.1 = f32[128,1,4096]{2,1,0:T(1,128)S(1)} async-done(((f32[128,1,4096]{2,1,0:T(1,128)}), f32[128,1,4096]{2,1,0:T(1,128)S(1)}, u32[]{:S(2)}, u32[]{:S(2)}) %all-to-all-start.1) | async-done | bytes 2097184 | tf_op jit(solution)/shard_map/all_to_all | solution.py:194
  1132.0 1.3 copy-done.2
  1133.9 7.4 reduce
  1141.3 52.1 %reshape.321 = f32[16384,2,2,8]{3,2,1,0:T(2,128)} reshape(f32[128,4096]{1,0:T(8,128)S(1)} %reduce) | data formatting | bytes 4194304
  1193.3 35.9 %copy.115 = f32[2,8,2,128,128]{4,2,3,1,0:T(2,128)S(1)} copy(f32[2,8,2,128,128]{1,2,0,4,3:T(2,128)} %bitcast.141) | data formatting | bytes 4194304 | tf_op jit(solution)/shard_map/all_to_all | solution.py:194
  1229.4 0.9 copy-done.6
  1230.3 1.9 fusion.35
  1232.4 1.3 copy.118
  (96 shorter events, 11.5 us)
Async XLA Ops:
  0.6 19.1 %copy-start = (f32[2048,8]{0,1:T(8,128)S(1)}, f32[2048,8]{0,1:T(8,128)}, u32[]{:S(2)}) copy-start(f32[2048,8]{0,1:T(8,128)} %param.18) | copy-start | bytes 196612
  4.8 15.1 %copy-start.8 = (s32[64]{0:T(128)S(1)}, s32[64]{0:T(128)}, u32[]{:S(2)}) copy-start(s32[64]{0:T(128)} %param.14) | copy-start | bytes 772
  7.4 42.0 %all-to-all-start = ((f32[2,8,256,128]{3,1,0,2:T(8,128)}), f32[2,8,256,128]{3,1,0,2:T(8,128)S(1)}, u32[]{:S(2)}, u32[]{:S(2)}) async-start(f32[2,8,256,128]{3,1,0,2:T(8,128)} %copy.101), calls=%async_computation | async-start | bytes 4194304 | tf_op jit(solution)/shard_map/all_to_all | solution.py:116
  113.9 107.2 %copy-start.7 = (f32[2,256,256]{2,1,0:T(8,128)S(1)}, f32[2,256,256]{2,1,0:T(8,128)}, u32[]{:S(2)}) copy-start(f32[2,256,256]{2,1,0:T(8,128)} %param.13) | copy-start | bytes 1572868
  184.8 27.2 %collective-permute-start = (f32[16,128]{1,0:T(8,128)S(1)}, f32[16,128]{1,0:T(8,128)S(1)}, u32[]{:S(2)}, u32[]{:S(2)}) collective-permute-start(f32[16,128]{1,0:T(8,128)S(1)} %get-tuple-element.174), channel_id=1, source_target_pairs={{2,0},{3,1},{4,2},{5,3},{6,4},{7,5},{8,6},{9,7},{10,8},{11,9},{12,... | collective-permute-start | bytes 24584 | tf_op jit(solution)/shard_map/ppermute | solution.py:17
  186.3 25.8 %collective-permute-start.1 = (f32[16,128]{1,0:T(8,128)S(1)}, f32[16,128]{1,0:T(8,128)S(1)}, u32[]{:S(2)}, u32[]{:S(2)}) collective-permute-start(f32[16,128]{1,0:T(8,128)S(1)} %get-tuple-element.177), channel_id=1, source_target_pairs={{1,0},{2,1},{3,2},{4,3},{5,4},{6,5},{7,6},{8,7},{9,8},{10,9},{11,1... | collective-permute-start | bytes 24584 | tf_op jit(solution)/shard_map/ppermute | solution.py:17
  211.2 1.2 collective-permute-start.2
  211.2 8.1 collective-permute-start.3
  220.0 10.1 collective-permute-start.4
  221.3 8.8 collective-permute-start.5
  221.4 8.8 collective-permute-start.6
  222.9 8.0 collective-permute-start.7
  524.0 1.4 copy-start.3
  640.3 461.3 %copy-start.4 = (f32[2,8,128,128]{3,2,1,0:T(8,128)S(1)}, f32[2,8,128,128]{3,2,1,0:T(8,128)}, u32[]{:S(2)}) copy-start(f32[2,8,128,128]{3,2,1,0:T(8,128)} %param.12) | copy-start | bytes 3145732
  640.3 491.7 %all-to-all-start.1 = ((f32[128,1,4096]{2,1,0:T(1,128)}), f32[128,1,4096]{2,1,0:T(1,128)S(1)}, u32[]{:S(2)}, u32[]{:S(2)}) async-start(f32[128,1,4096]{2,1,0:T(1,128)} %reshape.320), calls=%async_computation.1 | async-start | bytes 4194304 | tf_op jit(solution)/shard_map/all_to_all | solution.py:194
  1132.0 1.3 copy-start.2
  1229.2 1.0 copy-start.6
  1229.2 3.0 copy-start.5
  1230.3 3.5 copy-start.1
where the time goes:
time: 1240 us; the launch traced here: 1230 us
  starting transfers between devices  508 us (41%)
  local copies, waits for them, and re-layouts  361 us (29%)
  other arithmetic  245 us (20%)
  waiting for transfers between devices  66.4 us (5%)
  matrix products  50.5 us (4%)
    all_to_all x1, starting transfers between devices, per_device(): lax.all_to_all(grid_to_planes(applied[0], applied[1], cosine_lookup, sine...  461 us
    scatter-add x9, other arithmetic, apply_group(): return projected.at[:, offsets].add(slot_terms)  207 us
    unnamed x30, local copies, waits for them, and re-layouts  116 us
    gather x6, local copies, waits for them, and re-layouts, gather_group(): picked = fields[:, offsets]  62.5 us
    dot_general x6, matrix products, complex_step(): jnp.einsum(full_pattern, stacked, table, precision=lax.Precision.HIGHEST)  38.4 us
    all_to_all x2, local copies, waits for them, and re-layouts, per_device(): lax.all_to_all(grid_to_planes(applied[0], applied[1], cosine_lookup, sine...  36.4 us
    while x1, local copies, waits for them, and re-layouts, per_device(): lax.fori_loop(0, groups_live, apply_group, jnp.zeros_like(fields))  36.3 us
    ppermute x8, starting transfers between devices, passed_along(): return lax.ppermute(block, axis, route)  35.2 us
  transfers between devices with their start and end apart: 10, of which 5 were waited for; matrix products, arithmetic and copies ran while one was open for 0% of the time, Pallas kernels for 0%

commit v1 on v0

v1 whole, which is shorter than its diff:
```python
import jax
import jax.numpy as jnp
import ml_dtypes
import numpy as np
from jax import lax
from jax.experimental import pallas as pl
from jax.experimental.pallas import tpu as pltpu
from jax.sharding import PartitionSpec as P

GRID = 256
CUT = 128
NPROJ = 8
REACH = 2
BANDS = 8
SLOTS = 64
NPTS = 256
ROWS = 16384
WINDOW = 2 * REACH + 1
F32 = jnp.float32
BF16 = jnp.bfloat16
VMEM_LIMIT = 56 * 1024 * 1024


def halves(table):
    table = np.asarray(table, np.float64)
    high = table.astype(np.float32).astype(ml_dtypes.bfloat16)
    low = (table - high.astype(np.float64)).astype(np.float32).astype(ml_dtypes.bfloat16)
    return high, low


def make_tables():
    freq = np.arange(CUT) - CUT // 2
    turns = (freq[:, None] * np.arange(GRID)[None, :]) % GRID
    cos = np.cos(2 * np.pi * turns / GRID)
    sin = np.sin(2 * np.pi * turns / GRID)
    up = CUT ** -0.5
    down = GRID ** -0.5
    planes = np.concatenate([np.arange(0, GRID, 2), np.arange(1, GRID, 2)])
    cz, sz = cos[:, planes], sin[:, planes]
    fz = up * np.block([[cz.T, -sz.T], [sz.T, cz.T]])
    fy = up * np.block([[cos, sin], [-sin, cos]])
    fx = up * np.concatenate([cos.T, sin.T], 1)
    bx = down * np.concatenate([cos, sin], 0)
    by = down * np.block([[cos.T, -sin.T], [sin.T, cos.T]])
    bz = down * np.block([[cz.T, -sz.T], [sz.T, cz.T]])
    return {k: halves(v) for k, v in dict(fz=fz, fy=fy, fx=fx, bx=bx, by=by, bz=bz).items()}


TABLES = make_tables()


def split(value):
    high = value.astype(BF16)
    low = (value - high.astype(F32)).astype(BF16)
    return high, low


def mm(a, b):
    return lax.dot_general(a, b, (((1,), (0,)), ((), ())), preferred_element_type=F32)


def mm_nt(a, b):
    return lax.dot_general(a, b, (((1,), (1,)), ((), ())), preferred_element_type=F32)


def mm_tn(a, b):
    return lax.dot_general(a, b, (((0,), (0,)), ((), ())), preferred_element_type=F32)


def lane_iota(shape):
    return lax.broadcasted_iota(jnp.int32, shape, len(shape) - 1)


def exchange_blocks(arrays):
    rows = arrays[0].shape[0]
    block = lane_iota((rows, 128)) // 8
    rolled = [pltpu.roll(a, 8 * i, 1) if i else a for i, a in enumerate(arrays)]
    vals = [rolled[(-n) % 16] for n in range(16)]
    for bit in range(4):
        step = 1 << bit
        chosen = (block // step) % 2 == 1
        vals = [jnp.where(chosen, vals[(j - step) % 16], vals[j]) for j in range(16)]
    return [pltpu.roll(v, (128 - 8 * j) % 128, 1) if j else v for j, v in enumerate(vals)]


def swap_parts(value, first_sign):
    rolled = pltpu.roll(value, 64, 1)
    first = lane_iota(value.shape) < 64
    return jnp.where(first, first_sign * rolled, -first_sign * rolled)


def block_ones():
    row = lax.broadcasted_iota(jnp.int32, (128, 128), 0) // 8
    col = lax.broadcasted_iota(jnp.int32, (128, 128), 1) // 8
    return (row == col).astype(F32)


def three(value):
    a = value.astype(BF16)
    rest = value - a.astype(F32)
    b = rest.astype(BF16)
    c = (rest - b.astype(F32)).astype(BF16)
    return a, b, c


def exact_times_ones(value, ones):
    ones = ones.astype(BF16)
    a, b, c = three(value)
    return mm(a, ones) + mm(b, ones) + mm(c, ones)


def slot_weights(values, groups):
    return jnp.concatenate([jnp.where(groups == g, values, 0.0) for g in range(8)], 0)


def columns_kernel(coef_ref, th_ref, tl_ref, out_ref):
    th, tl = th_ref[...], tl_ref[...]
    for b in range(BANDS):
        a = jnp.concatenate([coef_ref[0, b], coef_ref[1, b]], 1)
        ah, al = split(a)
        res = mm_nt(th, ah) + mm_nt(tl, ah) + mm_nt(th, al)
        for q in range(4):
            out_ref[pl.ds(q * 8 + b, 128, stride=32), :] = res[q * 128:(q + 1) * 128]


def grid_kernel(
    rows_sm, count_sm,
    recv_ref, pot_ref, value_ref, group_ref, window_ref,
    yh_ref, yl_ref, xh_ref, xl_ref,
    field_hbm, partial_ref,
    ah_s, al_s, ys_s, inh_s, inl_s, u_s, w_s, gat_s, z_s, sem,
):
    yh, yl = yh_ref[...], yl_ref[...]
    piece = lax.broadcasted_iota(jnp.int32, (32, 128), 0)
    pick_group = (lane_iota((32, 128)) % 8 == piece % 8).astype(F32).astype(BF16)
    for zz in range(2):
        for b in range(BANDS):
            for r in range(2):
                part = recv_ref[pl.ds(r * 16 + zz * 8 + b, 128, stride=32), :]
                h, l = split(part)
                ah_s[b * 128:(b + 1) * 128, r * 128:(r + 1) * 128] = h
                al_s[b * 128:(b + 1) * 128, r * 128:(r + 1) * 128] = l
        ah, al = ah_s[...], al_s[...]
        ys_s[...] = mm(ah, yh) + mm(al, yh) + mm(ah, yl)
        for half in range(2):
            def permute(kc, carry, half=half):
                base = pl.multiple_of(kc * 16, 16)
                ins = [
                    ys_s[pl.ds((i % 8) * 128 + base, 16), ((i // 8) * 2 + half) * 128:((i // 8) * 2 + half + 1) * 128]
                    for i in range(16)
                ]
                outs = exchange_blocks(ins)
                for j, v in enumerate(outs):
                    s = swap_parts(v, -1.0)
                    pair = half * 8 + j // 2
                    cols = slice((j % 2) * 128, (j % 2 + 1) * 128)
                    vh, vl = split(v)
                    sh, sl = split(s)
                    inh_s[pair, pl.ds(base, 16), cols] = vh
                    inl_s[pair, pl.ds(base, 16), cols] = vl
                    inh_s[pair, pl.ds(128 + base, 16), cols] = sh
                    inl_s[pair, pl.ds(128 + base, 16), cols] = sl
                return carry

            lax.fori_loop(0, 8, permute, 0)

        def along_x(pair, carry, zz=zz):
            xh, xl = xh_ref[...], xl_ref[...]
            bh, bl = inh_s[pair], inl_s[pair]
            res = mm(xh, bh) + mm(xl, bh) + mm(xh, bl)
            for k in range(2):
                yg = pair * 2 + k
                pot = pot_ref[zz, pl.ds(pl.multiple_of(yg * 8, 8), 8), :]
                pa, pb, pc = three(pot)
                pieces = jnp.concatenate([pa.astype(F32), pb.astype(F32), pc.astype(F32), jnp.zeros((8, 256), F32)], 0)
                spread = mm_tn(pieces.astype(BF16), pick_group)
                u = res[:, k * 128:(k + 1) * 128]
                at = pl.multiple_of((zz * 32 + yg) * 256, 256)
                u_s[pl.ds(at, 256), :] = u
                w_s[pl.ds(at, 256), :] = u * spread
            return carry

        lax.fori_loop(0, 16, along_x, 0)
    out_copy = pltpu.make_async_copy(w_s, field_hbm, sem)
    out_copy.start()

    z_s[...] = jnp.zeros((SLOTS * 8, 128), F32)
    own = lane_iota((64, 128)) % 8 == lax.broadcasted_iota(jnp.int32, (64, 128), 0) // 8

    def one_slot(s, carry):
        def pick(c, carry):
            for k in range(32):
                t = c * 32 + k
                gat_s[pl.ds(t, 1), :] = u_s[pl.ds(rows_sm[s, t], 1), :]
            return carry

        lax.fori_loop(0, 8, pick, 0)
        gh, gl = split(gat_s[...])
        w = slot_weights(value_ref[s], group_ref[pl.ds(s, 1), :])
        wh, wl = split(w)
        prod = mm(jnp.concatenate([wh, wl], 0), jnp.concatenate([gh, gl], 1))
        total = prod[:64, :128] + prod[64:, :128] + prod[:64, 128:]
        total = jnp.where(own, total, 0.0)
        z = total[0:8]
        for g in range(1, 8):
            z = z + total[g * 8:(g + 1) * 8]
        z_s[pl.ds(pl.multiple_of(s * 8, 8), 8), :] = z
        return carry

    lax.fori_loop(0, count_sm[0], one_slot, 0)
    spread = exact_times_ones(z_s[...], block_ones())
    mine = lane_iota((512, 128)) % 8 == lax.broadcasted_iota(jnp.int32, (512, 128), 0) % 8
    slot_terms = jnp.sum(jnp.where(mine, spread, 0.0).reshape(SLOTS, 8, 128), 1)
    onehot = (lax.broadcasted_iota(jnp.int32, (WINDOW * 16, SLOTS), 0) == window_ref[...]).astype(F32).astype(BF16)
    a, b, c = three(slot_terms)
    partial_ref[...] = mm(onehot, a) + mm(onehot, b) + mm(onehot, c)
    out_copy.wait()


def back_kernel(
    rows_sm, count_sm,
    own_ref, p1, p2, p3, p4, m1, m2, m3, m4,
    mask_ref, strength_ref, window_ref, value_ref, group_ref, rowf_ref,
    xh_ref, xl_ref, yh_ref, yl_ref,
    field_hbm,
    out_ref, becp_ref,
    w_s, tot_s, f_s, gat_s, xb_s, ah_s, al_s, sem,
):
    in_copy = pltpu.make_async_copy(field_hbm, w_s, sem)
    in_copy.start()
    tot_s[...] = own_ref[...]
    for delta, ref in ((1, p1), (2, p2), (3, p3), (4, p4)):
        n = (WINDOW - delta) * 16
        tot_s[delta * 16:, :] = tot_s[delta * 16:, :] + ref[...]
    for delta, ref in ((1, m1), (2, m2), (3, m3), (4, m4)):
        n = (WINDOW - delta) * 16
        tot_s[:n, :] = tot_s[:n, :] + ref[...]
    becp = jnp.where(mask_ref[...] > 0.0, tot_s[...], 0.0)
    becp_ref[...] = becp[REACH * 16:(REACH + 1) * 16]
    energy = becp * strength_ref[...]
    onehot = (lax.broadcasted_iota(jnp.int32, (WINDOW * 16, SLOTS), 0) == window_ref[...]).astype(F32).astype(BF16)
    a, b, c = three(energy)
    slot_energy = mm_tn(onehot, a) + mm_tn(onehot, b) + mm_tn(onehot, c)
    mine = lane_iota((512, 128)) % 8 == lax.broadcasted_iota(jnp.int32, (512, 128), 0) % 8
    wide = jnp.broadcast_to(slot_energy[:, None, :], (SLOTS, 8, 128)).reshape(SLOTS * 8, 128)
    f_s[...] = exact_times_ones(jnp.where(mine, wide, 0.0), block_ones())
    own = lane_iota((64, 128)) % 8 == lax.broadcasted_iota(jnp.int32, (64, 128), 0) // 8
    in_copy.wait()

    def one_slot(s, carry):
        w = slot_weights(value_ref[s], group_ref[pl.ds(s, 1), :])
        wh, wl = split(w)
        f = f_s[pl.ds(pl.multiple_of(s * 8, 8), 8), :]
        diag = jnp.where(own, jnp.concatenate([f] * 8, 0), 0.0)
        dh, dl = split(diag)
        terms = mm_tn(jnp.concatenate([wh, wl, wh], 0), jnp.concatenate([dh, dh, dl], 0))
        rows = jnp.broadcast_to(rowf_ref[pl.ds(s, 1), :], (NPTS, NPTS))
        same = (rows == rows.T).astype(F32).astype(BF16)
        th, tl = split(terms)
        both = mm(same, jnp.concatenate([th, tl], 1))
        combined = both[:, :128] + both[:, 128:]

        def pick(c, carry):
            for k in range(32):
                t = c * 32 + k
                gat_s[pl.ds(t, 1), :] = w_s[pl.ds(rows_sm[s, t], 1), :]
            return carry

        lax.fori_loop(0, 8, pick, 0)
        gat_s[...] = gat_s[...] + combined

        def put(c, carry):
            for k in range(32):
                t = c * 32 + k
                w_s[pl.ds(rows_sm[s, t], 1), :] = gat_s[pl.ds(t, 1), :]
            return carry

        lax.fori_loop(0, 8, put, 0)
        return carry

    lax.fori_loop(0, count_sm[0], one_slot, 0)

    for zz in range(2):
        def along_x(pair, carry, zz=zz):
            xh, xl = xh_ref[...], xl_ref[...]
            at = pl.multiple_of((zz * 32 + pair * 2) * 256, 256)
            h0, l0 = split(w_s[pl.ds(at, 256), :])
            h1, l1 = split(w_s[pl.ds(at + 256, 256), :])
            bh, bl = jnp.concatenate([h0, h1], 1), jnp.concatenate([l0, l1], 1)
            res = mm(xh, bh) + mm(xl, bh) + mm(xh, bl)
            for k in range(2):
                cols = slice(k * 128, (k + 1) * 128)
                xb_s[pair * 2 + k] = res[:128, cols] + swap_parts(res[128:, cols], 1.0)
            return carry

        lax.fori_loop(0, 16, along_x, 0)
        for half in range(2):
            def permute(kc, carry, half=half):
                base = pl.multiple_of(kc * 16, 16)
                ins = [xb_s[half * 16 + j, pl.ds(base, 16), :] for j in range(16)]
                for i, v in enumerate(exchange_blocks(ins)):
                    vh, vl = split(v)
                    lo = ((i // 8) * 2 + half) * 128
                    ah_s[pl.ds((i % 8) * 128 + base, 16), lo:lo + 128] = vh
                    al_s[pl.ds((i % 8) * 128 + base, 16), lo:lo + 128] = vl
                return carry

            lax.fori_loop(0, 8, permute, 0)
        ah, al = ah_s[...], al_s[...]
        yh, yl = yh_ref[...], yl_ref[...]
        res = mm(ah, yh) + mm(al, yh) + mm(ah, yl)
        for b in range(BANDS):
            for o in range(2):
                out_ref[pl.ds(o * 16 + zz * 8 + b, 128, stride=32), :] = res[b * 128:(b + 1) * 128, o * 128:(o + 1) * 128]


def spectrum_kernel(recv_ref, coef_ref, kin_ref, th_ref, tl_ref, out_ref):
    th, tl = th_ref[...], tl_ref[...]
    kin = kin_ref[...]
    for b in range(BANDS):
        parts = [recv_ref[pl.ds(q * 8 + b, 128, stride=32), :] for q in range(4)]
        ah, al = split(jnp.concatenate(parts, 0))
        res = mm_tn(ah, th) + mm_tn(al, th) + mm_tn(ah, tl)
        for o in range(2):
            out_ref[o, b] = res[:, o * 128:(o + 1) * 128] + kin * coef_ref[o, b]


VM = pl.BlockSpec(memory_space=pltpu.VMEM)
SM = pl.BlockSpec(memory_space=pltpu.SMEM)
ANY = pl.BlockSpec(memory_space=pl.ANY)


def params():
    return pltpu.CompilerParams(vmem_limit_bytes=VMEM_LIMIT)


def run_columns(coef):
    return pl.pallas_call(
        columns_kernel,
        out_shape=jax.ShapeDtypeStruct((4096, 128), F32),
        in_specs=[VM] * 3, out_specs=VM, compiler_params=params(), name="columns",
    )(coef, *TABLES["fz"])


def run_grid(rows, count, recv, pot, value, group, window):
    return pl.pallas_call(
        grid_kernel,
        out_shape=(jax.ShapeDtypeStruct((ROWS, 128), F32), jax.ShapeDtypeStruct((WINDOW * 16, 128), F32)),
        in_specs=[SM, SM] + [VM] * 9,
        out_specs=(ANY, VM),
        scratch_shapes=[
            pltpu.VMEM((1024, 256), BF16), pltpu.VMEM((1024, 256), BF16),
            pltpu.VMEM((1024, 512), F32),
            pltpu.VMEM((16, 256, 256), BF16), pltpu.VMEM((16, 256, 256), BF16),
            pltpu.VMEM((ROWS, 128), F32), pltpu.VMEM((ROWS, 128), F32),
            pltpu.VMEM((NPTS, 128), F32), pltpu.VMEM((SLOTS * 8, 128), F32),
            pltpu.SemaphoreType.DMA(()),
        ],
        compiler_params=params(), name="grid",
    )(rows, count, recv, pot, value, group, window, *TABLES["fy"], *TABLES["fx"])


def run_back(rows, count, partials, mask, strength, window, value, group, rowf, field):
    return pl.pallas_call(
        back_kernel,
        out_shape=(jax.ShapeDtypeStruct((4096, 128), F32), jax.ShapeDtypeStruct((16, 128), F32)),
        in_specs=[SM, SM] + [VM] * 19 + [ANY],
        out_specs=(VM, VM),
        scratch_shapes=[
            pltpu.VMEM((ROWS, 128), F32), pltpu.VMEM((WINDOW * 16, 128), F32),
            pltpu.VMEM((SLOTS * 8, 128), F32), pltpu.VMEM((NPTS, 128), F32),
            pltpu.VMEM((32, 128, 128), F32),
            pltpu.VMEM((1024, 512), BF16), pltpu.VMEM((1024, 512), BF16),
            pltpu.SemaphoreType.DMA(()),
        ],
        compiler_params=params(), name="back",
    )(rows, count, *partials, mask, strength, window, value, group, rowf, *TABLES["bx"], *TABLES["by"], field)


def run_spectrum(recv, coef, kin):
    return pl.pallas_call(
        spectrum_kernel,
        out_shape=jax.ShapeDtypeStruct((2, BANDS, 128, 128), F32),
        in_specs=[VM] * 5, out_specs=VM, compiler_params=params(), name="spectrum",
    )(recv, coef, kin, *TABLES["bz"])


def to_all(block):
    block = block.reshape(128, 32, 128)
    block = lax.all_to_all(block, "pencil", split_axis=0, concat_axis=0, tiled=True)
    return block.reshape(4096, 128)


def from_offset(block, delta):
    n = lax.axis_size("pencil")
    return lax.ppermute(block, "pencil", [((i + delta) % n, i) for i in range(n)])


def per_device(coefficients, potential, slot_atom, slot_count, point_offset, proj_value, proj_strength, proj_count):
    device = lax.axis_index("pencil")
    n_dev = lax.axis_size("pencil")
    atom_dev = proj_strength.shape[0] // n_dev
    rows = (point_offset >> 11) * 256 + (point_offset & 255)
    group = (point_offset >> 8) & 7
    rowf = rows.astype(F32)
    window = ((slot_atom // atom_dev - device + REACH) % n_dev) * atom_dev + slot_atom % atom_dev
    window = window[None, :]
    atoms = ((device - REACH) * atom_dev + jnp.arange(WINDOW * atom_dev, dtype=jnp.int32)) % (n_dev * atom_dev)
    strength = jnp.tile(proj_strength[atoms], (1, 16))
    mask = ((jnp.arange(128, dtype=jnp.int32) % NPROJ)[None, :] < proj_count[atoms][:, None]).astype(F32)
    freq = jnp.arange(CUT, dtype=jnp.int32) - CUT // 2
    freq_x = device - CUT // 2
    kinetic = 6.0 / (CUT * CUT) * ((freq_x * freq_x + freq * freq)[:, None] + (freq * freq)[None, :]).astype(F32)

    recv = to_all(run_columns(coefficients))
    field, partial = run_grid(rows, slot_count, recv, potential, proj_value, group, window)
    partials = [partial]
    for delta in range(1, 2 * REACH + 1):
        partials.append(from_offset(partial[:(WINDOW - delta) * atom_dev], delta))
    for delta in range(1, 2 * REACH + 1):
        partials.append(from_offset(partial[delta * atom_dev:], -delta))
    send, becp = run_back(rows, slot_count, partials, mask, strength, window, proj_value, group, rowf, field)
    recv = to_all(send)
    return run_spectrum(recv, coefficients, kinetic), becp


def solution(mesh):
    in_specs = (
        P(None, None, "pencil", None), P("pencil", None, None), P("pencil"), P("pencil"),
        P("pencil", None), P("pencil", None, None), P(), P(),
    )
    out_specs = (P(None, None, "pencil", None), P("pencil", None))
    return jax.shard_map(per_device, mesh=mesh, in_specs=in_specs, out_specs=out_specs, check_vma=False)
```

time: 1240 us -> 328 us (0.26)
  starting transfers between devices: 508 us -> 155 us
  local copies, waits for them, and re-layouts: 361 us -> 9.28 us
  other arithmetic: 245 us -> 2.62 us
  Pallas kernels: 0 us -> 98.7 us
  matrix products: 50.5 us -> 0 us
    all_to_all x2, starting transfers between devices: 473 us -> 130 us  [to_all(): lax.all_to_all(block, 'pencil', split_axis=0, concat_axis=0, tiled=True)]
    scatter-add x9 -> x0, other arithmetic: 207 us -> none  [apply_group(): return projected.at[:, offsets].add(slot_terms)]
    unnamed x30 -> x29, local copies, waits for them, and re-layouts: 116 us -> 3.65 us
    pallas_call x0 -> x4, Pallas kernels: none -> 98.7 us  [the longest x1 51.9 us: run_back(): pl.pallas_call(back_kernel, out_shape=(jax.ShapeDtypeStruct((4096, 128),...]
    while x8 -> x0, local copies, waits for them, and re-layouts: 67.8 us -> none  [the longest x1 36.3 us: per_device(): lax.fori_loop(0, groups_live, apply_group, jnp.zeros_like(fields))]
    gather x6 -> x3, local copies, waits for them, and re-layouts: 62.5 us -> 1.83 us  [the longest x1 1.16 us: per_device(): proj_count[atoms][:, None]]
    another operation x4 -> x2, local copies, waits for them, and re-layouts: 44.4 us -> 0.7 us  [per_device(): strength = jnp.tile(proj_strength[atoms], (1, 16))]
    dot_general x11 -> x0, matrix products: 42.1 us -> none  [the longest x6 38.4 us: complex_step(): jnp.einsum(full_pattern, stacked, table, precision=lax.Precision.HIGHEST)]
  transfers between devices with their start and end apart: 10 -> 10, of which waited for: 5 -> 3; matrix products, arithmetic and copies ran while one was open for 0% -> 2% of each run, Pallas kernels for 0% -> 0%
where the time goes in v1:
time: 328 us; the launch traced here: 331 us
  starting transfers between devices  155 us (47%)
  Pallas kernels  98.7 us (30%)
  waiting for transfers between devices  63.7 us (19%)
  local copies, waits for them, and re-layouts  9.28 us (3%)
    all_to_all x2, starting transfers between devices, to_all(): lax.all_to_all(block, 'pencil', split_axis=0, concat_axis=0, tiled=True)  130 us
    all_to_all x2, waiting for transfers between devices, to_all(): lax.all_to_all(block, 'pencil', split_axis=0, concat_axis=0, tiled=True)  56.2 us
    pallas_call x1, Pallas kernels, run_back(): pl.pallas_call(back_kernel, out_shape=(jax.ShapeDtypeStruct((4096, 128),...  51.9 us
    pallas_call x1, Pallas kernels, run_grid(): pl.pallas_call(grid_kernel, out_shape=(jax.ShapeDtypeStruct((ROWS, 128),...  36.4 us
    ppermute x8, starting transfers between devices, from_offset(): lax.ppermute(block, 'pencil', [((i + delta) % n, i) for i in range(n)])  25.2 us
    ppermute x8, waiting for transfers between devices, from_offset(): lax.ppermute(block, 'pencil', [((i + delta) % n, i) for i in range(n)])  7.5 us
  transfers between devices with their start and end apart: 10, of which 3 were waited for; matrix products, arithmetic and copies ran while one was open for 2% of the time, Pallas kernels for 0%

profile of v1, /device:TPU:1, one launch (start us, length us, event | category | flops | bytes accessed | tf_op | source)
XLA Modules:
  0.0 331.0 jit_solution(5551982590459766597)
XLA Ops:
  0.6 0.0 copy-start
  0.6 5.5 %columns.1 = f32[4096,128]{1,0:T(8,128)} custom-call(f32[2,8,128,128]{3,2,1,0:T(8,128)} %coef_ref.3, bf16[512,256]{1,0:T(8,128)(2,1)} %constant.119.clone.th_ref, bf16[512,256]{1,0:T(8,128)(2,1)} %constant.120.clone.tl_ref), custom_call_target="tpu_custom_call" | custom-call | tf_op jit(solution)/shard_map/columns/pallas_call | solution.py:338
  6.1 0.0 copy-start.3
  6.1 0.0 copy-start.13
  6.1 11.5 %all-to-all-start = ((f32[128,32,128]{2,1,0:T(8,128)}), f32[128,32,128]{2,1,0:T(8,128)S(1)}, u32[]{:S(2)}, u32[]{:S(2)}) async-start(f32[128,32,128]{2,1,0:T(8,128)} %bitcast.10), calls=%async_computation | async-start | bytes 4194304 | tf_op jit(solution)/shard_map/all_to_all | solution.py:390
  17.6 0.0 copy-start.4
  18.3 0.0 copy-done.3
  18.3 0.3 copy.23
  18.7 0.6 gather_fusion.1
  19.3 0.1 copy.24
  19.4 0.0 copy-done
  19.4 1.2 gather_fusion
  20.6 0.0 copy-done.13
  20.6 0.5 fusion.5.window_ref
  21.1 0.0 copy-done.4
  21.1 0.7 fusion.6
  21.8 26.4 %all-to-all-done = f32[128,32,128]{2,1,0:T(8,128)S(1)} async-done(((f32[128,32,128]{2,1,0:T(8,128)}), f32[128,32,128]{2,1,0:T(8,128)S(1)}, u32[]{:S(2)}, u32[]{:S(2)}) %all-to-all-start) | async-done | bytes 2097184 | tf_op jit(solution)/shard_map/all_to_all | solution.py:390
  48.1 0.0 copy-start.2
  48.1 1.4 copy-done.2
  49.5 36.4 %grid.1 = (f32[16384,128]{1,0:T(8,128)}, f32[80,128]{1,0:T(8,128)}) custom-call(s32[64,256]{1,0:T(8,128)} %get-tuple-element.12.rows_sm, s32[1]{0:T(128)S(6)} %copy.26.count_sm, f32[4096,128]{1,0:T(8,128)} %bitcast.12, f32[2,256,256]{2,1,0:T(8,128)} %pot_ref.1, f32[64,8,256]{2,1,0:T(8,128)} %value_ref.3, s32[64,256]{1,0:T(8,128)} %get-tuple-element.11.group_ref, ...), custom_call_target="tpu_custom_call" | custom-call | tf_op jit(solution)/shard_map/grid/pallas_call | solution.py:346
  85.9 0.8 fusion.10
  86.7 0.7 fusion.8
  87.5 0.7 fusion.7
  88.2 15.6 %collective-permute-start.2 = (f32[32,128]{1,0:T(8,128)S(1)}, f32[32,128]{1,0:T(8,128)S(1)}, u32[]{:S(2)}, u32[]{:S(2)}) collective-permute-start(f32[32,128]{1,0:T(8,128)S(1)} %get-tuple-element.16), channel_id=1, source_target_pairs={{3,0},{4,1},{5,2},{6,3},{7,4},{8,5},{9,6},{10,7},{11,8},{12,9},{13... | collective-permute-start | bytes 49160 | tf_op jit(solution)/shard_map/ppermute | solution.py:396
  103.8 0.0 collective-permute-start.3
  103.8 3.0 collective-permute-start.7
  106.8 0.8 fusion.9
  107.6 0.0 collective-permute-start
  107.6 1.7 collective-permute-start.4
  109.4 0.0 collective-permute-done.3.p4
  109.4 0.0 copy-start.11
  109.4 4.8 %collective-permute-start.1 = (f32[48,128]{1,0:T(8,128)S(1)}, f32[48,128]{1,0:T(8,128)S(1)}, u32[]{:S(2)}, u32[]{:S(2)}) collective-permute-start(f32[48,128]{1,0:T(8,128)S(1)} %get-tuple-element.18), channel_id=1, source_target_pairs={{2,0},{3,1},{4,2},{5,3},{6,4},{7,5},{8,6},{9,7},{10,8},{11,9},{12,... | collective-permute-start | bytes 73736 | tf_op jit(solution)/shard_map/ppermute | solution.py:396
  114.2 0.0 collective-permute-done.7.m4
  114.2 0.0 copy-start.12
  114.2 0.0 collective-permute-start.5
  114.2 0.0 collective-permute-done.2.p3
  114.2 0.0 copy-start.9
  114.2 0.1 collective-permute-start.6
  114.3 0.7 compare_convert_fusion.mask_ref
  115.0 0.7 copy.25.strength_ref
  115.7 7.5 %collective-permute-done.6.m3 = f32[32,128]{1,0:T(8,128)S(1)} collective-permute-done((f32[32,128]{1,0:T(8,128)S(1)}, f32[32,128]{1,0:T(8,128)S(1)}, u32[]{:S(2)}, u32[]{:S(2)}) %collective-permute-start.6) | collective-permute-done | bytes 16416 | tf_op jit(solution)/shard_map/ppermute | solution.py:396
  123.1 0.0 collective-permute-done.1.p2
  123.1 0.0 copy-start.7
  123.1 0.0 collective-permute-done.5.m2
  123.2 0.0 copy-start.8
  123.2 0.0 collective-permute-done.p1
  123.2 0.0 copy-start.5
  123.2 0.0 collective-permute-done.4.m1
  123.2 0.0 copy-start.6
  123.2 0.0 copy-done.11
  123.2 0.0 copy-done.12
  123.2 0.0 copy-done.9
  123.2 0.5 copy-done.10
  123.7 0.0 copy-done.7
  123.8 0.0 copy-done.8
  123.8 0.0 copy-done.5
  123.8 0.0 copy-done.6
  123.8 51.9 %back.1 = (f32[4096,128]{1,0:T(8,128)}, f32[16,128]{1,0:T(8,128)}) custom-call(s32[64,256]{1,0:T(8,128)} %get-tuple-element.12.rows_sm, s32[1]{0:T(128)S(6)} %copy.26.count_sm, f32[80,128]{1,0:T(8,128)} %get-tuple-element.6.own_ref, f32[64,128]{1,0:T(8,128)} %copy-done.5, f32[48,128]{1,0:T(8,128)} %copy-done.7, f32[32,128]{1,0:T(8,128)} %copy-done.9, ...), custom_call_target="tpu_custom_call" | custom-call | tf_op jit(solution)/shard_map/back/pallas_call | solution.py:364
  175.8 118.4 %all-to-all-start.1 = ((f32[128,32,128]{2,1,0:T(8,128)}), f32[128,32,128]{2,1,0:T(8,128)S(1)}, u32[]{:S(2)}, u32[]{:S(2)}) async-start(f32[128,32,128]{2,1,0:T(8,128)} %bitcast.13), calls=%async_computation.1 | async-start | bytes 4194304 | tf_op jit(solution)/shard_map/all_to_all | solution.py:390
  294.2 0.7 convert_multiply_fusion.kin_ref
  294.9 29.8 %all-to-all-done.1 = f32[128,32,128]{2,1,0:T(8,128)S(1)} async-done(((f32[128,32,128]{2,1,0:T(8,128)}), f32[128,32,128]{2,1,0:T(8,128)S(1)}, u32[]{:S(2)}, u32[]{:S(2)}) %all-to-all-start.1) | async-done | bytes 2097184 | tf_op jit(solution)/shard_map/all_to_all | solution.py:390
  324.7 0.0 copy-start.1
  324.7 1.4 copy-done.1
  326.0 4.9 %spectrum.1 = f32[2,8,128,128]{3,2,1,0:T(8,128)} custom-call(f32[4096,128]{1,0:T(8,128)} %bitcast.11, f32[2,8,128,128]{3,2,1,0:T(8,128)} %coef_ref.3, f32[128,128]{1,0:T(8,128)} %convert_multiply_fusion.kin_ref, bf16[512,256]{1,0:T(8,128)(2,1)} %constant.129.clone.th_ref, bf16[512,256]{1,0:T(8,128)(2,1)} %constant.130.clone.tl_ref), custom_call_target="tpu_custom_call" | custom-call | tf_op jit(solution)/shard_map/spectrum/pallas_call | solution.py:381
  (6 shorter events, 0.0 us)
Async XLA Ops:
  0.6 18.7 %copy-start = (s32[2048]{0:T(1024)S(1)}, s32[2048]{0:T(1024)}, u32[]{:S(2)}) copy-start(s32[2048]{0:T(1024)} %param.27) | copy-start | bytes 24580
  6.1 12.2 %copy-start.3 = (f32[2048,8]{0,1:T(8,128)S(1)}, f32[2048,8]{0,1:T(8,128)}, u32[]{:S(2)}) copy-start(f32[2048,8]{0,1:T(8,128)} %param.26) | copy-start | bytes 196612
  6.1 14.4 %copy-start.13 = (s32[64]{0:T(128)S(1)}, s32[64]{0:T(128)}, u32[]{:S(2)}) copy-start(s32[64]{0:T(128)} %param.22) | copy-start | bytes 772
  6.1 42.0 %all-to-all-start = ((f32[128,32,128]{2,1,0:T(8,128)}), f32[128,32,128]{2,1,0:T(8,128)S(1)}, u32[]{:S(2)}, u32[]{:S(2)}) async-start(f32[128,32,128]{2,1,0:T(8,128)} %bitcast.10), calls=%async_computation | async-start | bytes 4194304 | tf_op jit(solution)/shard_map/all_to_all | solution.py:390
  17.6 3.5 %copy-start.4 = (s32[64,256]{1,0:T(8,128)S(1)}, s32[64,256]{1,0:T(8,128)}, u32[]{:S(2)}) copy-start(s32[64,256]{1,0:T(8,128)} %param.24) | copy-start | bytes 196612
  48.1 1.4 copy-start.2
  88.2 26.0 %collective-permute-start.2 = (f32[32,128]{1,0:T(8,128)S(1)}, f32[32,128]{1,0:T(8,128)S(1)}, u32[]{:S(2)}, u32[]{:S(2)}) collective-permute-start(f32[32,128]{1,0:T(8,128)S(1)} %get-tuple-element.16), channel_id=1, source_target_pairs={{3,0},{4,1},{5,2},{6,3},{7,4},{8,5},{9,6},{10,7},{11,8},{12,9},{13... | collective-permute-start | bytes 49160 | tf_op jit(solution)/shard_map/ppermute | solution.py:396
  103.8 5.5 %collective-permute-start.3 = (f32[16,128]{1,0:T(8,128)S(1)}, f32[16,128]{1,0:T(8,128)S(1)}, u32[]{:S(2)}, u32[]{:S(2)}) collective-permute-start(f32[16,128]{1,0:T(8,128)S(1)} %get-tuple-element.14), channel_id=1, source_target_pairs={{4,0},{5,1},{6,2},{7,3},{8,4},{9,5},{10,6},{11,7},{12,8},{13,9},{1... | collective-permute-start | bytes 24584 | tf_op jit(solution)/shard_map/ppermute | solution.py:396
  103.8 10.3 %collective-permute-start.7 = (f32[16,128]{1,0:T(8,128)S(1)}, f32[16,128]{1,0:T(8,128)S(1)}, u32[]{:S(2)}, u32[]{:S(2)}) collective-permute-start(f32[16,128]{1,0:T(8,128)S(1)} %get-tuple-element.13), channel_id=1, source_target_pairs={{124,0},{125,1},{126,2},{127,3},{0,4},{1,5},{2,6},{3,7},{4,8},{5,9... | collective-permute-start | bytes 24584 | tf_op jit(solution)/shard_map/ppermute | solution.py:396
  107.6 15.6 %collective-permute-start = (f32[64,128]{1,0:T(8,128)S(1)}, f32[64,128]{1,0:T(8,128)S(1)}, u32[]{:S(2)}, u32[]{:S(2)}) collective-permute-start(f32[64,128]{1,0:T(8,128)S(1)} %get-tuple-element.20), channel_id=1, source_target_pairs={{1,0},{2,1},{3,2},{4,3},{5,4},{6,5},{7,6},{8,7},{9,8},{10,9},{11,1... | collective-permute-start | bytes 98312 | tf_op jit(solution)/shard_map/ppermute | solution.py:396
  107.6 15.6 %collective-permute-start.4 = (f32[64,128]{1,0:T(8,128)S(1)}, f32[64,128]{1,0:T(8,128)S(1)}, u32[]{:S(2)}, u32[]{:S(2)}) collective-permute-start(f32[64,128]{1,0:T(8,128)S(1)} %get-tuple-element.19), channel_id=1, source_target_pairs={{127,0},{0,1},{1,2},{2,3},{3,4},{4,5},{5,6},{6,7},{7,8},{8,9},{9,1... | collective-permute-start | bytes 98312 | tf_op jit(solution)/shard_map/ppermute | solution.py:396
  109.4 13.9 %copy-start.11 = (f32[16,128]{1,0:T(8,128)}, f32[16,128]{1,0:T(8,128)S(1)}, u32[]{:S(2)}) copy-start(f32[16,128]{1,0:T(8,128)S(1)} %collective-permute-done.3.p4) | copy-start | bytes 24580
  109.4 13.8 %collective-permute-start.1 = (f32[48,128]{1,0:T(8,128)S(1)}, f32[48,128]{1,0:T(8,128)S(1)}, u32[]{:S(2)}, u32[]{:S(2)}) collective-permute-start(f32[48,128]{1,0:T(8,128)S(1)} %get-tuple-element.18), channel_id=1, source_target_pairs={{2,0},{3,1},{4,2},{5,3},{6,4},{7,5},{8,6},{9,7},{10,8},{11,9},{12,... | collective-permute-start | bytes 73736 | tf_op jit(solution)/shard_map/ppermute | solution.py:396
  114.2 9.0 %copy-start.12 = (f32[16,128]{1,0:T(8,128)}, f32[16,128]{1,0:T(8,128)S(1)}, u32[]{:S(2)}) copy-start(f32[16,128]{1,0:T(8,128)S(1)} %collective-permute-done.7.m4) | copy-start | bytes 24580
  114.2 9.0 %collective-permute-start.5 = (f32[48,128]{1,0:T(8,128)S(1)}, f32[48,128]{1,0:T(8,128)S(1)}, u32[]{:S(2)}, u32[]{:S(2)}) collective-permute-start(f32[48,128]{1,0:T(8,128)S(1)} %get-tuple-element.17), channel_id=1, source_target_pairs={{126,0},{127,1},{0,2},{1,3},{2,4},{3,5},{4,6},{5,7},{6,8},{7,9},{8... | collective-permute-start | bytes 73736 | tf_op jit(solution)/shard_map/ppermute | solution.py:396
  114.2 9.0 %copy-start.9 = (f32[32,128]{1,0:T(8,128)}, f32[32,128]{1,0:T(8,128)S(1)}, u32[]{:S(2)}) copy-start(f32[32,128]{1,0:T(8,128)S(1)} %collective-permute-done.2.p3) | copy-start | bytes 49156
  114.2 8.9 %collective-permute-start.6 = (f32[32,128]{1,0:T(8,128)S(1)}, f32[32,128]{1,0:T(8,128)S(1)}, u32[]{:S(2)}, u32[]{:S(2)}) collective-permute-start(f32[32,128]{1,0:T(8,128)S(1)} %get-tuple-element.15), channel_id=1, source_target_pairs={{125,0},{126,1},{127,2},{0,3},{1,4},{2,5},{3,6},{4,7},{5,8},{6,9},... | collective-permute-start | bytes 49160 | tf_op jit(solution)/shard_map/ppermute | solution.py:396
  123.1 0.6 copy-start.10
  123.1 0.6 copy-start.7
  123.2 0.6 copy-start.8
  123.2 0.6 copy-start.5
  123.2 0.6 copy-start.6
  175.8 148.9 %all-to-all-start.1 = ((f32[128,32,128]{2,1,0:T(8,128)}), f32[128,32,128]{2,1,0:T(8,128)S(1)}, u32[]{:S(2)}, u32[]{:S(2)}) async-start(f32[128,32,128]{2,1,0:T(8,128)} %bitcast.13), calls=%async_computation.1 | async-start | bytes 4194304 | tf_op jit(solution)/shard_map/all_to_all | solution.py:390
  324.7 1.4 copy-start.1

commit v2 on v1

--- a/solution.py
+++ b/solution.py
@@ -127,8 +127,8 @@
     rows_sm, count_sm,
     recv_ref, pot_ref, value_ref, group_ref, window_ref,
     yh_ref, yl_ref, xh_ref, xl_ref,
-    field_hbm, partial_ref,
-    ah_s, al_s, ys_s, inh_s, inl_s, u_s, w_s, gat_s, z_s, sem,
+    field_hbm, partial_ref, c1, c2, c3, c4, d1, d2, d3, d4,
+    ah_s, al_s, ys_s, inh_s, inl_s, u_s, w_s, ga_s, gb_s, z_s, sem,
 ):
     yh, yl = yh_ref[...], yl_ref[...]
     piece = lax.broadcasted_iota(jnp.int32, (32, 128), 0)
@@ -187,15 +187,16 @@
     z_s[...] = jnp.zeros((SLOTS * 8, 128), F32)
     own = lane_iota((64, 128)) % 8 == lax.broadcasted_iota(jnp.int32, (64, 128), 0) // 8
 
-    def one_slot(s, carry):
-        def pick(c, carry):
-            for k in range(32):
-                t = c * 32 + k
-                gat_s[pl.ds(t, 1), :] = u_s[pl.ds(rows_sm[s, t], 1), :]
-            return carry
-
-        lax.fori_loop(0, 8, pick, 0)
-        gh, gl = split(gat_s[...])
+    count = count_sm[0]
+
+    def pick(s, buf):
+        for c in range(0, NPTS, 16):
+            vals = [u_s[pl.ds(rows_sm[s * NPTS + c + k], 1), :] for k in range(16)]
+            for k in range(16):
+                buf[c + k:c + k + 1, :] = vals[k]
+
+    def reduce_slot(s, buf):
+        gh, gl = split(buf[...])
         w = slot_weights(value_ref[s], group_ref[pl.ds(s, 1), :])
         wh, wl = split(w)
         prod = mm(jnp.concatenate([wh, wl], 0), jnp.concatenate([gh, gl], 1))
@@ -204,16 +205,28 @@
         z = total[0:8]
         for g in range(1, 8):
             z = z + total[g * 8:(g + 1) * 8]
-        z_s[pl.ds(pl.multiple_of(s * 8, 8), 8), :] = z
+        z_s[pl.ds(pl.multiple_of(s * 8, 8), 8), :] = jnp.where(s < count, z, 0.0)
+
+    def two_slots(i, carry):
+        s = i * 2
+        pick(s + 1, gb_s)
+        reduce_slot(s, ga_s)
+        pick(jnp.minimum(s + 2, SLOTS - 1), ga_s)
+        reduce_slot(s + 1, gb_s)
         return carry
 
-    lax.fori_loop(0, count_sm[0], one_slot, 0)
+    pick(0, ga_s)
+    lax.fori_loop(0, (count + 1) // 2, two_slots, 0)
     spread = exact_times_ones(z_s[...], block_ones())
     mine = lane_iota((512, 128)) % 8 == lax.broadcasted_iota(jnp.int32, (512, 128), 0) % 8
     slot_terms = jnp.sum(jnp.where(mine, spread, 0.0).reshape(SLOTS, 8, 128), 1)
     onehot = (lax.broadcasted_iota(jnp.int32, (WINDOW * 16, SLOTS), 0) == window_ref[...]).astype(F32).astype(BF16)
     a, b, c = three(slot_terms)
-    partial_ref[...] = mm(onehot, a) + mm(onehot, b) + mm(onehot, c)
+    partial = mm(onehot, a) + mm(onehot, b) + mm(onehot, c)
+    partial_ref[...] = partial
+    for delta, below, above in ((1, c1, d1), (2, c2, d2), (3, c3, d3), (4, c4, d4)):
+        below[...] = partial[:(WINDOW - delta) * 16]
+        above[...] = partial[delta * 16:]
     out_copy.wait()
 
 
@@ -224,7 +237,7 @@
     xh_ref, xl_ref, yh_ref, yl_ref,
     field_hbm,
     out_ref, becp_ref,
-    w_s, tot_s, f_s, gat_s, xb_s, ah_s, al_s, sem,
+    w_s, tot_s, f_s, gat_s, ta_s, tb_s, xb_s, ah_s, al_s, sem,
 ):
     in_copy = pltpu.make_async_copy(field_hbm, w_s, sem)
     in_copy.start()
@@ -245,12 +258,13 @@
     wide = jnp.broadcast_to(slot_energy[:, None, :], (SLOTS, 8, 128)).reshape(SLOTS * 8, 128)
     f_s[...] = exact_times_ones(jnp.where(mine, wide, 0.0), block_ones())
     own = lane_iota((64, 128)) % 8 == lax.broadcasted_iota(jnp.int32, (64, 128), 0) // 8
-    in_copy.wait()
-
-    def one_slot(s, carry):
+    count = count_sm[0]
+
+    def terms_of(s, buf):
         w = slot_weights(value_ref[s], group_ref[pl.ds(s, 1), :])
         wh, wl = split(w)
         f = f_s[pl.ds(pl.multiple_of(s * 8, 8), 8), :]
+        f = jnp.where(s < count, f, 0.0)
         diag = jnp.where(own, jnp.concatenate([f] * 8, 0), 0.0)
         dh, dl = split(diag)
         terms = mm_tn(jnp.concatenate([wh, wl, wh], 0), jnp.concatenate([dh, dh, dl], 0))
@@ -258,27 +272,30 @@
         same = (rows == rows.T).astype(F32).astype(BF16)
         th, tl = split(terms)
         both = mm(same, jnp.concatenate([th, tl], 1))
-        combined = both[:, :128] + both[:, 128:]
-
-        def pick(c, carry):
-            for k in range(32):
-                t = c * 32 + k
-                gat_s[pl.ds(t, 1), :] = w_s[pl.ds(rows_sm[s, t], 1), :]
-            return carry
-
-        lax.fori_loop(0, 8, pick, 0)
-        gat_s[...] = gat_s[...] + combined
-
-        def put(c, carry):
-            for k in range(32):
-                t = c * 32 + k
-                w_s[pl.ds(rows_sm[s, t], 1), :] = gat_s[pl.ds(t, 1), :]
-            return carry
-
-        lax.fori_loop(0, 8, put, 0)
+        buf[...] = both[:, :128] + both[:, 128:]
+
+    def add_slot(s, buf):
+        for c in range(0, NPTS, 16):
+            vals = [w_s[pl.ds(rows_sm[s * NPTS + c + k], 1), :] for k in range(16)]
+            for k in range(16):
+                gat_s[c + k:c + k + 1, :] = vals[k]
+        gat_s[...] = gat_s[...] + buf[...]
+        for c in range(0, NPTS, 16):
+            vals = [gat_s[c + k:c + k + 1, :] for k in range(16)]
+            for k in range(16):
+                w_s[pl.ds(rows_sm[s * NPTS + c + k], 1), :] = vals[k]
+
+    def two_slots(i, carry):
+        s = i * 2
+        terms_of(s + 1, tb_s)
+        add_slot(s, ta_s)
+        terms_of(jnp.minimum(s + 2, SLOTS - 1), ta_s)
+        add_slot(s + 1, tb_s)
         return carry
 
-    lax.fori_loop(0, count_sm[0], one_slot, 0)
+    terms_of(0, ta_s)
+    in_copy.wait()
+    lax.fori_loop(0, (count + 1) // 2, two_slots, 0)
 
     for zz in range(2):
         def along_x(pair, carry, zz=zz):
@@ -345,15 +362,17 @@
 def run_grid(rows, count, recv, pot, value, group, window):
     return pl.pallas_call(
         grid_kernel,
-        out_shape=(jax.ShapeDtypeStruct((ROWS, 128), F32), jax.ShapeDtypeStruct((WINDOW * 16, 128), F32)),
+        out_shape=[jax.ShapeDtypeStruct((ROWS, 128), F32)] + [
+            jax.ShapeDtypeStruct((blocks * 16, 128), F32) for blocks in (5, 4, 3, 2, 1, 4, 3, 2, 1)
+        ],
         in_specs=[SM, SM] + [VM] * 9,
-        out_specs=(ANY, VM),
+        out_specs=[ANY] + [VM] * 9,
         scratch_shapes=[
             pltpu.VMEM((1024, 256), BF16), pltpu.VMEM((1024, 256), BF16),
             pltpu.VMEM((1024, 512), F32),
             pltpu.VMEM((16, 256, 256), BF16), pltpu.VMEM((16, 256, 256), BF16),
             pltpu.VMEM((ROWS, 128), F32), pltpu.VMEM((ROWS, 128), F32),
-            pltpu.VMEM((NPTS, 128), F32), pltpu.VMEM((SLOTS * 8, 128), F32),
+            pltpu.VMEM((NPTS, 128), F32), pltpu.VMEM((NPTS, 128), F32), pltpu.VMEM((SLOTS * 8, 128), F32),
             pltpu.SemaphoreType.DMA(()),
         ],
         compiler_params=params(), name="grid",
@@ -369,6 +388,7 @@
         scratch_shapes=[
             pltpu.VMEM((ROWS, 128), F32), pltpu.VMEM((WINDOW * 16, 128), F32),
             pltpu.VMEM((SLOTS * 8, 128), F32), pltpu.VMEM((NPTS, 128), F32),
+            pltpu.VMEM((NPTS, 128), F32), pltpu.VMEM((NPTS, 128), F32),
             pltpu.VMEM((32, 128, 128), F32),
             pltpu.VMEM((1024, 512), BF16), pltpu.VMEM((1024, 512), BF16),
             pltpu.SemaphoreType.DMA(()),
@@ -403,6 +423,7 @@
     rows = (point_offset >> 11) * 256 + (point_offset & 255)
     group = (point_offset >> 8) & 7
     rowf = rows.astype(F32)
+    rows = rows.reshape(-1)
     window = ((slot_atom // atom_dev - device + REACH) % n_dev) * atom_dev + slot_atom % atom_dev
     window = window[None, :]
     atoms = ((device - REACH) * atom_dev + jnp.arange(WINDOW * atom_dev, dtype=jnp.int32)) % (n_dev * atom_dev)
@@ -413,12 +434,9 @@
     kinetic = 6.0 / (CUT * CUT) * ((freq_x * freq_x + freq * freq)[:, None] + (freq * freq)[None, :]).astype(F32)
 
     recv = to_all(run_columns(coefficients))
-    field, partial = run_grid(rows, slot_count, recv, potential, proj_value, group, window)
-    partials = [partial]
-    for delta in range(1, 2 * REACH + 1):
-        partials.append(from_offset(partial[:(WINDOW - delta) * atom_dev], delta))
-    for delta in range(1, 2 * REACH + 1):
-        partials.append(from_offset(partial[delta * atom_dev:], -delta))
+    field, partial, *windows = run_grid(rows, slot_count, recv, potential, proj_value, group, window)
+    deltas = (1, 2, 3, 4, -1, -2, -3, -4)
+    partials = [partial] + [from_offset(block, delta) for block, delta in zip(windows, deltas)]
     send, becp = run_back(rows, slot_count, partials, mask, strength, window, proj_value, group, rowf, field)
     recv = to_all(send)
     return run_spectrum(recv, coefficients, kinetic), becp

time: 328 us -> 216 us (0.66)
  starting transfers between devices: 155 us -> 52.7 us
  Pallas kernels: 98.7 us -> 88.8 us
    all_to_all x2, starting transfers between devices: 130 us -> 36.8 us  [to_all(): lax.all_to_all(block, 'pencil', split_axis=0, concat_axis=0, tiled=True)]
    ppermute x8, starting transfers between devices: 25.2 us -> 15.9 us  [from_offset(): lax.ppermute(block, 'pencil', [((i + delta) % n, i) for i in range(n)])]
    pallas_call x1, Pallas kernels: 51.9 us -> 43.3 us  [run_back(): pl.pallas_call(back_kernel, out_shape=(jax.ShapeDtypeStruct((4096, 128),...]
  transfers between devices with their start and end apart: 10 -> 10, of which waited for: 3 -> 3; matrix products, arithmetic and copies ran while one was open for 2% -> 3% of each run, Pallas kernels for 0% -> 0%
where the time goes in v2:
time: 216 us; the launch traced here: 217 us
  Pallas kernels  88.8 us (41%)
  waiting for transfers between devices  64.1 us (30%)
  starting transfers between devices  52.7 us (24%)
  local copies, waits for them, and re-layouts  6.82 us (3%)
  other arithmetic  2.67 us (1%)
    all_to_all x2, waiting for transfers between devices, to_all(): lax.all_to_all(block, 'pencil', split_axis=0, concat_axis=0, tiled=True)  56.7 us
    pallas_call x1, Pallas kernels, run_back(): pl.pallas_call(back_kernel, out_shape=(jax.ShapeDtypeStruct((4096, 128),...  43.3 us
    all_to_all x2, starting transfers between devices, to_all(): lax.all_to_all(block, 'pencil', split_axis=0, concat_axis=0, tiled=True)  36.8 us
    pallas_call x1, Pallas kernels, run_grid(): pl.pallas_call(grid_kernel, out_shape=[jax.ShapeDtypeStruct((ROWS, 128),...  35.1 us
    ppermute x8, starting transfers between devices, from_offset(): lax.ppermute(block, 'pencil', [((i + delta) % n, i) for i in range(n)])  15.9 us
    ppermute x8, waiting for transfers between devices, from_offset(): lax.ppermute(block, 'pencil', [((i + delta) % n, i) for i in range(n)])  7.42 us
    pallas_call x1, Pallas kernels, run_columns(): pl.pallas_call(columns_kernel, out_shape=jax.ShapeDtypeStruct((4096, 128)...  5.46 us
    pallas_call x1, Pallas kernels, run_spectrum(): pl.pallas_call(spectrum_kernel, out_shape=jax.ShapeDtypeStruct((2, BANDS,...  4.92 us
  transfers between devices with their start and end apart: 10, of which 3 were waited for; matrix products, arithmetic and copies ran while one was open for 3% of the time, Pallas kernels for 0%

profile of v2, /device:TPU:1, one launch (start us, length us, event | category | flops | bytes accessed | tf_op | source)
XLA Modules:
  0.0 216.6 jit_solution(10366542011826608005)
XLA Ops:
  0.6 0.0 copy-start
  0.6 5.5 %columns.1 = f32[4096,128]{1,0:T(8,128)} custom-call(f32[2,8,128,128]{3,2,1,0:T(8,128)} %coef_ref.3, bf16[512,256]{1,0:T(8,128)(2,1)} %constant.119.clone.th_ref, bf16[512,256]{1,0:T(8,128)(2,1)} %constant.120.clone.tl_ref), custom_call_target="tpu_custom_call" | custom-call | tf_op jit(solution)/shard_map/columns/pallas_call | solution.py:355
  6.1 0.0 copy-start.4
  6.1 0.0 copy-start.3
  6.1 0.0 copy-start.13
  6.1 11.5 %all-to-all-start = ((f32[128,32,128]{2,1,0:T(8,128)}), f32[128,32,128]{2,1,0:T(8,128)S(1)}, u32[]{:S(2)}, u32[]{:S(2)}) async-start(f32[128,32,128]{2,1,0:T(8,128)} %bitcast.13), calls=%async_computation | async-start | bytes 4194304 | tf_op jit(solution)/shard_map/all_to_all | solution.py:410
  17.6 0.0 copy-done.4
  17.6 0.7 fusion
  18.3 0.7 copy.26
  19.6 0.0 copy-done.3
  19.6 0.3 copy.23
  20.0 0.6 gather_fusion.1
  20.6 0.1 copy.24
  20.7 0.0 copy-done.13
  20.7 0.6 fusion.7.window_ref
  21.2 26.9 %all-to-all-done = f32[128,32,128]{2,1,0:T(8,128)S(1)} async-done(((f32[128,32,128]{2,1,0:T(8,128)}), f32[128,32,128]{2,1,0:T(8,128)S(1)}, u32[]{:S(2)}, u32[]{:S(2)}) %all-to-all-start) | async-done | bytes 2097184 | tf_op jit(solution)/shard_map/all_to_all | solution.py:410
  48.1 0.0 copy-start.2
  48.1 1.4 copy-done.2
  49.5 35.1 %grid.1 = (f32[16384,128]{1,0:T(8,128)}, f32[80,128]{1,0:T(8,128)}, f32[64,128]{1,0:T(8,128)}, f32[48,128]{1,0:T(8,128)}, f32[32,128]{1,0:T(8,128)}, /*index=5*/...) custom-call(s32[16384]{0:T(1024)} %bitcast.17, ...), custom_call_target="tpu_custom_call" | custom-call | tf_op jit(solution)/shard_map/grid/pallas_call | solution.py:363
  84.6 0.1 collective-permute-start.2
  84.7 2.0 collective-permute-start.3
  86.6 1.1 collective-permute-start.7
  87.7 0.0 copy-done
  87.7 1.1 gather_fusion
  88.9 1.2 collective-permute-start
  90.1 0.6 collective-permute-start.4
  90.7 0.0 collective-permute-done.3.p4
  90.7 0.0 copy-start.11
  90.7 10.9 %collective-permute-start.1 = (f32[48,128]{1,0:T(8,128)}, f32[48,128]{1,0:T(8,128)S(1)}, u32[]{:S(2)}, u32[]{:S(2)}) collective-permute-start(f32[48,128]{1,0:T(8,128)} %get-tuple-element.16), channel_id=1, source_target_pairs={{2,0},{3,1},{4,2},{5,3},{6,4},{7,5},{8,6},{9,7},{10,8},{11,9},{12,... | collective-permute-start | bytes 73736 | tf_op jit(solution)/shard_map/ppermute | solution.py:416
  101.6 0.0 collective-permute-done.7.m4
  101.6 0.0 copy-start.12
  101.6 0.0 collective-permute-start.5
  101.6 0.0 collective-permute-done.2.p3
  101.6 0.0 copy-start.9
  101.6 0.1 collective-permute-start.6
  101.7 0.7 compare_convert_fusion.mask_ref
  102.4 0.7 copy.25.strength_ref
  103.1 7.4 %collective-permute-done.6.m3 = f32[32,128]{1,0:T(8,128)S(1)} collective-permute-done((f32[32,128]{1,0:T(8,128)}, f32[32,128]{1,0:T(8,128)S(1)}, u32[]{:S(2)}, u32[]{:S(2)}) %collective-permute-start.6) | collective-permute-done | bytes 16416 | tf_op jit(solution)/shard_map/ppermute | solution.py:416
  110.5 0.0 copy-start.10
  110.5 0.0 collective-permute-done.1.p2
  110.5 0.0 copy-start.7
  110.5 0.0 collective-permute-done.5.m2
  110.5 0.0 copy-start.8
  110.5 0.0 collective-permute-done.p1
  110.5 0.0 copy-start.5
  110.5 0.0 collective-permute-done.4.m1
  110.6 0.0 copy-start.6
  110.6 0.0 copy-done.11
  110.6 0.0 copy-done.12
  110.6 0.0 copy-done.9
  110.6 0.5 copy-done.10
  111.1 0.0 copy-done.7
  111.1 0.0 copy-done.8
  111.1 0.0 copy-done.5
  111.1 0.0 copy-done.6
  111.2 43.3 %back.1 = (f32[4096,128]{1,0:T(8,128)}, f32[16,128]{1,0:T(8,128)}) custom-call(s32[16384]{0:T(1024)} %bitcast.18, s32[1]{0:T(128)S(6)} %copy.27.count_sm, f32[80,128]{1,0:T(8,128)} %get-tuple-element.14.own_ref, f32[64,128]{1,0:T(8,128)} %copy-done.5, f32[48,128]{1,0:T(8,128)} %copy-done.7, f32[32,128]{1,0:T(8,128)} %copy-done.9, f32[16,128]{1,0:T(8,128)} %copy-done.11, ...), custom_call_target="tpu_custom_call" | custom-call | tf_op jit(solution)/shard_map/back/pallas_call | solution.py:383
  154.5 25.3 %all-to-all-start.1 = ((f32[128,32,128]{2,1,0:T(8,128)}), f32[128,32,128]{2,1,0:T(8,128)S(1)}, u32[]{:S(2)}, u32[]{:S(2)}) async-start(f32[128,32,128]{2,1,0:T(8,128)} %bitcast.16), calls=%async_computation.1 | async-start | bytes 4194304 | tf_op jit(solution)/shard_map/all_to_all | solution.py:410
  179.8 0.7 convert_multiply_fusion.kin_ref
  180.5 29.8 %all-to-all-done.1 = f32[128,32,128]{2,1,0:T(8,128)S(1)} async-done(((f32[128,32,128]{2,1,0:T(8,128)}), f32[128,32,128]{2,1,0:T(8,128)S(1)}, u32[]{:S(2)}, u32[]{:S(2)}) %all-to-all-start.1) | async-done | bytes 2097184 | tf_op jit(solution)/shard_map/all_to_all | solution.py:410
  210.3 0.0 copy-start.1
  210.3 1.3 copy-done.1
  211.7 4.9 %spectrum.1 = f32[2,8,128,128]{3,2,1,0:T(8,128)} custom-call(f32[4096,128]{1,0:T(8,128)} %bitcast.14, f32[2,8,128,128]{3,2,1,0:T(8,128)} %coef_ref.3, f32[128,128]{1,0:T(8,128)} %convert_multiply_fusion.kin_ref, bf16[512,256]{1,0:T(8,128)(2,1)} %constant.129.clone.th_ref, bf16[512,256]{1,0:T(8,128)(2,1)} %constant.130.clone.tl_ref), custom_call_target="tpu_custom_call" | custom-call | tf_op jit(solution)/shard_map/spectrum/pallas_call | solution.py:401
  (5 shorter events, 0.0 us)
Async XLA Ops:
  0.6 87.1 %copy-start = (s32[2048]{0:T(1024)S(1)}, s32[2048]{0:T(1024)}, u32[]{:S(2)}) copy-start(s32[2048]{0:T(1024)} %param.27) | copy-start | bytes 24580
  6.1 11.5 %copy-start.4 = (s32[64,256]{1,0:T(8,128)S(1)}, s32[64,256]{1,0:T(8,128)}, u32[]{:S(2)}) copy-start(s32[64,256]{1,0:T(8,128)} %param.24) | copy-start | bytes 196612
  6.1 13.5 %copy-start.3 = (f32[2048,8]{0,1:T(8,128)S(1)}, f32[2048,8]{0,1:T(8,128)}, u32[]{:S(2)}) copy-start(f32[2048,8]{0,1:T(8,128)} %param.26) | copy-start | bytes 196612
  6.1 14.5 %copy-start.13 = (s32[64]{0:T(128)S(1)}, s32[64]{0:T(128)}, u32[]{:S(2)}) copy-start(s32[64]{0:T(128)} %param.22) | copy-start | bytes 772
  6.1 42.0 %all-to-all-start = ((f32[128,32,128]{2,1,0:T(8,128)}), f32[128,32,128]{2,1,0:T(8,128)S(1)}, u32[]{:S(2)}, u32[]{:S(2)}) async-start(f32[128,32,128]{2,1,0:T(8,128)} %bitcast.13), calls=%async_computation | async-start | bytes 4194304 | tf_op jit(solution)/shard_map/all_to_all | solution.py:410
  48.1 1.4 copy-start.2
  84.6 17.0 %collective-permute-start.2 = (f32[32,128]{1,0:T(8,128)}, f32[32,128]{1,0:T(8,128)S(1)}, u32[]{:S(2)}, u32[]{:S(2)}) collective-permute-start(f32[32,128]{1,0:T(8,128)} %get-tuple-element.17), channel_id=1, source_target_pairs={{3,0},{4,1},{5,2},{6,3},{7,4},{8,5},{9,6},{10,7},{11,8},{12,9},{13... | collective-permute-start | bytes 49160 | tf_op jit(solution)/shard_map/ppermute | solution.py:416
  84.7 6.0 %collective-permute-start.3 = (f32[16,128]{1,0:T(8,128)}, f32[16,128]{1,0:T(8,128)S(1)}, u32[]{:S(2)}, u32[]{:S(2)}) collective-permute-start(f32[16,128]{1,0:T(8,128)} %get-tuple-element.18), channel_id=1, source_target_pairs={{4,0},{5,1},{6,2},{7,3},{8,4},{9,5},{10,6},{11,7},{12,8},{13,9},{1... | collective-permute-start | bytes 24584 | tf_op jit(solution)/shard_map/ppermute | solution.py:416
  86.6 15.0 %collective-permute-start.7 = (f32[16,128]{1,0:T(8,128)}, f32[16,128]{1,0:T(8,128)S(1)}, u32[]{:S(2)}, u32[]{:S(2)}) collective-permute-start(f32[16,128]{1,0:T(8,128)} %get-tuple-element.22), channel_id=1, source_target_pairs={{124,0},{125,1},{126,2},{127,3},{0,4},{1,5},{2,6},{3,7},{4,8},{5,9... | collective-permute-start | bytes 24584 | tf_op jit(solution)/shard_map/ppermute | solution.py:416
  88.9 21.6 %collective-permute-start = (f32[64,128]{1,0:T(8,128)}, f32[64,128]{1,0:T(8,128)S(1)}, u32[]{:S(2)}, u32[]{:S(2)}) collective-permute-start(f32[64,128]{1,0:T(8,128)} %get-tuple-element.15), channel_id=1, source_target_pairs={{1,0},{2,1},{3,2},{4,3},{5,4},{6,5},{7,6},{8,7},{9,8},{10,9},{11,1... | collective-permute-start | bytes 98312 | tf_op jit(solution)/shard_map/ppermute | solution.py:416
  90.1 20.5 %collective-permute-start.4 = (f32[64,128]{1,0:T(8,128)}, f32[64,128]{1,0:T(8,128)S(1)}, u32[]{:S(2)}, u32[]{:S(2)}) collective-permute-start(f32[64,128]{1,0:T(8,128)} %get-tuple-element.19), channel_id=1, source_target_pairs={{127,0},{0,1},{1,2},{2,3},{3,4},{4,5},{5,6},{6,7},{7,8},{8,9},{9,1... | collective-permute-start | bytes 98312 | tf_op jit(solution)/shard_map/ppermute | solution.py:416
  90.7 19.9 %copy-start.11 = (f32[16,128]{1,0:T(8,128)}, f32[16,128]{1,0:T(8,128)S(1)}, u32[]{:S(2)}) copy-start(f32[16,128]{1,0:T(8,128)S(1)} %collective-permute-done.3.p4) | copy-start | bytes 24580
  90.7 19.8 %collective-permute-start.1 = (f32[48,128]{1,0:T(8,128)}, f32[48,128]{1,0:T(8,128)S(1)}, u32[]{:S(2)}, u32[]{:S(2)}) collective-permute-start(f32[48,128]{1,0:T(8,128)} %get-tuple-element.16), channel_id=1, source_target_pairs={{2,0},{3,1},{4,2},{5,3},{6,4},{7,5},{8,6},{9,7},{10,8},{11,9},{12,... | collective-permute-start | bytes 73736 | tf_op jit(solution)/shard_map/ppermute | solution.py:416
  101.6 9.0 %copy-start.12 = (f32[16,128]{1,0:T(8,128)}, f32[16,128]{1,0:T(8,128)S(1)}, u32[]{:S(2)}) copy-start(f32[16,128]{1,0:T(8,128)S(1)} %collective-permute-done.7.m4) | copy-start | bytes 24580
  101.6 8.9 %collective-permute-start.5 = (f32[48,128]{1,0:T(8,128)}, f32[48,128]{1,0:T(8,128)S(1)}, u32[]{:S(2)}, u32[]{:S(2)}) collective-permute-start(f32[48,128]{1,0:T(8,128)} %get-tuple-element.20), channel_id=1, source_target_pairs={{126,0},{127,1},{0,2},{1,3},{2,4},{3,5},{4,6},{5,7},{6,8},{7,9},{8... | collective-permute-start | bytes 73736 | tf_op jit(solution)/shard_map/ppermute | solution.py:416
  101.6 9.0 %copy-start.9 = (f32[32,128]{1,0:T(8,128)}, f32[32,128]{1,0:T(8,128)S(1)}, u32[]{:S(2)}) copy-start(f32[32,128]{1,0:T(8,128)S(1)} %collective-permute-done.2.p3) | copy-start | bytes 49156
  101.6 8.9 %collective-permute-start.6 = (f32[32,128]{1,0:T(8,128)}, f32[32,128]{1,0:T(8,128)S(1)}, u32[]{:S(2)}, u32[]{:S(2)}) collective-permute-start(f32[32,128]{1,0:T(8,128)} %get-tuple-element.21), channel_id=1, source_target_pairs={{125,0},{126,1},{127,2},{0,3},{1,4},{2,5},{3,6},{4,7},{5,8},{6,9},... | collective-permute-start | bytes 49160 | tf_op jit(solution)/shard_map/ppermute | solution.py:416
  110.5 0.6 copy-start.10
  110.5 0.6 copy-start.7
  110.5 0.6 copy-start.8
  110.5 0.6 copy-start.5
  110.6 0.6 copy-start.6
  154.5 55.8 %all-to-all-start.1 = ((f32[128,32,128]{2,1,0:T(8,128)}), f32[128,32,128]{2,1,0:T(8,128)S(1)}, u32[]{:S(2)}, u32[]{:S(2)}) async-start(f32[128,32,128]{2,1,0:T(8,128)} %bitcast.16), calls=%async_computation.1 | async-start | bytes 4194304 | tf_op jit(solution)/shard_map/all_to_all | solution.py:410
  210.3 1.3 copy-start.1

commit v3 on v2

--- a/solution.py
+++ b/solution.py
@@ -18,6 +18,9 @@
 WINDOW = 2 * REACH + 1
 F32 = jnp.float32
 BF16 = jnp.bfloat16
+UNROLL = 4
+TO_GRID = CUT ** -1.5
+TO_WAVES = GRID ** -1.5
 VMEM_LIMIT = 56 * 1024 * 1024
 
 
@@ -33,17 +36,15 @@
     turns = (freq[:, None] * np.arange(GRID)[None, :]) % GRID
     cos = np.cos(2 * np.pi * turns / GRID)
     sin = np.sin(2 * np.pi * turns / GRID)
-    up = CUT ** -0.5
-    down = GRID ** -0.5
     planes = np.concatenate([np.arange(0, GRID, 2), np.arange(1, GRID, 2)])
     cz, sz = cos[:, planes], sin[:, planes]
-    fz = up * np.block([[cz.T, -sz.T], [sz.T, cz.T]])
-    fy = up * np.block([[cos, sin], [-sin, cos]])
-    fx = up * np.concatenate([cos.T, sin.T], 1)
-    bx = down * np.concatenate([cos, sin], 0)
-    by = down * np.block([[cos.T, -sin.T], [sin.T, cos.T]])
-    bz = down * np.block([[cz.T, -sz.T], [sz.T, cz.T]])
-    return {k: halves(v) for k, v in dict(fz=fz, fy=fy, fx=fx, bx=bx, by=by, bz=bz).items()}
+    tables = dict(
+        z=np.block([[cz.T, -sz.T], [sz.T, cz.T]]),
+        y=np.block([[cos, sin], [-sin, cos]]),
+        fx=np.concatenate([cos.T, sin.T], 1),
+        bx=np.concatenate([cos, sin], 0),
+    )
+    return {name: halves(table) for name, table in tables.items()}
 
 
 TABLES = make_tables()
@@ -65,6 +66,14 @@
 
 def mm_tn(a, b):
     return lax.dot_general(a, b, (((0,), (0,)), ((), ())), preferred_element_type=F32)
+
+
+def mm_three(table_high, table_low, high, low):
+    return mm(jnp.concatenate([table_high, table_low, table_high], 1), jnp.concatenate([high, high, low], 0))
+
+
+def mm_three_right(high, low, table_high, table_low):
+    return mm(jnp.concatenate([high, low, high], 1), jnp.concatenate([table_high, table_high, table_low], 0))
 
 
 def lane_iota(shape):
@@ -84,9 +93,8 @@
 
 
 def swap_parts(value, first_sign):
-    rolled = pltpu.roll(value, 64, 1)
-    first = lane_iota(value.shape) < 64
-    return jnp.where(first, first_sign * rolled, -first_sign * rolled)
+    sign = jnp.where(lane_iota(value.shape) < 64, first_sign, -first_sign)
+    return pltpu.roll(value, 64, 1) * sign
 
 
 def block_ones():
@@ -118,9 +126,9 @@
     for b in range(BANDS):
         a = jnp.concatenate([coef_ref[0, b], coef_ref[1, b]], 1)
         ah, al = split(a)
-        res = mm_nt(th, ah) + mm_nt(tl, ah) + mm_nt(th, al)
+        res = mm_nt(jnp.concatenate([th, tl, th], 1), jnp.concatenate([ah, ah, al], 1))
         for q in range(4):
-            out_ref[pl.ds(q * 8 + b, 128, stride=32), :] = res[q * 128:(q + 1) * 128]
+            out_ref[pl.ds(q * 8 + b, 128, stride=32), :] = TO_GRID * res[q * 128:(q + 1) * 128]
 
 
 def grid_kernel(
@@ -128,7 +136,7 @@
     recv_ref, pot_ref, value_ref, group_ref, window_ref,
     yh_ref, yl_ref, xh_ref, xl_ref,
     field_hbm, partial_ref, c1, c2, c3, c4, d1, d2, d3, d4,
-    ah_s, al_s, ys_s, inh_s, inl_s, u_s, w_s, ga_s, gb_s, z_s, sem,
+    ah_s, al_s, ys_s, inha_s, inla_s, inhb_s, inlb_s, u_s, w_s, ga_s, gb_s, z_s, sem,
 ):
     yh, yl = yh_ref[...], yl_ref[...]
     piece = lax.broadcasted_iota(jnp.int32, (32, 128), 0)
@@ -140,47 +148,50 @@
                 h, l = split(part)
                 ah_s[b * 128:(b + 1) * 128, r * 128:(r + 1) * 128] = h
                 al_s[b * 128:(b + 1) * 128, r * 128:(r + 1) * 128] = l
-        ah, al = ah_s[...], al_s[...]
-        ys_s[...] = mm(ah, yh) + mm(al, yh) + mm(ah, yl)
-        for half in range(2):
-            def permute(kc, carry, half=half):
-                base = pl.multiple_of(kc * 16, 16)
-                ins = [
-                    ys_s[pl.ds((i % 8) * 128 + base, 16), ((i // 8) * 2 + half) * 128:((i // 8) * 2 + half + 1) * 128]
-                    for i in range(16)
-                ]
-                outs = exchange_blocks(ins)
-                for j, v in enumerate(outs):
-                    s = swap_parts(v, -1.0)
-                    pair = half * 8 + j // 2
-                    cols = slice((j % 2) * 128, (j % 2 + 1) * 128)
-                    vh, vl = split(v)
-                    sh, sl = split(s)
-                    inh_s[pair, pl.ds(base, 16), cols] = vh
-                    inl_s[pair, pl.ds(base, 16), cols] = vl
-                    inh_s[pair, pl.ds(128 + base, 16), cols] = sh
-                    inl_s[pair, pl.ds(128 + base, 16), cols] = sl
-                return carry
-
-            lax.fori_loop(0, 8, permute, 0)
-
-        def along_x(pair, carry, zz=zz):
-            xh, xl = xh_ref[...], xl_ref[...]
-            bh, bl = inh_s[pair], inl_s[pair]
-            res = mm(xh, bh) + mm(xl, bh) + mm(xh, bl)
-            for k in range(2):
-                yg = pair * 2 + k
-                pot = pot_ref[zz, pl.ds(pl.multiple_of(yg * 8, 8), 8), :]
-                pa, pb, pc = three(pot)
-                pieces = jnp.concatenate([pa.astype(F32), pb.astype(F32), pc.astype(F32), jnp.zeros((8, 256), F32)], 0)
-                spread = mm_tn(pieces.astype(BF16), pick_group)
-                u = res[:, k * 128:(k + 1) * 128]
-                at = pl.multiple_of((zz * 32 + yg) * 256, 256)
-                u_s[pl.ds(at, 256), :] = u
-                w_s[pl.ds(at, 256), :] = u * spread
+        ys_s[zz] = mm_three_right(ah_s[...], al_s[...], yh, yl)
+
+    def permute(unit, kc):
+        zz, half = unit // 2, unit % 2
+        base = pl.multiple_of(kc * 16, 16)
+        ins = [
+            ys_s[zz, pl.ds((i % 8) * 128 + base, 16), ((i // 8) * 2 + half) * 128:((i // 8) * 2 + half + 1) * 128]
+            for i in range(16)
+        ]
+        for j, v in enumerate(exchange_blocks(ins)):
+            cols = slice((j % 2) * 128, (j % 2 + 1) * 128)
+            vh, vl = split(v)
+            sh, sl = split(swap_parts(v, -1.0))
+            inh_s, inl_s = buffers[unit % 2]
+            inh_s[j // 2, pl.ds(base, 16), cols] = vh
+            inl_s[j // 2, pl.ds(base, 16), cols] = vl
+            inh_s[j // 2, pl.ds(128 + base, 16), cols] = sh
+            inl_s[j // 2, pl.ds(128 + base, 16), cols] = sl
+
+    def along_x(unit, pair):
+        zz, half = unit // 2, unit % 2
+        inh_s, inl_s = buffers[unit % 2]
+        res = mm_three(xh_ref[...], xl_ref[...], inh_s[pair], inl_s[pair])
+        for k in range(2):
+            yg = half * 16 + pair * 2 + k
+            pot = pot_ref[zz, pl.ds(pl.multiple_of(yg * 8, 8), 8), :]
+            pa, pb, pc = three(pot)
+            pieces = jnp.concatenate([pa.astype(F32), pb.astype(F32), pc.astype(F32), jnp.zeros((8, 256), F32)], 0)
+            spread = mm_tn(pieces.astype(BF16), pick_group)
+            u = res[:, k * 128:(k + 1) * 128]
+            at = pl.multiple_of((zz * 32 + yg) * 256, 256)
+            u_s[pl.ds(at, 256), :] = u
+            w_s[pl.ds(at, 256), :] = u * spread
+
+    buffers = ((inha_s, inla_s), (inhb_s, inlb_s))
+    for unit in range(-1, 4):
+        def step(i, carry, unit=unit):
+            if unit >= 0:
+                along_x(unit, i)
+            if unit < 3:
+                permute(unit + 1, i)
             return carry
 
-        lax.fori_loop(0, 16, along_x, 0)
+        lax.fori_loop(0, 8, step, 0, unroll=UNROLL)
     out_copy = pltpu.make_async_copy(w_s, field_hbm, sem)
     out_copy.start()
 
@@ -237,7 +248,7 @@
     xh_ref, xl_ref, yh_ref, yl_ref,
     field_hbm,
     out_ref, becp_ref,
-    w_s, tot_s, f_s, gat_s, ta_s, tb_s, xb_s, ah_s, al_s, sem,
+    w_s, tot_s, f_s, gat_s, ta_s, tb_s, xa_s, xb_s, ah_s, al_s, sem,
 ):
     in_copy = pltpu.make_async_copy(field_hbm, w_s, sem)
     in_copy.start()
@@ -297,38 +308,46 @@
     in_copy.wait()
     lax.fori_loop(0, (count + 1) // 2, two_slots, 0)
 
-    for zz in range(2):
-        def along_x(pair, carry, zz=zz):
-            xh, xl = xh_ref[...], xl_ref[...]
-            at = pl.multiple_of((zz * 32 + pair * 2) * 256, 256)
-            h0, l0 = split(w_s[pl.ds(at, 256), :])
-            h1, l1 = split(w_s[pl.ds(at + 256, 256), :])
-            bh, bl = jnp.concatenate([h0, h1], 1), jnp.concatenate([l0, l1], 1)
-            res = mm(xh, bh) + mm(xl, bh) + mm(xh, bl)
-            for k in range(2):
-                cols = slice(k * 128, (k + 1) * 128)
-                xb_s[pair * 2 + k] = res[:128, cols] + swap_parts(res[128:, cols], 1.0)
+    def along_x(unit, pair):
+        zz, half = unit // 2, unit % 2
+        at = pl.multiple_of((zz * 32 + half * 16 + pair * 2) * 256, 256)
+        h0, l0 = split(w_s[pl.ds(at, 256), :])
+        h1, l1 = split(w_s[pl.ds(at + 256, 256), :])
+        bh, bl = jnp.concatenate([h0, h1], 1), jnp.concatenate([l0, l1], 1)
+        res = mm_three(xh_ref[...], xl_ref[...], bh, bl)
+        for k in range(2):
+            cols = slice(k * 128, (k + 1) * 128)
+            buffers[unit % 2][pair * 2 + k] = res[:128, cols] + swap_parts(res[128:, cols], 1.0)
+
+    def permute(unit, kc):
+        half = unit % 2
+        base = pl.multiple_of(kc * 16, 16)
+        ins = [buffers[unit % 2][j, pl.ds(base, 16), :] for j in range(16)]
+        for i, v in enumerate(exchange_blocks(ins)):
+            vh, vl = split(v)
+            lo = ((i // 8) * 2 + half) * 128
+            ah_s[pl.ds((i % 8) * 128 + base, 16), lo:lo + 128] = vh
+            al_s[pl.ds((i % 8) * 128 + base, 16), lo:lo + 128] = vl
+
+    buffers = (xa_s, xb_s)
+    for unit in range(-1, 4):
+        def step(i, carry, unit=unit):
+            if unit < 3:
+                along_x(unit + 1, i)
+            if unit >= 0:
+                permute(unit, i)
             return carry
 
-        lax.fori_loop(0, 16, along_x, 0)
-        for half in range(2):
-            def permute(kc, carry, half=half):
-                base = pl.multiple_of(kc * 16, 16)
-                ins = [xb_s[half * 16 + j, pl.ds(base, 16), :] for j in range(16)]
-                for i, v in enumerate(exchange_blocks(ins)):
-                    vh, vl = split(v)
-                    lo = ((i // 8) * 2 + half) * 128
-                    ah_s[pl.ds((i % 8) * 128 + base, 16), lo:lo + 128] = vh
-                    al_s[pl.ds((i % 8) * 128 + base, 16), lo:lo + 128] = vl
-                return carry
-
-            lax.fori_loop(0, 8, permute, 0)
-        ah, al = ah_s[...], al_s[...]
-        yh, yl = yh_ref[...], yl_ref[...]
-        res = mm(ah, yh) + mm(al, yh) + mm(ah, yl)
-        for b in range(BANDS):
-            for o in range(2):
-                out_ref[pl.ds(o * 16 + zz * 8 + b, 128, stride=32), :] = res[b * 128:(b + 1) * 128, o * 128:(o + 1) * 128]
+        lax.fori_loop(0, 8, step, 0, unroll=UNROLL)
+        if unit in (1, 3):
+            zz = unit // 2
+            yh, yl = yh_ref[...], yl_ref[...]
+            ah, al = ah_s[...], al_s[...]
+            res = mm_nt(jnp.concatenate([ah, al, ah], 1), jnp.concatenate([yh, yh, yl], 1))
+            for b in range(BANDS):
+                for o in range(2):
+                    part = res[b * 128:(b + 1) * 128, o * 128:(o + 1) * 128]
+                    out_ref[pl.ds(o * 16 + zz * 8 + b, 128, stride=32), :] = part
 
 
 def spectrum_kernel(recv_ref, coef_ref, kin_ref, th_ref, tl_ref, out_ref):
@@ -337,14 +356,15 @@
     for b in range(BANDS):
         parts = [recv_ref[pl.ds(q * 8 + b, 128, stride=32), :] for q in range(4)]
         ah, al = split(jnp.concatenate(parts, 0))
-        res = mm_tn(ah, th) + mm_tn(al, th) + mm_tn(ah, tl)
+        res = mm_tn(jnp.concatenate([ah, al, ah], 0), jnp.concatenate([th, th, tl], 0))
         for o in range(2):
-            out_ref[o, b] = res[:, o * 128:(o + 1) * 128] + kin * coef_ref[o, b]
+            out_ref[o, b] = TO_WAVES * res[:, o * 128:(o + 1) * 128] + kin * coef_ref[o, b]
 
 
 VM = pl.BlockSpec(memory_space=pltpu.VMEM)
 SM = pl.BlockSpec(memory_space=pltpu.SMEM)
 ANY = pl.BlockSpec(memory_space=pl.ANY)
+SEND = pltpu.VMEM((4096, 128), F32)
 
 
 def params():
@@ -354,47 +374,48 @@
 def run_columns(coef):
     return pl.pallas_call(
         columns_kernel,
-        out_shape=jax.ShapeDtypeStruct((4096, 128), F32),
+        out_shape=SEND,
         in_specs=[VM] * 3, out_specs=VM, compiler_params=params(), name="columns",
-    )(coef, *TABLES["fz"])
+    )(coef, *TABLES["z"])
 
 
 def run_grid(rows, count, recv, pot, value, group, window):
     return pl.pallas_call(
         grid_kernel,
         out_shape=[jax.ShapeDtypeStruct((ROWS, 128), F32)] + [
-            jax.ShapeDtypeStruct((blocks * 16, 128), F32) for blocks in (5, 4, 3, 2, 1, 4, 3, 2, 1)
+            pltpu.VMEM((blocks * 16, 128), F32) for blocks in (5, 4, 3, 2, 1, 4, 3, 2, 1)
         ],
         in_specs=[SM, SM] + [VM] * 9,
         out_specs=[ANY] + [VM] * 9,
         scratch_shapes=[
             pltpu.VMEM((1024, 256), BF16), pltpu.VMEM((1024, 256), BF16),
-            pltpu.VMEM((1024, 512), F32),
-            pltpu.VMEM((16, 256, 256), BF16), pltpu.VMEM((16, 256, 256), BF16),
+            pltpu.VMEM((2, 1024, 512), F32),
+            pltpu.VMEM((8, 256, 256), BF16), pltpu.VMEM((8, 256, 256), BF16),
+            pltpu.VMEM((8, 256, 256), BF16), pltpu.VMEM((8, 256, 256), BF16),
             pltpu.VMEM((ROWS, 128), F32), pltpu.VMEM((ROWS, 128), F32),
             pltpu.VMEM((NPTS, 128), F32), pltpu.VMEM((NPTS, 128), F32), pltpu.VMEM((SLOTS * 8, 128), F32),
             pltpu.SemaphoreType.DMA(()),
         ],
         compiler_params=params(), name="grid",
-    )(rows, count, recv, pot, value, group, window, *TABLES["fy"], *TABLES["fx"])
+    )(rows, count, recv, pot, value, group, window, *TABLES["y"], *TABLES["fx"])
 
 
 def run_back(rows, count, partials, mask, strength, window, value, group, rowf, field):
     return pl.pallas_call(
         back_kernel,
-        out_shape=(jax.ShapeDtypeStruct((4096, 128), F32), jax.ShapeDtypeStruct((16, 128), F32)),
+        out_shape=(SEND, jax.ShapeDtypeStruct((16, 128), F32)),
         in_specs=[SM, SM] + [VM] * 19 + [ANY],
         out_specs=(VM, VM),
         scratch_shapes=[
             pltpu.VMEM((ROWS, 128), F32), pltpu.VMEM((WINDOW * 16, 128), F32),
             pltpu.VMEM((SLOTS * 8, 128), F32), pltpu.VMEM((NPTS, 128), F32),
             pltpu.VMEM((NPTS, 128), F32), pltpu.VMEM((NPTS, 128), F32),
-            pltpu.VMEM((32, 128, 128), F32),
+            pltpu.VMEM((16, 128, 128), F32), pltpu.VMEM((16, 128, 128), F32),
             pltpu.VMEM((1024, 512), BF16), pltpu.VMEM((1024, 512), BF16),
             pltpu.SemaphoreType.DMA(()),
         ],
         compiler_params=params(), name="back",
-    )(rows, count, *partials, mask, strength, window, value, group, rowf, *TABLES["bx"], *TABLES["by"], field)
+    )(rows, count, *partials, mask, strength, window, value, group, rowf, *TABLES["bx"], *TABLES["y"], field)
 
 
 def run_spectrum(recv, coef, kin):
@@ -402,18 +423,19 @@
         spectrum_kernel,
         out_shape=jax.ShapeDtypeStruct((2, BANDS, 128, 128), F32),
         in_specs=[VM] * 5, out_specs=VM, compiler_params=params(), name="spectrum",
-    )(recv, coef, kin, *TABLES["bz"])
+    )(recv, coef, kin, *TABLES["z"])
 
 
 def to_all(block):
     block = block.reshape(128, 32, 128)
     block = lax.all_to_all(block, "pencil", split_axis=0, concat_axis=0, tiled=True)
-    return block.reshape(4096, 128)
+    return pltpu.with_memory_space_constraint(block.reshape(4096, 128), pltpu.VMEM)
 
 
 def from_offset(block, delta):
     n = lax.axis_size("pencil")
-    return lax.ppermute(block, "pencil", [((i + delta) % n, i) for i in range(n)])
+    block = lax.ppermute(block, "pencil", [((i + delta) % n, i) for i in range(n)])
+    return pltpu.with_memory_space_constraint(block, pltpu.VMEM)
 
 
 def per_device(coefficients, potential, slot_atom, slot_count, point_offset, proj_value, proj_strength, proj_count):
@@ -434,9 +456,11 @@
     kinetic = 6.0 / (CUT * CUT) * ((freq_x * freq_x + freq * freq)[:, None] + (freq * freq)[None, :]).astype(F32)
 
     recv = to_all(run_columns(coefficients))
+    prepared = (recv, rows, group, rowf, window, strength, mask, kinetic)
+    recv, rows, group, rowf, window, strength, mask, kinetic = lax.optimization_barrier(prepared)
     field, partial, *windows = run_grid(rows, slot_count, recv, potential, proj_value, group, window)
     deltas = (1, 2, 3, 4, -1, -2, -3, -4)
-    partials = [partial] + [from_offset(block, delta) for block, delta in zip(windows, deltas)]
+    partials = [pltpu.with_memory_space_constraint(partial, pltpu.VMEM)] + [from_offset(block, delta) for block, delta in zip(windows, deltas)]
     send, becp = run_back(rows, slot_count, partials, mask, strength, window, proj_value, group, rowf, field)
     recv = to_all(send)
     return run_spectrum(recv, coefficients, kinetic), becp

time: 216 us -> 188 us (0.87)
  blocking collectives: 0 us -> 58 us
  Pallas kernels: 88.8 us -> 52.4 us
  waiting for transfers between devices: 64.1 us -> 34.5 us
  starting transfers between devices: 52.7 us -> 36.9 us
  local copies, waits for them, and re-layouts: 6.82 us -> 3.53 us
    all_to_all x0 -> x1, blocking collectives: none -> 58 us  [to_all(): lax.all_to_all(block, 'pencil', split_axis=0, concat_axis=0, tiled=True)]
    all_to_all x2 -> x1, waiting for transfers between devices: 56.7 us -> 24.3 us  [to_all(): lax.all_to_all(block, 'pencil', split_axis=0, concat_axis=0, tiled=True)]
    all_to_all x2 -> x1, starting transfers between devices: 36.8 us -> 11.5 us  [to_all(): lax.all_to_all(block, 'pencil', split_axis=0, concat_axis=0, tiled=True)]
    pallas_call x2, Pallas kernels: 48.8 us -> 28.9 us  [the longest x1 23.4 us: run_back(): pl.pallas_call(back_kernel, out_shape=(SEND, jax.ShapeDtypeStruct((16, 12...]
    pallas_call x1, Pallas kernels: 35.1 us -> 19 us  [run_grid(): pl.pallas_call(grid_kernel, out_shape=[jax.ShapeDtypeStruct((ROWS, 128),...]
    ppermute x8, starting transfers between devices: 15.9 us -> 25.4 us  [from_offset(): lax.ppermute(block, 'pencil', [((i + delta) % n, i) for i in range(n)])]
    unnamed x30 -> x10, local copies, waits for them, and re-layouts: 4.3 us -> 1.01 us
    ppermute x8, waiting for transfers between devices: 7.42 us -> 10.2 us  [from_offset(): lax.ppermute(block, 'pencil', [((i + delta) % n, i) for i in range(n)])]
  transfers between devices with their start and end apart: 10 -> 9, of which waited for: 3 -> 3; matrix products, arithmetic and copies ran while one was open for 3% -> 3% of each run, Pallas kernels for 0% -> 0%
where the time goes in v3:
time: 188 us; the launch traced here: 189 us
  blocking collectives  58 us (31%)
  Pallas kernels  52.4 us (28%)
  starting transfers between devices  36.9 us (20%)
  waiting for transfers between devices  34.5 us (18%)
  local copies, waits for them, and re-layouts  3.53 us (2%)
  other arithmetic  2.65 us (1%)
    all_to_all x1, blocking collectives, to_all(): lax.all_to_all(block, 'pencil', split_axis=0, concat_axis=0, tiled=True)  58 us
    ppermute x8, starting transfers between devices, from_offset(): lax.ppermute(block, 'pencil', [((i + delta) % n, i) for i in range(n)])  25.4 us
    all_to_all x1, waiting for transfers between devices, to_all(): lax.all_to_all(block, 'pencil', split_axis=0, concat_axis=0, tiled=True)  24.3 us
    pallas_call x1, Pallas kernels, run_back(): pl.pallas_call(back_kernel, out_shape=(SEND, jax.ShapeDtypeStruct((16, 12...  23.4 us
    pallas_call x1, Pallas kernels, run_grid(): pl.pallas_call(grid_kernel, out_shape=[jax.ShapeDtypeStruct((ROWS, 128),...  19 us
    all_to_all x1, starting transfers between devices, to_all(): lax.all_to_all(block, 'pencil', split_axis=0, concat_axis=0, tiled=True)  11.5 us
    ppermute x8, waiting for transfers between devices, from_offset(): lax.ppermute(block, 'pencil', [((i + delta) % n, i) for i in range(n)])  10.2 us
    pallas_call x1, Pallas kernels, run_columns(): pl.pallas_call(columns_kernel, out_shape=SEND, in_specs=[VM] * 3, out_spe...  5.52 us
  transfers between devices with their start and end apart: 9, of which 3 were waited for; matrix products, arithmetic and copies ran while one was open for 3% of the time, Pallas kernels for 0%

profile of v3, /device:TPU:1, one launch (start us, length us, event | category | flops | bytes accessed | tf_op | source)
XLA Modules:
  0.0 189.4 jit_solution(15717337019034402955)
XLA Ops:
  0.6 0.0 copy-start
  0.6 5.5 %columns.1 = f32[4096,128]{1,0:T(8,128)} custom-call(f32[2,8,128,128]{3,2,1,0:T(8,128)} %coef_ref.3, bf16[512,256]{1,0:T(8,128)(2,1)} %constant.111.clone.th_ref, bf16[512,256]{1,0:T(8,128)(2,1)} %constant.112.clone.tl_ref), custom_call_target="tpu_custom_call" | custom-call | tf_op jit(solution)/shard_map/columns/pallas_call | solution.py:375
  6.2 0.0 copy-start.2
  6.2 0.0 copy-start.1
  6.2 11.5 %all-to-all-start = ((f32[128,32,128]{2,1,0:T(8,128)}), f32[128,32,128]{2,1,0:T(8,128)S(1)}, u32[]{:S(2)}, u32[]{:S(2)}) async-start(f32[128,32,128]{2,1,0:T(8,128)} %bitcast), calls=%async_computation | async-start | bytes 4194304 | tf_op jit(solution)/shard_map/all_to_all | solution.py:431
  17.7 0.0 copy-start.3
  18.3 0.0 copy-done.2
  18.4 0.7 fusion
  19.0 0.7 copy.22
  19.7 0.0 copy-done.1
  19.7 0.3 copy.19
  20.0 0.0 copy-done
  20.1 1.1 gather_fusion.1
  21.2 0.6 gather_fusion
  21.8 0.1 copy.20
  21.9 0.0 copy-done.3
  21.9 0.6 fusion.7.window_ref
  22.5 0.7 compare_convert_fusion.mask_ref
  23.2 0.7 convert_multiply_fusion.kin_ref
  23.9 24.3 %all-to-all-done = f32[128,32,128]{2,1,0:T(8,128)S(1)} async-done(((f32[128,32,128]{2,1,0:T(8,128)}), f32[128,32,128]{2,1,0:T(8,128)S(1)}, u32[]{:S(2)}, u32[]{:S(2)}) %all-to-all-start) | async-done | bytes 2097184 | tf_op jit(solution)/shard_map/all_to_all | solution.py:431
  48.2 19.0 %grid.1 = (f32[16384,128]{1,0:T(8,128)}, f32[80,128]{1,0:T(8,128)S(1)}, f32[64,128]{1,0:T(8,128)S(1)}, f32[48,128]{1,0:T(8,128)S(1)}, f32[32,128]{1,0:T(8,128)S(...) custom-call(s32[16384]{0:T(1024)} %bitcast.16, ...), custom_call_target="tpu_custom_call" | custom-call | tf_op jit(solution)/shard_map/grid/pallas_call | solution.py:383
  67.2 5.5 %collective-permute-start.3 = (f32[16,128]{1,0:T(8,128)S(1)}, f32[16,128]{1,0:T(8,128)S(1)}, u32[]{:S(2)}, u32[]{:S(2)}) collective-permute-start(f32[16,128]{1,0:T(8,128)S(1)} %get-tuple-element.30), channel_id=1, source_target_pairs={{4,0},{5,1},{6,2},{7,3},{8,4},{9,5},{10,6},{11,7},{12,8},{13,9},{1... | collective-permute-start | bytes 24584 | tf_op jit(solution)/shard_map/ppermute | solution.py:437
  72.6 12.1 %collective-permute-start.2 = (f32[32,128]{1,0:T(8,128)S(1)}, f32[32,128]{1,0:T(8,128)S(1)}, u32[]{:S(2)}, u32[]{:S(2)}) collective-permute-start(f32[32,128]{1,0:T(8,128)S(1)} %get-tuple-element.29), channel_id=1, source_target_pairs={{3,0},{4,1},{5,2},{6,3},{7,4},{8,5},{9,6},{10,7},{11,8},{12,9},{13... | collective-permute-start | bytes 49160 | tf_op jit(solution)/shard_map/ppermute | solution.py:437
  84.7 2.6 %collective-permute-start.7 = (f32[16,128]{1,0:T(8,128)S(1)}, f32[16,128]{1,0:T(8,128)S(1)}, u32[]{:S(2)}, u32[]{:S(2)}) collective-permute-start(f32[16,128]{1,0:T(8,128)S(1)} %get-tuple-element.34), channel_id=1, source_target_pairs={{124,0},{125,1},{126,2},{127,3},{0,4},{1,5},{2,6},{3,7},{4,8},{5,9... | collective-permute-start | bytes 24584 | tf_op jit(solution)/shard_map/ppermute | solution.py:437
  87.3 0.0 collective-permute-start
  87.3 1.7 collective-permute-start.4
  89.0 0.0 collective-permute-done.3.p4
  89.1 3.5 %collective-permute-start.1 = (f32[48,128]{1,0:T(8,128)S(1)}, f32[48,128]{1,0:T(8,128)S(1)}, u32[]{:S(2)}, u32[]{:S(2)}) collective-permute-start(f32[48,128]{1,0:T(8,128)S(1)} %get-tuple-element.28), channel_id=1, source_target_pairs={{2,0},{3,1},{4,2},{5,3},{6,4},{7,5},{8,6},{9,7},{10,8},{11,9},{12,... | collective-permute-start | bytes 73736 | tf_op jit(solution)/shard_map/ppermute | solution.py:437
  92.5 0.4 collective-permute-done.7.m4
  93.0 0.0 collective-permute-start.5
  93.0 0.0 collective-permute-done.2.p3
  93.0 0.0 collective-permute-start.6
  93.0 0.7 copy.21.strength_ref
  93.7 9.8 %collective-permute-done.6.m3 = f32[32,128]{1,0:T(8,128)S(1)} collective-permute-done((f32[32,128]{1,0:T(8,128)S(1)}, f32[32,128]{1,0:T(8,128)S(1)}, u32[]{:S(2)}, u32[]{:S(2)}) %collective-permute-start.6) | collective-permute-done | bytes 16416 | tf_op jit(solution)/shard_map/ppermute | solution.py:437
  103.5 0.0 collective-permute-done.1.p2
  103.5 0.0 collective-permute-done.5.m2
  103.5 0.0 collective-permute-done.p1
  103.5 0.0 collective-permute-done.4.m1
  103.5 23.4 %back.1 = (f32[4096,128]{1,0:T(8,128)S(1)}, f32[16,128]{1,0:T(8,128)}) custom-call(s32[16384]{0:T(1024)} %bitcast.17, s32[1]{0:T(128)S(6)} %copy.23.count_sm, f32[80,128]{1,0:T(8,128)S(1)} %get-tuple-element.26.own_ref, f32[64,128]{1,0:T(8,128)S(1)} %collective-permute-done.p1, f32[48,128]{1,0:T(8,128)S(1)} %collective-permute-done.1.p2, ...), custom_call_target="tpu_custom_call" | custom-call | tf_op jit(solution)/shard_map/back/pallas_call | solution.py:404
  126.9 58.0 %all_to_all.10 = f32[128,32,128]{2,1,0:T(8,128)S(1)} all-to-all(f32[128,32,128]{2,1,0:T(8,128)S(1)} %bitcast.15), channel_id=1, replica_groups=mesh['pencil'=128] {'pencil'}, dimensions={0} | all-to-all | bytes 4194304 | tf_op jit(solution)/shard_map/all_to_all | solution.py:431
  185.0 4.4 %spectrum.1 = f32[2,8,128,128]{3,2,1,0:T(8,128)} custom-call(f32[4096,128]{1,0:T(8,128)S(1)} %bitcast.13, f32[2,8,128,128]{3,2,1,0:T(8,128)} %coef_ref.3, f32[128,128]{1,0:T(8,128)} %convert_multiply_fusion.kin_ref, bf16[512,256]{1,0:T(8,128)(2,1)} %constant.111.clone.th_ref, bf16[512,256]{1,0:T(8,128)(2,1)} %constant.112.clone.tl_ref), custom_call_target="tpu_custom_call" | custom-call | tf_op jit(solution)/shard_map/spectrum/pallas_call | solution.py:422
  (5 shorter events, 0.0 us)
Async XLA Ops:
  0.6 19.4 %copy-start = (s32[2048]{0:T(1024)S(1)}, s32[2048]{0:T(1024)}, u32[]{:S(2)}) copy-start(s32[2048]{0:T(1024)} %param.23) | copy-start | bytes 24580
  6.2 12.2 %copy-start.2 = (s32[64,256]{1,0:T(8,128)S(1)}, s32[64,256]{1,0:T(8,128)}, u32[]{:S(2)}) copy-start(s32[64,256]{1,0:T(8,128)} %param.20) | copy-start | bytes 196612
  6.2 13.5 %copy-start.1 = (f32[2048,8]{0,1:T(8,128)S(1)}, f32[2048,8]{0,1:T(8,128)}, u32[]{:S(2)}) copy-start(f32[2048,8]{0,1:T(8,128)} %param.22) | copy-start | bytes 196612
  6.2 42.0 %all-to-all-start = ((f32[128,32,128]{2,1,0:T(8,128)}), f32[128,32,128]{2,1,0:T(8,128)S(1)}, u32[]{:S(2)}, u32[]{:S(2)}) async-start(f32[128,32,128]{2,1,0:T(8,128)} %bitcast), calls=%async_computation | async-start | bytes 4194304 | tf_op jit(solution)/shard_map/all_to_all | solution.py:431
  17.7 4.2 %copy-start.3 = (s32[64]{0:T(128)S(1)}, s32[64]{0:T(128)}, u32[]{:S(2)}) copy-start(s32[64]{0:T(128)} %param.18) | copy-start | bytes 772
  67.2 21.9 %collective-permute-start.3 = (f32[16,128]{1,0:T(8,128)S(1)}, f32[16,128]{1,0:T(8,128)S(1)}, u32[]{:S(2)}, u32[]{:S(2)}) collective-permute-start(f32[16,128]{1,0:T(8,128)S(1)} %get-tuple-element.30), channel_id=1, source_target_pairs={{4,0},{5,1},{6,2},{7,3},{8,4},{9,5},{10,6},{11,7},{12,8},{13,9},{1... | collective-permute-start | bytes 24584 | tf_op jit(solution)/shard_map/ppermute | solution.py:437
  72.6 20.3 %collective-permute-start.2 = (f32[32,128]{1,0:T(8,128)S(1)}, f32[32,128]{1,0:T(8,128)S(1)}, u32[]{:S(2)}, u32[]{:S(2)}) collective-permute-start(f32[32,128]{1,0:T(8,128)S(1)} %get-tuple-element.29), channel_id=1, source_target_pairs={{3,0},{4,1},{5,2},{6,3},{7,4},{8,5},{9,6},{10,7},{11,8},{12,9},{13... | collective-permute-start | bytes 49160 | tf_op jit(solution)/shard_map/ppermute | solution.py:437
  84.7 8.2 %collective-permute-start.7 = (f32[16,128]{1,0:T(8,128)S(1)}, f32[16,128]{1,0:T(8,128)S(1)}, u32[]{:S(2)}, u32[]{:S(2)}) collective-permute-start(f32[16,128]{1,0:T(8,128)S(1)} %get-tuple-element.34), channel_id=1, source_target_pairs={{124,0},{125,1},{126,2},{127,3},{0,4},{1,5},{2,6},{3,7},{4,8},{5,9... | collective-permute-start | bytes 24584 | tf_op jit(solution)/shard_map/ppermute | solution.py:437
  87.3 16.2 %collective-permute-start = (f32[64,128]{1,0:T(8,128)S(1)}, f32[64,128]{1,0:T(8,128)S(1)}, u32[]{:S(2)}, u32[]{:S(2)}) collective-permute-start(f32[64,128]{1,0:T(8,128)S(1)} %get-tuple-element.27), channel_id=1, source_target_pairs={{1,0},{2,1},{3,2},{4,3},{5,4},{6,5},{7,6},{8,7},{9,8},{10,9},{11,1... | collective-permute-start | bytes 98312 | tf_op jit(solution)/shard_map/ppermute | solution.py:437
  87.3 16.2 %collective-permute-start.4 = (f32[64,128]{1,0:T(8,128)S(1)}, f32[64,128]{1,0:T(8,128)S(1)}, u32[]{:S(2)}, u32[]{:S(2)}) collective-permute-start(f32[64,128]{1,0:T(8,128)S(1)} %get-tuple-element.31), channel_id=1, source_target_pairs={{127,0},{0,1},{1,2},{2,3},{3,4},{4,5},{5,6},{6,7},{7,8},{8,9},{9,1... | collective-permute-start | bytes 98312 | tf_op jit(solution)/shard_map/ppermute | solution.py:437
  89.1 14.4 %collective-permute-start.1 = (f32[48,128]{1,0:T(8,128)S(1)}, f32[48,128]{1,0:T(8,128)S(1)}, u32[]{:S(2)}, u32[]{:S(2)}) collective-permute-start(f32[48,128]{1,0:T(8,128)S(1)} %get-tuple-element.28), channel_id=1, source_target_pairs={{2,0},{3,1},{4,2},{5,3},{6,4},{7,5},{8,6},{9,7},{10,8},{11,9},{12,... | collective-permute-start | bytes 73736 | tf_op jit(solution)/shard_map/ppermute | solution.py:437
  93.0 10.5 %collective-permute-start.5 = (f32[48,128]{1,0:T(8,128)S(1)}, f32[48,128]{1,0:T(8,128)S(1)}, u32[]{:S(2)}, u32[]{:S(2)}) collective-permute-start(f32[48,128]{1,0:T(8,128)S(1)} %get-tuple-element.32), channel_id=1, source_target_pairs={{126,0},{127,1},{0,2},{1,3},{2,4},{3,5},{4,6},{5,7},{6,8},{7,9},{8... | collective-permute-start | bytes 73736 | tf_op jit(solution)/shard_map/ppermute | solution.py:437
  93.0 10.5 %collective-permute-start.6 = (f32[32,128]{1,0:T(8,128)S(1)}, f32[32,128]{1,0:T(8,128)S(1)}, u32[]{:S(2)}, u32[]{:S(2)}) collective-permute-start(f32[32,128]{1,0:T(8,128)S(1)} %get-tuple-element.33), channel_id=1, source_target_pairs={{125,0},{126,1},{127,2},{0,3},{1,4},{2,5},{3,6},{4,7},{5,8},{6,9},... | collective-permute-start | bytes 49160 | tf_op jit(solution)/shard_map/ppermute | solution.py:437

commit v4 on v3

--- a/solution.py
+++ b/solution.py
@@ -19,9 +19,9 @@
 F32 = jnp.float32
 BF16 = jnp.bfloat16
 UNROLL = 4
+BATCH = 16
 TO_GRID = CUT ** -1.5
 TO_WAVES = GRID ** -1.5
-VMEM_LIMIT = 56 * 1024 * 1024
 
 
 def halves(table):
@@ -36,15 +36,8 @@
     turns = (freq[:, None] * np.arange(GRID)[None, :]) % GRID
     cos = np.cos(2 * np.pi * turns / GRID)
     sin = np.sin(2 * np.pi * turns / GRID)
-    planes = np.concatenate([np.arange(0, GRID, 2), np.arange(1, GRID, 2)])
-    cz, sz = cos[:, planes], sin[:, planes]
-    tables = dict(
-        z=np.block([[cz.T, -sz.T], [sz.T, cz.T]]),
-        y=np.block([[cos, sin], [-sin, cos]]),
-        fx=np.concatenate([cos.T, sin.T], 1),
-        bx=np.concatenate([cos, sin], 0),
-    )
-    return {name: halves(table) for name, table in tables.items()}
+    forward = np.block([[cos, sin], [-sin, cos]])
+    return dict(f=halves(forward), ft=halves(forward.T))
 
 
 TABLES = make_tables()
@@ -127,16 +120,42 @@
         a = jnp.concatenate([coef_ref[0, b], coef_ref[1, b]], 1)
         ah, al = split(a)
         res = mm_nt(jnp.concatenate([th, tl, th], 1), jnp.concatenate([ah, ah, al], 1))
-        for q in range(4):
-            out_ref[pl.ds(q * 8 + b, 128, stride=32), :] = TO_GRID * res[q * 128:(q + 1) * 128]
+        for o in range(2):
+            out_ref[pl.ds(o * 8 + b, 256, stride=16), :] = TO_GRID * res[o * 256:(o + 1) * 256]
+
+
+def slots_kernel(count_sm, value_ref, group_ref, rowf_ref, out_ref):
+    near = lax.broadcasted_iota(jnp.int32, (128, 128), 0) // BATCH == lane_iota((128, 128)) // BATCH
+    low_lane = lane_iota((128, 128)) < 64
+
+    def one_slot(s):
+        w = slot_weights(value_ref[s], group_ref[pl.ds(s, 1), :])
+        wh, wl = split(w)
+        both = jnp.concatenate([wh, wl], 0)
+        all_rows = rowf_ref[pl.ds(s, 1), :]
+        for h in range(2):
+            cols = slice(h * 128, (h + 1) * 128)
+            rows = jnp.broadcast_to(all_rows[:, cols], (128, 128))
+            same = jnp.where((rows == rows.T) & near, 1.0, 0.0).astype(BF16)
+            res = mm_nt(same, both[:, cols])
+            total = res + pltpu.roll(res, 64, 1)
+            high = total.astype(BF16).astype(F32)
+            out_ref[s, cols, :] = jnp.where(low_lane, high, total - high).astype(BF16)
+
+    def two_slots(i, carry):
+        one_slot(i * 2)
+        one_slot(i * 2 + 1)
+        return carry
+
+    lax.fori_loop(0, (count_sm[0] + 1) // 2, two_slots, 0)
 
 
 def grid_kernel(
     rows_sm, count_sm,
     recv_ref, pot_ref, value_ref, group_ref, window_ref,
-    yh_ref, yl_ref, xh_ref, xl_ref,
-    field_hbm, partial_ref, c1, c2, c3, c4, d1, d2, d3, d4,
-    ah_s, al_s, ys_s, inha_s, inla_s, inhb_s, inlb_s, u_s, w_s, ga_s, gb_s, z_s, sem,
+    yh_ref, yl_ref, th_ref, tl_ref,
+    w_ref, partial_ref,
+    ah_s, al_s, ys_s, inha_s, inla_s, inhb_s, inlb_s, u_s, ga_s, gb_s, z_s,
 ):
     yh, yl = yh_ref[...], yl_ref[...]
     piece = lax.broadcasted_iota(jnp.int32, (32, 128), 0)
@@ -144,7 +163,7 @@
     for zz in range(2):
         for b in range(BANDS):
             for r in range(2):
-                part = recv_ref[pl.ds(r * 16 + zz * 8 + b, 128, stride=32), :]
+                part = recv_ref[pl.ds(zz * 16 + r * 8 + b, 128, stride=32), :]
                 h, l = split(part)
                 ah_s[b * 128:(b + 1) * 128, r * 128:(r + 1) * 128] = h
                 al_s[b * 128:(b + 1) * 128, r * 128:(r + 1) * 128] = l
@@ -170,7 +189,9 @@
     def along_x(unit, pair):
         zz, half = unit // 2, unit % 2
         inh_s, inl_s = buffers[unit % 2]
-        res = mm_three(xh_ref[...], xl_ref[...], inh_s[pair], inl_s[pair])
+        xh = jnp.concatenate([th_ref[:256, :128], th_ref[256:, :128]], 1)
+        xl = jnp.concatenate([tl_ref[:256, :128], tl_ref[256:, :128]], 1)
+        res = mm_three(xh, xl, inh_s[pair], inl_s[pair])
         for k in range(2):
             yg = half * 16 + pair * 2 + k
             pot = pot_ref[zz, pl.ds(pl.multiple_of(yg * 8, 8), 8), :]
@@ -180,7 +201,7 @@
             u = res[:, k * 128:(k + 1) * 128]
             at = pl.multiple_of((zz * 32 + yg) * 256, 256)
             u_s[pl.ds(at, 256), :] = u
-            w_s[pl.ds(at, 256), :] = u * spread
+            w_ref[pl.ds(at, 256), :] = u * spread
 
     buffers = ((inha_s, inla_s), (inhb_s, inlb_s))
     for unit in range(-1, 4):
@@ -192,9 +213,6 @@
             return carry
 
         lax.fori_loop(0, 8, step, 0, unroll=UNROLL)
-    out_copy = pltpu.make_async_copy(w_s, field_hbm, sem)
-    out_copy.start()
-
     z_s[...] = jnp.zeros((SLOTS * 8, 128), F32)
     own = lane_iota((64, 128)) % 8 == lax.broadcasted_iota(jnp.int32, (64, 128), 0) // 8
 
@@ -233,32 +251,21 @@
     slot_terms = jnp.sum(jnp.where(mine, spread, 0.0).reshape(SLOTS, 8, 128), 1)
     onehot = (lax.broadcasted_iota(jnp.int32, (WINDOW * 16, SLOTS), 0) == window_ref[...]).astype(F32).astype(BF16)
     a, b, c = three(slot_terms)
-    partial = mm(onehot, a) + mm(onehot, b) + mm(onehot, c)
-    partial_ref[...] = partial
-    for delta, below, above in ((1, c1, d1), (2, c2, d2), (3, c3, d3), (4, c4, d4)):
-        below[...] = partial[:(WINDOW - delta) * 16]
-        above[...] = partial[delta * 16:]
-    out_copy.wait()
+    partial_ref[...] = mm(onehot, a) + mm(onehot, b) + mm(onehot, c)
 
 
 def back_kernel(
     rows_sm, count_sm,
-    own_ref, p1, p2, p3, p4, m1, m2, m3, m4,
-    mask_ref, strength_ref, window_ref, value_ref, group_ref, rowf_ref,
-    xh_ref, xl_ref, yh_ref, yl_ref,
-    field_hbm,
-    out_ref, becp_ref,
-    w_s, tot_s, f_s, gat_s, ta_s, tb_s, xa_s, xb_s, ah_s, al_s, sem,
+    near_ref, after_ref, before_ref,
+    mask_ref, strength_ref, window_ref, weight_ref,
+    yh_ref, yl_ref,
+    _,
+    out_ref, becp_ref, w_s,
+    tot_s, f_s, ta_s, tb_s, xa_s, xb_s, ah_s, al_s,
 ):
-    in_copy = pltpu.make_async_copy(field_hbm, w_s, sem)
-    in_copy.start()
-    tot_s[...] = own_ref[...]
-    for delta, ref in ((1, p1), (2, p2), (3, p3), (4, p4)):
-        n = (WINDOW - delta) * 16
-        tot_s[delta * 16:, :] = tot_s[delta * 16:, :] + ref[...]
-    for delta, ref in ((1, m1), (2, m2), (3, m3), (4, m4)):
-        n = (WINDOW - delta) * 16
-        tot_s[:n, :] = tot_s[:n, :] + ref[...]
+    tot_s[...] = near_ref[16:96]
+    tot_s[32:] = tot_s[32:] + after_ref[...]
+    tot_s[:48] = tot_s[:48] + before_ref[...]
     becp = jnp.where(mask_ref[...] > 0.0, tot_s[...], 0.0)
     becp_ref[...] = becp[REACH * 16:(REACH + 1) * 16]
     energy = becp * strength_ref[...]
@@ -272,29 +279,19 @@
     count = count_sm[0]
 
     def terms_of(s, buf):
-        w = slot_weights(value_ref[s], group_ref[pl.ds(s, 1), :])
-        wh, wl = split(w)
         f = f_s[pl.ds(pl.multiple_of(s * 8, 8), 8), :]
         f = jnp.where(s < count, f, 0.0)
         diag = jnp.where(own, jnp.concatenate([f] * 8, 0), 0.0)
-        dh, dl = split(diag)
-        terms = mm_tn(jnp.concatenate([wh, wl, wh], 0), jnp.concatenate([dh, dh, dl], 0))
-        rows = jnp.broadcast_to(rowf_ref[pl.ds(s, 1), :], (NPTS, NPTS))
-        same = (rows == rows.T).astype(F32).astype(BF16)
-        th, tl = split(terms)
-        both = mm(same, jnp.concatenate([th, tl], 1))
+        pieces = jnp.concatenate(split(diag), 1)
+        both = mm(weight_ref[s], jnp.concatenate([pieces, pieces], 0))
         buf[...] = both[:, :128] + both[:, 128:]
 
     def add_slot(s, buf):
-        for c in range(0, NPTS, 16):
-            vals = [w_s[pl.ds(rows_sm[s * NPTS + c + k], 1), :] for k in range(16)]
-            for k in range(16):
-                gat_s[c + k:c + k + 1, :] = vals[k]
-        gat_s[...] = gat_s[...] + buf[...]
-        for c in range(0, NPTS, 16):
-            vals = [gat_s[c + k:c + k + 1, :] for k in range(16)]
-            for k in range(16):
-                w_s[pl.ds(rows_sm[s * NPTS + c + k], 1), :] = vals[k]
+        for c in range(0, NPTS, BATCH):
+            at = [rows_sm[s * NPTS + c + k] for k in range(BATCH)]
+            vals = [w_s[pl.ds(at[k], 1), :] + buf[c + k:c + k + 1, :] for k in range(BATCH)]
+            for k in range(BATCH):
+                w_s[pl.ds(at[k], 1), :] = vals[k]
 
     def two_slots(i, carry):
         s = i * 2
@@ -305,7 +302,6 @@
         return carry
 
     terms_of(0, ta_s)
-    in_copy.wait()
     lax.fori_loop(0, (count + 1) // 2, two_slots, 0)
 
     def along_x(unit, pair):
@@ -314,7 +310,9 @@
         h0, l0 = split(w_s[pl.ds(at, 256), :])
         h1, l1 = split(w_s[pl.ds(at + 256, 256), :])
         bh, bl = jnp.concatenate([h0, h1], 1), jnp.concatenate([l0, l1], 1)
-        res = mm_three(xh_ref[...], xl_ref[...], bh, bl)
+        xh = jnp.concatenate([yh_ref[:128, :256], yh_ref[:128, 256:]], 0)
+        xl = jnp.concatenate([yl_ref[:128, :256], yl_ref[:128, 256:]], 0)
+        res = mm_three(xh, xl, bh, bl)
         for k in range(2):
             cols = slice(k * 128, (k + 1) * 128)
             buffers[unit % 2][pair * 2 + k] = res[:128, cols] + swap_parts(res[128:, cols], 1.0)
@@ -347,14 +345,14 @@
             for b in range(BANDS):
                 for o in range(2):
                     part = res[b * 128:(b + 1) * 128, o * 128:(o + 1) * 128]
-                    out_ref[pl.ds(o * 16 + zz * 8 + b, 128, stride=32), :] = part
+                    out_ref[pl.ds(zz * 16 + o * 8 + b, 128, stride=32), :] = part
 
 
 def spectrum_kernel(recv_ref, coef_ref, kin_ref, th_ref, tl_ref, out_ref):
     th, tl = th_ref[...], tl_ref[...]
     kin = kin_ref[...]
     for b in range(BANDS):
-        parts = [recv_ref[pl.ds(q * 8 + b, 128, stride=32), :] for q in range(4)]
+        parts = [recv_ref[pl.ds(o * 8 + b, 256, stride=16), :] for o in range(2)]
         ah, al = split(jnp.concatenate(parts, 0))
         res = mm_tn(jnp.concatenate([ah, al, ah], 0), jnp.concatenate([th, th, tl], 0))
         for o in range(2):
@@ -363,67 +361,73 @@
 
 VM = pl.BlockSpec(memory_space=pltpu.VMEM)
 SM = pl.BlockSpec(memory_space=pltpu.SMEM)
-ANY = pl.BlockSpec(memory_space=pl.ANY)
+FIELD = pltpu.VMEM((ROWS, 128), F32)
 SEND = pltpu.VMEM((4096, 128), F32)
 
 
-def params():
-    return pltpu.CompilerParams(vmem_limit_bytes=VMEM_LIMIT)
+def params(mebibytes):
+    return pltpu.CompilerParams(vmem_limit_bytes=mebibytes * 1024 * 1024)
 
 
 def run_columns(coef):
     return pl.pallas_call(
         columns_kernel,
-        out_shape=SEND,
-        in_specs=[VM] * 3, out_specs=VM, compiler_params=params(), name="columns",
-    )(coef, *TABLES["z"])
+        out_shape=jax.ShapeDtypeStruct((4096, 128), F32),
+        in_specs=[VM] * 3, out_specs=VM, compiler_params=params(56), name="columns",
+    )(coef, *TABLES["ft"])
 
 
 def run_grid(rows, count, recv, pot, value, group, window):
     return pl.pallas_call(
         grid_kernel,
-        out_shape=[jax.ShapeDtypeStruct((ROWS, 128), F32)] + [
-            pltpu.VMEM((blocks * 16, 128), F32) for blocks in (5, 4, 3, 2, 1, 4, 3, 2, 1)
-        ],
+        out_shape=(FIELD, pltpu.VMEM((WINDOW * 16, 128), F32)),
         in_specs=[SM, SM] + [VM] * 9,
-        out_specs=[ANY] + [VM] * 9,
+        out_specs=(VM, VM),
         scratch_shapes=[
             pltpu.VMEM((1024, 256), BF16), pltpu.VMEM((1024, 256), BF16),
             pltpu.VMEM((2, 1024, 512), F32),
             pltpu.VMEM((8, 256, 256), BF16), pltpu.VMEM((8, 256, 256), BF16),
             pltpu.VMEM((8, 256, 256), BF16), pltpu.VMEM((8, 256, 256), BF16),
-            pltpu.VMEM((ROWS, 128), F32), pltpu.VMEM((ROWS, 128), F32),
+            pltpu.VMEM((ROWS, 128), F32),
             pltpu.VMEM((NPTS, 128), F32), pltpu.VMEM((NPTS, 128), F32), pltpu.VMEM((SLOTS * 8, 128), F32),
-            pltpu.SemaphoreType.DMA(()),
         ],
-        compiler_params=params(), name="grid",
-    )(rows, count, recv, pot, value, group, window, *TABLES["y"], *TABLES["fx"])
-
-
-def run_back(rows, count, partials, mask, strength, window, value, group, rowf, field):
+        compiler_params=params(24), name="grid",
+    )(rows, count, recv, pot, value, group, window, *TABLES["f"], *TABLES["ft"])
+
+
+def run_slots(count, value, group, rowf):
+    return pl.pallas_call(
+        slots_kernel,
+        out_shape=pltpu.VMEM((SLOTS, NPTS, 128), BF16),
+        in_specs=[SM] + [VM] * 3, out_specs=VM, compiler_params=params(16), name="slots",
+        cost_estimate=pl.CostEstimate(flops=10 ** 10, transcendentals=0, bytes_accessed=5 * 10 ** 6),
+    )(count, value, group, rowf)
+
+
+def run_back(rows, count, partials, mask, strength, window, weights, field):
     return pl.pallas_call(
         back_kernel,
-        out_shape=(SEND, jax.ShapeDtypeStruct((16, 128), F32)),
-        in_specs=[SM, SM] + [VM] * 19 + [ANY],
-        out_specs=(VM, VM),
+        out_shape=(SEND, jax.ShapeDtypeStruct((16, 128), F32), FIELD),
+        in_specs=[SM, SM] + [VM] * 10,
+        out_specs=(VM, VM, VM),
+        input_output_aliases={11: 2},
         scratch_shapes=[
-            pltpu.VMEM((ROWS, 128), F32), pltpu.VMEM((WINDOW * 16, 128), F32),
-            pltpu.VMEM((SLOTS * 8, 128), F32), pltpu.VMEM((NPTS, 128), F32),
+            pltpu.VMEM((WINDOW * 16, 128), F32),
+            pltpu.VMEM((SLOTS * 8, 128), F32),
             pltpu.VMEM((NPTS, 128), F32), pltpu.VMEM((NPTS, 128), F32),
             pltpu.VMEM((16, 128, 128), F32), pltpu.VMEM((16, 128, 128), F32),
             pltpu.VMEM((1024, 512), BF16), pltpu.VMEM((1024, 512), BF16),
-            pltpu.SemaphoreType.DMA(()),
         ],
-        compiler_params=params(), name="back",
-    )(rows, count, *partials, mask, strength, window, value, group, rowf, *TABLES["bx"], *TABLES["y"], field)
+        compiler_params=params(14), name="back",
+    )(rows, count, *partials, mask, strength, window, weights, *TABLES["f"], field)
 
 
 def run_spectrum(recv, coef, kin):
     return pl.pallas_call(
         spectrum_kernel,
         out_shape=jax.ShapeDtypeStruct((2, BANDS, 128, 128), F32),
-        in_specs=[VM] * 5, out_specs=VM, compiler_params=params(), name="spectrum",
-    )(recv, coef, kin, *TABLES["z"])
+        in_specs=[VM] * 5, out_specs=VM, compiler_params=params(16), name="spectrum",
+    )(recv, coef, kin, *TABLES["ft"])
 
 
 def to_all(block):
@@ -434,8 +438,7 @@
 
 def from_offset(block, delta):
     n = lax.axis_size("pencil")
-    block = lax.ppermute(block, "pencil", [((i + delta) % n, i) for i in range(n)])
-    return pltpu.with_memory_space_constraint(block, pltpu.VMEM)
+    return lax.ppermute(block, "pencil", [((i + delta) % n, i) for i in range(n)])
 
 
 def per_device(coefficients, potential, slot_atom, slot_count, point_offset, proj_value, proj_strength, proj_count):
@@ -456,12 +459,16 @@
     kinetic = 6.0 / (CUT * CUT) * ((freq_x * freq_x + freq * freq)[:, None] + (freq * freq)[None, :]).astype(F32)
 
     recv = to_all(run_columns(coefficients))
-    prepared = (recv, rows, group, rowf, window, strength, mask, kinetic)
-    recv, rows, group, rowf, window, strength, mask, kinetic = lax.optimization_barrier(prepared)
-    field, partial, *windows = run_grid(rows, slot_count, recv, potential, proj_value, group, window)
-    deltas = (1, 2, 3, 4, -1, -2, -3, -4)
-    partials = [pltpu.with_memory_space_constraint(partial, pltpu.VMEM)] + [from_offset(block, delta) for block, delta in zip(windows, deltas)]
-    send, becp = run_back(rows, slot_count, partials, mask, strength, window, proj_value, group, rowf, field)
+    weights = pltpu.with_memory_space_constraint(run_slots(slot_count, proj_value, group, rowf), pltpu.VMEM)
+    prepared = (recv, rows, group, weights, window, strength, mask, kinetic)
+    recv, rows, group, weights, window, strength, mask, kinetic = lax.optimization_barrier(prepared)
+    field, partial = run_grid(rows, slot_count, recv, potential, proj_value, group, window)
+    wide = jnp.pad(partial, ((16, 16), (0, 0)))
+    wide = wide + jnp.pad(from_offset(partial, 1), ((32, 0), (0, 0))) + jnp.pad(from_offset(partial, -1), ((0, 32), (0, 0)))
+    partials = (wide, from_offset(wide[:48], 3), from_offset(wide[64:], -3))
+    partials = [pltpu.with_memory_space_constraint(block, pltpu.VMEM) for block in partials]
+    field = pltpu.with_memory_space_constraint(field, pltpu.VMEM)
+    send, becp, _ = run_back(rows, slot_count, partials, mask, strength, window, weights, field)
     recv = to_all(send)
     return run_spectrum(recv, coefficients, kinetic), becp
 

time: 188 us -> 178 us (0.947)
  local copies, waits for them, and re-layouts: 3.53 us -> 18.5 us
  starting transfers between devices: 36.9 us -> 25 us
  Pallas kernels: 52.4 us -> 42.5 us
  waiting for transfers between devices: 34.5 us -> 29 us
  blocking collectives: 58 us -> 60.9 us
  other arithmetic: 2.65 us -> 0.23 us
    unnamed x10 -> x34, local copies, waits for them, and re-layouts: 1.01 us -> 15.3 us
    ppermute x8 -> x4, starting transfers between devices: 25.4 us -> 13.6 us  [from_offset(): lax.ppermute(block, 'pencil', [((i + delta) % n, i) for i in range(n)])]
    pallas_call x1, Pallas kernels: 23.4 us -> 16.7 us  [run_back(): pl.pallas_call(back_kernel, out_shape=(SEND, jax.ShapeDtypeStruct((16, 12...]
    all_to_all x1, waiting for transfers between devices: 24.3 us -> 20.4 us  [to_all(): lax.all_to_all(block, 'pencil', split_axis=0, concat_axis=0, tiled=True)]
    all_to_all x1, blocking collectives: 58 us -> 60.9 us  [to_all(): lax.all_to_all(block, 'pencil', split_axis=0, concat_axis=0, tiled=True)]
    pallas_call x1, Pallas kernels: 4.43 us -> 2.46 us  [run_spectrum(): pl.pallas_call(spectrum_kernel, out_shape=jax.ShapeDtypeStruct((2, BANDS,...]
    ppermute x8 -> x4, waiting for transfers between devices: 10.2 us -> 8.67 us  [from_offset(): lax.ppermute(block, 'pencil', [((i + delta) % n, i) for i in range(n)])]
    pallas_call x2 -> x3, Pallas kernels: 24.5 us -> 23.4 us  [the longest x1 17 us: run_grid(): pl.pallas_call(grid_kernel, out_shape=(FIELD, pltpu.VMEM((WINDOW * 16, 12...]
  transfers between devices with their start and end apart: 9 -> 5, of which waited for: 3 -> 4; matrix products, arithmetic and copies ran while one was open for 3% -> 3% of each run, Pallas kernels for 0% -> 1%
where the time goes in v4:
time: 178 us
  blocking collectives  60.9 us (34%)
  Pallas kernels  42.5 us (24%)
  waiting for transfers between devices  29 us (16%)
  starting transfers between devices  25 us (14%)
  local copies, waits for them, and re-layouts  18.5 us (10%)
    all_to_all x1, blocking collectives, to_all(): lax.all_to_all(block, 'pencil', split_axis=0, concat_axis=0, tiled=True)  60.9 us
    all_to_all x1, waiting for transfers between devices, to_all(): lax.all_to_all(block, 'pencil', split_axis=0, concat_axis=0, tiled=True)  20.4 us
    pallas_call x1, Pallas kernels, run_grid(): pl.pallas_call(grid_kernel, out_shape=(FIELD, pltpu.VMEM((WINDOW * 16, 12...  17 us
    pallas_call x1, Pallas kernels, run_back(): pl.pallas_call(back_kernel, out_shape=(SEND, jax.ShapeDtypeStruct((16, 12...  16.7 us
    unnamed x34, local copies, waits for them, and re-layouts  15.3 us
    ppermute x4, starting transfers between devices, from_offset(): lax.ppermute(block, 'pencil', [((i + delta) % n, i) for i in range(n)])  13.6 us
    all_to_all x1, starting transfers between devices, to_all(): lax.all_to_all(block, 'pencil', split_axis=0, concat_axis=0, tiled=True)  11.5 us
    ppermute x4, waiting for transfers between devices, from_offset(): lax.ppermute(block, 'pencil', [((i + delta) % n, i) for i in range(n)])  8.67 us
  transfers between devices with their start and end apart: 5, of which 4 were waited for; matrix products, arithmetic and copies ran while one was open for 3% of the time, Pallas kernels for 1%

profile of v4, /device:TPU:1, one launch (start us, length us, event | category | flops | bytes accessed | tf_op | source)
XLA Modules:
  0.0 177.7 jit_solution(7897495928374777363)
XLA Ops:
  0.6 0.0 copy-start
  0.6 4.7 %columns.1 = f32[4096,128]{1,0:T(8,128)} custom-call(f32[2,8,128,128]{3,2,1,0:T(8,128)} %coef_ref.3, bf16[512,256]{1,0:T(8,128)(2,1)} %constant.106.clone.th_ref, bf16[512,256]{1,0:T(8,128)(2,1)} %constant.107.clone.tl_ref), custom_call_target="tpu_custom_call" | custom-call | tf_op jit(solution)/shard_map/columns/pallas_call | solution.py:373
  5.3 0.0 copy-start.14
  5.3 0.0 copy-start.13
  5.3 11.5 %all-to-all-start = ((f32[128,32,128]{2,1,0:T(8,128)}), f32[128,32,128]{2,1,0:T(8,128)S(1)}, u32[]{:S(2)}, u32[]{:S(2)}) async-start(f32[128,32,128]{2,1,0:T(8,128)} %bitcast.18), calls=%async_computation | async-start | bytes 4194304 | tf_op jit(solution)/shard_map/all_to_all | solution.py:435
  16.8 0.0 copy-start.15
  16.9 0.0 copy-done.14
  17.6 0.0 copy-done.13
  17.6 1.3 copy.16
  18.9 0.0 copy-done
  18.9 1.1 gather_fusion.1
  20.1 1.8 %gather_fusion = f32[80,8]{1,0:T(8,128)S(1)} fusion(f32[2048,8]{1,0:T(8,128)} %copy.16, s32[1024]{0:T(1024)S(1)} %pad_clamp_fusion), kind=kCustom, calls=%fused_computation | custom fusion | bytes 5440 | tf_op jit(solution)/shard_map/gather | solution.py:455
  21.9 0.1 copy.17
  22.0 0.0 copy-done.15
  22.0 0.1 compare_convert_fusion.mask_ref
  22.1 0.1 convert_multiply_fusion.kin_ref
  22.2 0.0 copy-start.11
  22.2 1.0 copy-done.11
  23.3 0.0 copy-start.6
  23.3 0.0 copy-start.7
  23.3 0.0 copy-start.8
  23.3 0.0 copy-start.9
  23.3 1.7 slots.1.weight_ref
  25.0 0.0 copy-start.3
  25.0 2.0 %copy-done.3 = bf16[64,256,128]{2,1,0:T(8,128)(2,1)} copy-done((bf16[64,256,128]{2,1,0:T(8,128)(2,1)}, bf16[64,256,128]{2,1,0:T(8,128)(2,1)S(1)}, u32[]{:S(2)}) %copy-start.3) | copy-done | bytes 4194328
  27.0 20.4 %all-to-all-done = f32[128,32,128]{2,1,0:T(8,128)S(1)} async-done(((f32[128,32,128]{2,1,0:T(8,128)}), f32[128,32,128]{2,1,0:T(8,128)S(1)}, u32[]{:S(2)}, u32[]{:S(2)}) %all-to-all-start) | async-done | bytes 2097184 | tf_op jit(solution)/shard_map/all_to_all | solution.py:435
  47.3 0.0 copy-done.6
  47.3 0.0 copy-done.7
  47.3 0.0 copy-done.8
  47.3 0.0 copy-done.9
  47.4 0.0 copy-start.10
  47.4 1.0 copy-done.10
  48.4 0.0 copy-start.12
  48.4 1.0 copy-done.12
  49.4 17.0 %grid.1 = (f32[16384,128]{1,0:T(8,128)S(1)}, f32[80,128]{1,0:T(8,128)S(1)}) custom-call(s32[16384]{0:T(1024)S(1)} %bitcast.16, s32[1]{0:T(128)S(6)} %copy.21.count_sm, f32[4096,128]{1,0:T(8,128)S(1)} %bitcast.13, f32[2,256,256]{2,1,0:T(8,128)S(1)} %copy-done.10, f32[64,8,256]{2,1,0:T(8,128)S(1)} %copy-done.12, s32[64,256]{1,0:T(8,128)S(1)} %get-tuple-element.16.group_ref, ...), custom_call_target="tpu_custom_call" | custom-call | tf_op jit(solution)/shard_map/grid/pallas_call | solution.py:381
  66.5 0.0 copy-start.1
  66.5 3.3 %copy-done.1 = f32[16384,128]{1,0:T(8,128)} copy-done((f32[16384,128]{1,0:T(8,128)}, f32[16384,128]{1,0:T(8,128)S(1)}, u32[]{:S(2)}) %copy-start.1) | copy-done | bytes 8388632
  69.7 0.4 collective-permute-start.1
  70.1 0.1 collective-permute-start
  70.3 1.0 collective-permute-done.1
  71.2 6.5 %collective-permute-done = f32[80,128]{1,0:T(8,128)S(1)} collective-permute-done((f32[80,128]{1,0:T(8,128)S(1)}, f32[80,128]{1,0:T(8,128)S(1)}, u32[]{:S(2)}, u32[]{:S(2)}) %collective-permute-start) | collective-permute-done | bytes 40992 | tf_op jit(solution)/shard_map/ppermute | solution.py:441
  77.8 1.4 collective-permute-start.3
  79.3 11.6 %collective-permute-start.2 = (f32[48,128]{1,0:T(8,128)S(1)}, f32[48,128]{1,0:T(8,128)S(1)}, u32[]{:S(2)}, u32[]{:S(2)}) collective-permute-start(f32[48,128]{1,0:T(8,128)S(1)} %get-tuple-element.30), channel_id=1, source_target_pairs={{3,0},{4,1},{5,2},{6,3},{7,4},{8,5},{9,6},{10,7},{11,8},{12,9},{13... | collective-permute-start | bytes 73736 | tf_op jit(solution)/shard_map/ppermute | solution.py:441
  90.8 0.1 copy.18.strength_ref
  90.9 1.2 collective-permute-done.3.before_ref
  92.1 0.0 collective-permute-done.2.after_ref
  92.1 0.0 copy-start.2
  92.1 3.4 %copy-done.2 = f32[16384,128]{1,0:T(8,128)S(1)} copy-done((f32[16384,128]{1,0:T(8,128)S(1)}, f32[16384,128]{1,0:T(8,128)}, u32[]{:S(2)}) %copy-start.2) | copy-done | bytes 8388632
  95.5 0.0 copy-start.4
  95.5 2.2 %copy-done.4 = bf16[64,256,128]{2,1,0:T(8,128)(2,1)S(1)} copy-done((bf16[64,256,128]{2,1,0:T(8,128)(2,1)S(1)}, bf16[64,256,128]{2,1,0:T(8,128)(2,1)}, u32[]{:S(2)}) %copy-start.4) | copy-done | bytes 4194328
  97.6 16.7 %back.1 = (f32[4096,128]{1,0:T(8,128)S(1)}, f32[16,128]{1,0:T(8,128)}, f32[16384,128]{1,0:T(8,128)S(1)}) custom-call(s32[16384]{0:T(1024)S(1)} %bitcast.17, s32[1]{0:T(128)S(6)} %copy.21.count_sm, f32[112,128]{1,0:T(8,128)S(1)} %pad_add_fusion.near_ref, f32[48,128]{1,0:T(8,128)S(1)} %collective-permute-done.2.after_ref, ...), custom_call_target="tpu_custom_call", output_to_operand_aliasing={{2}: (11, {})} | custom-call | tf_op jit(solution)/shard_map/back/pallas_call | solution.py:408
  114.3 0.0 copy-start.5
  114.3 60.9 %all_to_all.10 = f32[128,32,128]{2,1,0:T(8,128)S(1)} all-to-all(f32[128,32,128]{2,1,0:T(8,128)S(1)} %bitcast.15), channel_id=1, replica_groups=mesh['pencil'=128] {'pencil'}, dimensions={0} | all-to-all | bytes 4194304 | tf_op jit(solution)/shard_map/all_to_all | solution.py:435
  175.2 0.0 copy-done.5
  175.2 2.5 %spectrum.1 = f32[2,8,128,128]{3,2,1,0:T(8,128)} custom-call(f32[4096,128]{1,0:T(8,128)S(1)} %bitcast.14, f32[2,8,128,128]{3,2,1,0:T(8,128)S(1)} %copy-done.5, f32[128,128]{1,0:T(8,128)S(1)} %convert_multiply_fusion.kin_ref, bf16[512,256]{1,0:T(8,128)(2,1)S(1)} %copy-done.7, bf16[512,256]{1,0:T(8,128)(2,1)S(1)} %copy-done.6), custom_call_target="tpu_custom_call" | custom-call | tf_op jit(solution)/shard_map/spectrum/pallas_call | solution.py:426
  (10 shorter events, 0.1 us)
Async XLA Ops:
  0.6 18.3 %copy-start = (s32[2048]{0:T(1024)S(1)}, s32[2048]{0:T(1024)}, u32[]{:S(2)}) copy-start(s32[2048]{0:T(1024)} %param.19) | copy-start | bytes 24580
  5.3 11.5 %copy-start.14 = (s32[64,256]{1,0:T(8,128)S(1)}, s32[64,256]{1,0:T(8,128)}, u32[]{:S(2)}) copy-start(s32[64,256]{1,0:T(8,128)} %param.16) | copy-start | bytes 196612
  5.3 12.3 %copy-start.13 = (f32[2048,8]{0,1:T(8,128)S(1)}, f32[2048,8]{0,1:T(8,128)}, u32[]{:S(2)}) copy-start(f32[2048,8]{0,1:T(8,128)} %param.18) | copy-start | bytes 196612
  5.3 42.0 %all-to-all-start = ((f32[128,32,128]{2,1,0:T(8,128)}), f32[128,32,128]{2,1,0:T(8,128)S(1)}, u32[]{:S(2)}, u32[]{:S(2)}) async-start(f32[128,32,128]{2,1,0:T(8,128)} %bitcast.18), calls=%async_computation | async-start | bytes 4194304 | tf_op jit(solution)/shard_map/all_to_all | solution.py:435
  16.8 5.2 %copy-start.15 = (s32[64]{0:T(128)S(1)}, s32[64]{0:T(128)}, u32[]{:S(2)}) copy-start(s32[64]{0:T(128)} %param.14) | copy-start | bytes 772
  22.2 1.0 copy-start.11
  23.3 24.1 %copy-start.6 = (bf16[512,256]{1,0:T(8,128)(2,1)S(1)}, bf16[512,256]{1,0:T(8,128)(2,1)}, u32[]{:S(2)}) copy-start(bf16[512,256]{1,0:T(8,128)(2,1)} %constant.107.clone.tl_ref) | copy-start | bytes 786436
  23.3 24.1 %copy-start.7 = (bf16[512,256]{1,0:T(8,128)(2,1)S(1)}, bf16[512,256]{1,0:T(8,128)(2,1)}, u32[]{:S(2)}) copy-start(bf16[512,256]{1,0:T(8,128)(2,1)} %constant.106.clone.th_ref) | copy-start | bytes 786436
  23.3 24.1 %copy-start.8 = (bf16[256,512]{1,0:T(8,128)(2,1)S(1)}, bf16[256,512]{1,0:T(8,128)(2,1)}, u32[]{:S(2)}) copy-start(bf16[256,512]{1,0:T(8,128)(2,1)} %constant.109.clone.yl_ref) | copy-start | bytes 786436
  23.3 24.1 %copy-start.9 = (bf16[256,512]{1,0:T(8,128)(2,1)S(1)}, bf16[256,512]{1,0:T(8,128)(2,1)}, u32[]{:S(2)}) copy-start(bf16[256,512]{1,0:T(8,128)(2,1)} %constant.108.clone.yh_ref) | copy-start | bytes 786436
  25.0 2.0 %copy-start.3 = (bf16[64,256,128]{2,1,0:T(8,128)(2,1)}, bf16[64,256,128]{2,1,0:T(8,128)(2,1)S(1)}, u32[]{:S(2)}) copy-start(bf16[64,256,128]{2,1,0:T(8,128)(2,1)S(1)} %slots.1.weight_ref) | copy-start | bytes 12582916
  47.4 1.0 copy-start.10
  48.4 1.0 copy-start.12
  66.5 3.3 %copy-start.1 = (f32[16384,128]{1,0:T(8,128)}, f32[16384,128]{1,0:T(8,128)S(1)}, u32[]{:S(2)}) copy-start(f32[16384,128]{1,0:T(8,128)S(1)} %get-tuple-element.22._) | copy-start | bytes 25165828
  69.7 1.5 collective-permute-start.1
  70.1 7.6 %collective-permute-start = (f32[80,128]{1,0:T(8,128)S(1)}, f32[80,128]{1,0:T(8,128)S(1)}, u32[]{:S(2)}, u32[]{:S(2)}) collective-permute-start(f32[80,128]{1,0:T(8,128)S(1)} %get-tuple-element.18), channel_id=1, source_target_pairs={{1,0},{2,1},{3,2},{4,3},{5,4},{6,5},{7,6},{8,7},{9,8},{10,9},{11,1... | collective-permute-start | bytes 122888 | tf_op jit(solution)/shard_map/ppermute | solution.py:441
  77.8 14.3 %collective-permute-start.3 = (f32[48,128]{1,0:T(8,128)S(1)}, f32[48,128]{1,0:T(8,128)S(1)}, u32[]{:S(2)}, u32[]{:S(2)}) collective-permute-start(f32[48,128]{1,0:T(8,128)S(1)} %get-tuple-element.29), channel_id=1, source_target_pairs={{125,0},{126,1},{127,2},{0,3},{1,4},{2,5},{3,6},{4,7},{5,8},{6,9},... | collective-permute-start | bytes 73736 | tf_op jit(solution)/shard_map/ppermute | solution.py:441
  79.3 12.8 %collective-permute-start.2 = (f32[48,128]{1,0:T(8,128)S(1)}, f32[48,128]{1,0:T(8,128)S(1)}, u32[]{:S(2)}, u32[]{:S(2)}) collective-permute-start(f32[48,128]{1,0:T(8,128)S(1)} %get-tuple-element.30), channel_id=1, source_target_pairs={{3,0},{4,1},{5,2},{6,3},{7,4},{8,5},{9,6},{10,7},{11,8},{12,9},{13... | collective-permute-start | bytes 73736 | tf_op jit(solution)/shard_map/ppermute | solution.py:441
  92.1 3.4 %copy-start.2 = (f32[16384,128]{1,0:T(8,128)S(1)}, f32[16384,128]{1,0:T(8,128)}, u32[]{:S(2)}) copy-start(f32[16384,128]{1,0:T(8,128)} %copy-done.1) | copy-start | bytes 25165828
  95.5 2.2 %copy-start.4 = (bf16[64,256,128]{2,1,0:T(8,128)(2,1)S(1)}, bf16[64,256,128]{2,1,0:T(8,128)(2,1)}, u32[]{:S(2)}) copy-start(bf16[64,256,128]{2,1,0:T(8,128)(2,1)} %copy-done.3) | copy-start | bytes 12582916
  114.3 60.9 %copy-start.5 = (f32[2,8,128,128]{3,2,1,0:T(8,128)S(1)}, f32[2,8,128,128]{3,2,1,0:T(8,128)}, u32[]{:S(2)}) copy-start(f32[2,8,128,128]{3,2,1,0:T(8,128)} %coef_ref.3) | copy-start | bytes 3145732

commit v5 on v4

--- a/solution.py
+++ b/solution.py
@@ -20,6 +20,7 @@
 BF16 = jnp.bfloat16
 UNROLL = 4
 BATCH = 16
+CHUNK = 8
 TO_GRID = CUT ** -1.5
 TO_WAVES = GRID ** -1.5
 
@@ -147,16 +148,20 @@
         one_slot(i * 2 + 1)
         return carry
 
-    lax.fori_loop(0, (count_sm[0] + 1) // 2, two_slots, 0)
+    lax.fori_loop(0, (count_sm[0] + 3) // 4 * 2, two_slots, 0)
 
 
 def grid_kernel(
     rows_sm, count_sm,
-    recv_ref, pot_ref, value_ref, group_ref, window_ref,
+    pot_hbm, value_hbm, recv_ref, group_ref, window_ref,
     yh_ref, yl_ref, th_ref, tl_ref,
-    w_ref, partial_ref,
-    ah_s, al_s, ys_s, inha_s, inla_s, inhb_s, inlb_s, u_s, ga_s, gb_s, z_s,
+    field_hbm, partial_ref,
+    ah_s, al_s, ys_s, inha_s, inla_s, inhb_s, inlb_s, u_s, w_s, ga_s, gb_s, z_s, pot_ref, value_ref, sem, pot_sem, value_sem,
 ):
+    pot_copy = pltpu.make_async_copy(pot_hbm, pot_ref, pot_sem)
+    pot_copy.start()
+    value_copy = pltpu.make_async_copy(value_hbm, value_ref, value_sem)
+    value_copy.start()
     yh, yl = yh_ref[...], yl_ref[...]
     piece = lax.broadcasted_iota(jnp.int32, (32, 128), 0)
     pick_group = (lane_iota((32, 128)) % 8 == piece % 8).astype(F32).astype(BF16)
@@ -201,10 +206,13 @@
             u = res[:, k * 128:(k + 1) * 128]
             at = pl.multiple_of((zz * 32 + yg) * 256, 256)
             u_s[pl.ds(at, 256), :] = u
-            w_ref[pl.ds(at, 256), :] = u * spread
+            w_s[pl.ds(at, 256), :] = u * spread
 
     buffers = ((inha_s, inla_s), (inhb_s, inlb_s))
     for unit in range(-1, 4):
+        if unit == 0:
+            pot_copy.wait()
+
         def step(i, carry, unit=unit):
             if unit >= 0:
                 along_x(unit, i)
@@ -213,6 +221,8 @@
             return carry
 
         lax.fori_loop(0, 8, step, 0, unroll=UNROLL)
+    out_copy = pltpu.make_async_copy(w_s, field_hbm, sem)
+    out_copy.start()
     z_s[...] = jnp.zeros((SLOTS * 8, 128), F32)
     own = lane_iota((64, 128)) % 8 == lax.broadcasted_iota(jnp.int32, (64, 128), 0) // 8
 
@@ -244,6 +254,7 @@
         reduce_slot(s + 1, gb_s)
         return carry
 
+    value_copy.wait()
     pick(0, ga_s)
     lax.fori_loop(0, (count + 1) // 2, two_slots, 0)
     spread = exact_times_ones(z_s[...], block_ones())
@@ -252,17 +263,28 @@
     onehot = (lax.broadcasted_iota(jnp.int32, (WINDOW * 16, SLOTS), 0) == window_ref[...]).astype(F32).astype(BF16)
     a, b, c = three(slot_terms)
     partial_ref[...] = mm(onehot, a) + mm(onehot, b) + mm(onehot, c)
+    out_copy.wait()
 
 
 def back_kernel(
     rows_sm, count_sm,
     near_ref, after_ref, before_ref,
-    mask_ref, strength_ref, window_ref, weight_ref,
+    mask_ref, strength_ref, window_ref,
     yh_ref, yl_ref,
-    _,
-    out_ref, becp_ref, w_s,
-    tot_s, f_s, ta_s, tb_s, xa_s, xb_s, ah_s, al_s,
+    weight_hbm, field_hbm,
+    out_ref, becp_ref,
+    w_s, weight_ref, tot_s, f_s, ta_s, tb_s, tc_s, td_s, xa_s, xb_s, ah_s, al_s, sem, chunk_sem,
 ):
+    def chunk_copy(c):
+        part = pl.ds(c * CHUNK, CHUNK)
+        return pltpu.make_async_copy(weight_hbm.at[part], weight_ref.at[part], chunk_sem.at[c])
+
+    chunk_copy(0).start()
+    field_copy = pltpu.make_async_copy(field_hbm, w_s, sem)
+    field_copy.start()
+    for c in range(1, SLOTS // CHUNK):
+        chunk_copy(c).start()
+
     tot_s[...] = near_ref[16:96]
     tot_s[32:] = tot_s[32:] + after_ref[...]
     tot_s[:48] = tot_s[:48] + before_ref[...]
@@ -286,23 +308,42 @@
         both = mm(weight_ref[s], jnp.concatenate([pieces, pieces], 0))
         buf[...] = both[:, :128] + both[:, 128:]
 
-    def add_slot(s, buf):
-        for c in range(0, NPTS, BATCH):
-            at = [rows_sm[s * NPTS + c + k] for k in range(BATCH)]
-            vals = [w_s[pl.ds(at[k], 1), :] + buf[c + k:c + k + 1, :] for k in range(BATCH)]
-            for k in range(BATCH):
-                w_s[pl.ds(at[k], 1), :] = vals[k]
-
-    def two_slots(i, carry):
-        s = i * 2
-        terms_of(s + 1, tb_s)
-        add_slot(s, ta_s)
-        terms_of(jnp.minimum(s + 2, SLOTS - 1), ta_s)
-        add_slot(s + 1, tb_s)
+    def add_two(s, first, second):
+        for buf, slot in ((first, s), (second, s + 1)):
+            for c in range(0, NPTS, BATCH):
+                at = [rows_sm[slot * NPTS + c + k] for k in range(BATCH)]
+                vals = [w_s[pl.ds(at[k], 1), :] + buf[c + k:c + k + 1, :] for k in range(BATCH)]
+                for k in range(BATCH):
+                    w_s[pl.ds(at[k], 1), :] = vals[k]
+
+    def four_slots(i, carry):
+        s = i * 4
+        later = jnp.minimum(s + 4, SLOTS - 2)
+
+        @pl.when((lax.rem(i, 2) == 1) & (s + 4 < SLOTS))
+        def _():
+            chunk_copy((s + 4) // CHUNK).wait()
+
+        terms_of(s + 2, tc_s)
+        terms_of(s + 3, td_s)
+        add_two(s, ta_s, tb_s)
+        terms_of(later, ta_s)
+        terms_of(later + 1, tb_s)
+        add_two(s + 2, tc_s, td_s)
         return carry
 
+    fours = (count + 3) // 4
+    chunk_copy(0).wait()
     terms_of(0, ta_s)
-    lax.fori_loop(0, (count + 1) // 2, two_slots, 0)
+    terms_of(1, tb_s)
+    field_copy.wait()
+    lax.fori_loop(0, fours, four_slots, 0)
+
+    def drain(c, carry):
+        chunk_copy(c).wait()
+        return carry
+
+    lax.fori_loop(jnp.minimum(fours // 2, SLOTS // CHUNK - 1) + 1, SLOTS // CHUNK, drain, 0)
 
     def along_x(unit, pair):
         zz, half = unit // 2, unit % 2
@@ -360,8 +401,8 @@
 
 
 VM = pl.BlockSpec(memory_space=pltpu.VMEM)
+HBM = pl.BlockSpec(memory_space=pltpu.HBM)
 SM = pl.BlockSpec(memory_space=pltpu.SMEM)
-FIELD = pltpu.VMEM((ROWS, 128), F32)
 SEND = pltpu.VMEM((4096, 128), F32)
 
 
@@ -380,25 +421,27 @@
 def run_grid(rows, count, recv, pot, value, group, window):
     return pl.pallas_call(
         grid_kernel,
-        out_shape=(FIELD, pltpu.VMEM((WINDOW * 16, 128), F32)),
-        in_specs=[SM, SM] + [VM] * 9,
-        out_specs=(VM, VM),
+        out_shape=(jax.ShapeDtypeStruct((ROWS, 128), F32), pltpu.VMEM((WINDOW * 16, 128), F32)),
+        in_specs=[SM, SM, HBM, HBM] + [VM] * 7,
+        out_specs=(HBM, VM),
         scratch_shapes=[
             pltpu.VMEM((1024, 256), BF16), pltpu.VMEM((1024, 256), BF16),
             pltpu.VMEM((2, 1024, 512), F32),
             pltpu.VMEM((8, 256, 256), BF16), pltpu.VMEM((8, 256, 256), BF16),
             pltpu.VMEM((8, 256, 256), BF16), pltpu.VMEM((8, 256, 256), BF16),
-            pltpu.VMEM((ROWS, 128), F32),
+            pltpu.VMEM((ROWS, 128), F32), pltpu.VMEM((ROWS, 128), F32),
             pltpu.VMEM((NPTS, 128), F32), pltpu.VMEM((NPTS, 128), F32), pltpu.VMEM((SLOTS * 8, 128), F32),
+            pltpu.VMEM((2, GRID, GRID), F32), pltpu.VMEM((SLOTS, NPROJ, NPTS), F32),
+            pltpu.SemaphoreType.DMA(()), pltpu.SemaphoreType.DMA(()), pltpu.SemaphoreType.DMA(()),
         ],
-        compiler_params=params(24), name="grid",
-    )(rows, count, recv, pot, value, group, window, *TABLES["f"], *TABLES["ft"])
+        compiler_params=params(34), name="grid",
+    )(rows, count, pot, value, recv, group, window, *TABLES["f"], *TABLES["ft"])
 
 
 def run_slots(count, value, group, rowf):
     return pl.pallas_call(
         slots_kernel,
-        out_shape=pltpu.VMEM((SLOTS, NPTS, 128), BF16),
+        out_shape=pltpu.HBM((SLOTS, NPTS, 128), BF16),
         in_specs=[SM] + [VM] * 3, out_specs=VM, compiler_params=params(16), name="slots",
         cost_estimate=pl.CostEstimate(flops=10 ** 10, transcendentals=0, bytes_accessed=5 * 10 ** 6),
     )(count, value, group, rowf)
@@ -407,19 +450,21 @@
 def run_back(rows, count, partials, mask, strength, window, weights, field):
     return pl.pallas_call(
         back_kernel,
-        out_shape=(SEND, jax.ShapeDtypeStruct((16, 128), F32), FIELD),
-        in_specs=[SM, SM] + [VM] * 10,
-        out_specs=(VM, VM, VM),
-        input_output_aliases={11: 2},
+        out_shape=(SEND, jax.ShapeDtypeStruct((16, 128), F32)),
+        in_specs=[SM, SM] + [VM] * 8 + [HBM, HBM],
+        out_specs=(VM, VM),
         scratch_shapes=[
+            pltpu.VMEM((ROWS, 128), F32), pltpu.VMEM((SLOTS, NPTS, 128), BF16),
             pltpu.VMEM((WINDOW * 16, 128), F32),
             pltpu.VMEM((SLOTS * 8, 128), F32),
             pltpu.VMEM((NPTS, 128), F32), pltpu.VMEM((NPTS, 128), F32),
+            pltpu.VMEM((NPTS, 128), F32), pltpu.VMEM((NPTS, 128), F32),
             pltpu.VMEM((16, 128, 128), F32), pltpu.VMEM((16, 128, 128), F32),
             pltpu.VMEM((1024, 512), BF16), pltpu.VMEM((1024, 512), BF16),
+            pltpu.SemaphoreType.DMA(()), pltpu.SemaphoreType.DMA((SLOTS // CHUNK,)),
         ],
-        compiler_params=params(14), name="back",
-    )(rows, count, *partials, mask, strength, window, weights, *TABLES["f"], field)
+        compiler_params=params(28), name="back",
+    )(rows, count, *partials, mask, strength, window, *TABLES["f"], weights, field)
 
 
 def run_spectrum(recv, coef, kin):
@@ -459,7 +504,7 @@
     kinetic = 6.0 / (CUT * CUT) * ((freq_x * freq_x + freq * freq)[:, None] + (freq * freq)[None, :]).astype(F32)
 
     recv = to_all(run_columns(coefficients))
-    weights = pltpu.with_memory_space_constraint(run_slots(slot_count, proj_value, group, rowf), pltpu.VMEM)
+    weights = run_slots(slot_count, proj_value, group, rowf)
     prepared = (recv, rows, group, weights, window, strength, mask, kinetic)
     recv, rows, group, weights, window, strength, mask, kinetic = lax.optimization_barrier(prepared)
     field, partial = run_grid(rows, slot_count, recv, potential, proj_value, group, window)
@@ -467,8 +512,9 @@
     wide = wide + jnp.pad(from_offset(partial, 1), ((32, 0), (0, 0))) + jnp.pad(from_offset(partial, -1), ((0, 32), (0, 0)))
     partials = (wide, from_offset(wide[:48], 3), from_offset(wide[64:], -3))
     partials = [pltpu.with_memory_space_constraint(block, pltpu.VMEM) for block in partials]
-    field = pltpu.with_memory_space_constraint(field, pltpu.VMEM)
-    send, becp, _ = run_back(rows, slot_count, partials, mask, strength, window, weights, field)
+    field = pltpu.with_memory_space_constraint(field, pltpu.HBM)
+    weights = pltpu.with_memory_space_constraint(weights, pltpu.HBM)
+    send, becp = run_back(rows, slot_count, partials, mask, strength, window, weights, field)
     recv = to_all(send)
     return run_spectrum(recv, coefficients, kinetic), becp
 

time: 178 us -> 176 us (0.989)
  Pallas kernels: 42.5 us -> 68.1 us
  blocking collectives: 60.9 us -> 48.3 us
  local copies, waits for them, and re-layouts: 18.5 us -> 10.9 us
  starting transfers between devices: 25 us -> 19.3 us
    pallas_call x2, Pallas kernels: 18.7 us -> 32.1 us  [the longest x1 24.6 us: run_grid(): pl.pallas_call(grid_kernel, out_shape=(jax.ShapeDtypeStruct((ROWS, 128),...]
    all_to_all x1, blocking collectives: 60.9 us -> 48.3 us  [to_all(): lax.all_to_all(block, 'pencil', split_axis=0, concat_axis=0, tiled=True)]
    pallas_call x1, Pallas kernels: 16.7 us -> 28.9 us  [run_back(): pl.pallas_call(back_kernel, out_shape=(SEND, jax.ShapeDtypeStruct((16, 12...]
    unnamed x34 -> x28, local copies, waits for them, and re-layouts: 15.3 us -> 7.76 us
    ppermute x4, starting transfers between devices: 13.6 us -> 7.76 us  [from_offset(): lax.ppermute(block, 'pencil', [((i + delta) % n, i) for i in range(n)])]
    all_to_all x1, waiting for transfers between devices: 20.4 us -> 16.6 us  [to_all(): lax.all_to_all(block, 'pencil', split_axis=0, concat_axis=0, tiled=True)]
    ppermute x4, waiting for transfers between devices: 8.67 us -> 10.7 us  [from_offset(): lax.ppermute(block, 'pencil', [((i + delta) % n, i) for i in range(n)])]
  transfers between devices with their start and end apart: 5 -> 5, of which waited for: 4 -> 5; matrix products, arithmetic and copies ran while one was open for 3% -> 3% of each run, Pallas kernels for 1% -> 4%
where the time goes in v5:
time: 176 us
  Pallas kernels  68.1 us (39%)
  blocking collectives  48.3 us (27%)
  waiting for transfers between devices  27.3 us (16%)
  starting transfers between devices  19.3 us (11%)
  local copies, waits for them, and re-layouts  10.9 us (6%)
    all_to_all x1, blocking collectives, to_all(): lax.all_to_all(block, 'pencil', split_axis=0, concat_axis=0, tiled=True)  48.3 us
    pallas_call x1, Pallas kernels, run_back(): pl.pallas_call(back_kernel, out_shape=(SEND, jax.ShapeDtypeStruct((16, 12...  28.9 us
    pallas_call x1, Pallas kernels, run_grid(): pl.pallas_call(grid_kernel, out_shape=(jax.ShapeDtypeStruct((ROWS, 128),...  24.6 us
    all_to_all x1, waiting for transfers between devices, to_all(): lax.all_to_all(block, 'pencil', split_axis=0, concat_axis=0, tiled=True)  16.6 us
    all_to_all x1, starting transfers between devices, to_all(): lax.all_to_all(block, 'pencil', split_axis=0, concat_axis=0, tiled=True)  11.5 us
    ppermute x4, waiting for transfers between devices, from_offset(): lax.ppermute(block, 'pencil', [((i + delta) % n, i) for i in range(n)])  10.7 us
    unnamed x28, local copies, waits for them, and re-layouts  7.76 us
    ppermute x4, starting transfers between devices, from_offset(): lax.ppermute(block, 'pencil', [((i + delta) % n, i) for i in range(n)])  7.76 us
  transfers between devices with their start and end apart: 5, of which 5 were waited for; matrix products, arithmetic and copies ran while one was open for 3% of the time, Pallas kernels for 4%

profile of v5, /device:TPU:1, one launch (start us, length us, event | category | flops | bytes accessed | tf_op | source)
XLA Modules:
  0.0 175.6 jit_solution(9174489392647197466)
XLA Ops:
  0.6 0.0 copy-start
  0.6 4.7 %columns.1 = f32[4096,128]{1,0:T(8,128)} custom-call(f32[2,8,128,128]{3,2,1,0:T(8,128)} %coef_ref.3, bf16[512,256]{1,0:T(8,128)(2,1)} %constant.106.clone.th_ref, bf16[512,256]{1,0:T(8,128)(2,1)} %constant.107.clone.tl_ref), custom_call_target="tpu_custom_call" | custom-call | tf_op jit(solution)/shard_map/columns/pallas_call | solution.py:414
  5.3 0.0 copy-start.11
  5.3 0.0 copy-start.10
  5.3 11.5 %all-to-all-start = ((f32[128,32,128]{2,1,0:T(8,128)}), f32[128,32,128]{2,1,0:T(8,128)S(1)}, u32[]{:S(2)}, u32[]{:S(2)}) async-start(f32[128,32,128]{2,1,0:T(8,128)} %bitcast.18), calls=%async_computation | async-start | bytes 4194304 | tf_op jit(solution)/shard_map/all_to_all | solution.py:480
  16.8 0.0 copy-start.12
  16.9 0.0 copy-done.11
  17.6 0.0 copy-done.10
  17.6 1.3 copy.15
  18.9 0.0 copy-done
  18.9 1.1 gather_fusion.1
  20.1 1.8 %gather_fusion = f32[80,8]{1,0:T(8,128)S(1)} fusion(f32[2048,8]{1,0:T(8,128)} %copy.15, s32[1024]{0:T(1024)S(1)} %pad_clamp_fusion), kind=kCustom, calls=%fused_computation | custom fusion | bytes 5440 | tf_op jit(solution)/shard_map/gather | solution.py:500
  21.9 0.1 copy.16
  22.0 0.0 copy-done.12
  22.0 0.1 compare_convert_fusion.mask_ref
  22.1 0.1 convert_multiply_fusion.kin_ref
  22.2 0.0 copy-start.8
  22.2 1.0 copy-done.8
  23.3 0.0 copy-start.3
  23.3 0.0 copy-start.4
  23.3 0.0 copy-start.5
  23.3 0.0 copy-start.6
  23.3 7.5 %slots.1.weight_hbm = bf16[64,256,128]{2,1,0:T(8,128)(2,1)} custom-call(s32[1]{0:T(128)S(6)} %copy.19.count_sm, f32[64,8,256]{2,1,0:T(8,128)S(1)} %copy-done.8, s32[64,256]{1,0:T(8,128)S(1)} %get-tuple-element.16.group_ref, f32[64,256]{1,0:T(8,128)S(1)} %get-tuple-element.26.rowf_ref), custom_call_target="tpu_custom_call" | custom-call | flops 10000000000 | bytes 5000000 | tf_op jit(solution)/shard_map/slots/pallas_call | solution.py:442
  30.7 16.6 %all-to-all-done = f32[128,32,128]{2,1,0:T(8,128)S(1)} async-done(((f32[128,32,128]{2,1,0:T(8,128)}), f32[128,32,128]{2,1,0:T(8,128)S(1)}, u32[]{:S(2)}, u32[]{:S(2)}) %all-to-all-start) | async-done | bytes 2097184 | tf_op jit(solution)/shard_map/all_to_all | solution.py:480
  47.3 0.0 copy-done.3
  47.3 0.0 copy-done.4
  47.3 0.0 copy-done.5
  47.3 0.0 copy-done.6
  47.4 0.0 copy-start.7
  47.4 1.0 copy-done.7
  48.4 0.0 copy-start.9
  48.4 1.0 copy-done.9
  49.4 24.6 %grid.1 = (f32[16384,128]{1,0:T(8,128)S(1)}, f32[80,128]{1,0:T(8,128)S(1)}) custom-call(s32[16384]{0:T(1024)S(1)} %bitcast.16, s32[1]{0:T(128)S(6)} %copy.19.count_sm, f32[2,256,256]{2,1,0:T(8,128)S(1)} %copy-done.7, f32[64,8,256]{2,1,0:T(8,128)S(1)} %copy-done.9, f32[4096,128]{1,0:T(8,128)S(1)} %bitcast.13, s32[64,256]{1,0:T(8,128)S(1)} %get-tuple-element.16.group_ref, ...), custom_call_target="tpu_custom_call" | custom-call | tf_op jit(solution)/shard_map/grid/pallas_call | solution.py:422
  74.1 0.0 copy-start.1
  74.1 3.2 %copy-done.1 = f32[16384,128]{1,0:T(8,128)} copy-done((f32[16384,128]{1,0:T(8,128)}, f32[16384,128]{1,0:T(8,128)S(1)}, u32[]{:S(2)}) %copy-start.1) | copy-done | bytes 8388632
  77.3 0.0 collective-permute-start.1
  77.3 0.5 collective-permute-start
  77.8 0.7 collective-permute-done.1
  78.5 2.2 %collective-permute-done = f32[80,128]{1,0:T(8,128)S(1)} collective-permute-done((f32[80,128]{1,0:T(8,128)S(1)}, f32[80,128]{1,0:T(8,128)S(1)}, u32[]{:S(2)}, u32[]{:S(2)}) %collective-permute-start) | collective-permute-done | bytes 40992 | tf_op jit(solution)/shard_map/ppermute | solution.py:486
  80.8 0.5 collective-permute-start.3
  81.2 6.8 %collective-permute-start.2 = (f32[48,128]{1,0:T(8,128)S(1)}, f32[48,128]{1,0:T(8,128)S(1)}, u32[]{:S(2)}, u32[]{:S(2)}) collective-permute-start(f32[48,128]{1,0:T(8,128)S(1)} %get-tuple-element.30), channel_id=1, source_target_pairs={{3,0},{4,1},{5,2},{6,3},{7,4},{8,5},{9,6},{10,7},{11,8},{12,9},{13... | collective-permute-start | bytes 73736 | tf_op jit(solution)/shard_map/ppermute | solution.py:486
  88.0 0.1 copy.17.strength_ref
  88.1 1.4 collective-permute-done.3.before_ref
  89.5 6.4 %collective-permute-done.2.after_ref = f32[48,128]{1,0:T(8,128)S(1)} collective-permute-done((f32[48,128]{1,0:T(8,128)S(1)}, f32[48,128]{1,0:T(8,128)S(1)}, u32[]{:S(2)}, u32[]{:S(2)}) %collective-permute-start.2) | collective-permute-done | bytes 24608 | tf_op jit(solution)/shard_map/ppermute | solution.py:486
  95.9 28.9 %back.1 = (f32[4096,128]{1,0:T(8,128)S(1)}, f32[16,128]{1,0:T(8,128)}) custom-call(s32[16384]{0:T(1024)S(1)} %bitcast.17, s32[1]{0:T(128)S(6)} %copy.19.count_sm, f32[112,128]{1,0:T(8,128)S(1)} %pad_add_fusion.near_ref, f32[48,128]{1,0:T(8,128)S(1)} %collective-permute-done.2.after_ref, f32[48,128]{1,0:T(8,128)S(1)} %collective-permute-done.3.before_ref, ...), custom_call_target="tpu_custom_call" | custom-call | tf_op jit(solution)/shard_map/back/pallas_call | solution.py:451
  124.8 0.0 copy-start.2
  124.8 48.3 %all_to_all.10 = f32[128,32,128]{2,1,0:T(8,128)S(1)} all-to-all(f32[128,32,128]{2,1,0:T(8,128)S(1)} %bitcast.15), channel_id=1, replica_groups=mesh['pencil'=128] {'pencil'}, dimensions={0} | all-to-all | bytes 4194304 | tf_op jit(solution)/shard_map/all_to_all | solution.py:480
  173.1 0.0 copy-done.2
  173.1 2.5 %spectrum.1 = f32[2,8,128,128]{3,2,1,0:T(8,128)} custom-call(f32[4096,128]{1,0:T(8,128)S(1)} %bitcast.14, f32[2,8,128,128]{3,2,1,0:T(8,128)S(1)} %copy-done.2, f32[128,128]{1,0:T(8,128)S(1)} %convert_multiply_fusion.kin_ref, bf16[512,256]{1,0:T(8,128)(2,1)S(1)} %copy-done.4, bf16[512,256]{1,0:T(8,128)(2,1)S(1)} %copy-done.3), custom_call_target="tpu_custom_call" | custom-call | tf_op jit(solution)/shard_map/spectrum/pallas_call | solution.py:471
  (10 shorter events, 0.1 us)
Async XLA Ops:
  0.6 18.3 %copy-start = (s32[2048]{0:T(1024)S(1)}, s32[2048]{0:T(1024)}, u32[]{:S(2)}) copy-start(s32[2048]{0:T(1024)} %param.19) | copy-start | bytes 24580
  5.3 11.5 %copy-start.11 = (s32[64,256]{1,0:T(8,128)S(1)}, s32[64,256]{1,0:T(8,128)}, u32[]{:S(2)}) copy-start(s32[64,256]{1,0:T(8,128)} %param.16) | copy-start | bytes 196612
  5.3 12.3 %copy-start.10 = (f32[2048,8]{0,1:T(8,128)S(1)}, f32[2048,8]{0,1:T(8,128)}, u32[]{:S(2)}) copy-start(f32[2048,8]{0,1:T(8,128)} %param.18) | copy-start | bytes 196612
  5.3 42.0 %all-to-all-start = ((f32[128,32,128]{2,1,0:T(8,128)}), f32[128,32,128]{2,1,0:T(8,128)S(1)}, u32[]{:S(2)}, u32[]{:S(2)}) async-start(f32[128,32,128]{2,1,0:T(8,128)} %bitcast.18), calls=%async_computation | async-start | bytes 4194304 | tf_op jit(solution)/shard_map/all_to_all | solution.py:480
  16.8 5.2 %copy-start.12 = (s32[64]{0:T(128)S(1)}, s32[64]{0:T(128)}, u32[]{:S(2)}) copy-start(s32[64]{0:T(128)} %param.14) | copy-start | bytes 772
  22.2 1.0 copy-start.8
  23.3 24.1 %copy-start.3 = (bf16[512,256]{1,0:T(8,128)(2,1)S(1)}, bf16[512,256]{1,0:T(8,128)(2,1)}, u32[]{:S(2)}) copy-start(bf16[512,256]{1,0:T(8,128)(2,1)} %constant.107.clone.tl_ref) | copy-start | bytes 786436
  23.3 24.1 %copy-start.4 = (bf16[512,256]{1,0:T(8,128)(2,1)S(1)}, bf16[512,256]{1,0:T(8,128)(2,1)}, u32[]{:S(2)}) copy-start(bf16[512,256]{1,0:T(8,128)(2,1)} %constant.106.clone.th_ref) | copy-start | bytes 786436
  23.3 24.1 %copy-start.5 = (bf16[256,512]{1,0:T(8,128)(2,1)S(1)}, bf16[256,512]{1,0:T(8,128)(2,1)}, u32[]{:S(2)}) copy-start(bf16[256,512]{1,0:T(8,128)(2,1)} %constant.109.clone.yl_ref) | copy-start | bytes 786436
  23.3 24.1 %copy-start.6 = (bf16[256,512]{1,0:T(8,128)(2,1)S(1)}, bf16[256,512]{1,0:T(8,128)(2,1)}, u32[]{:S(2)}) copy-start(bf16[256,512]{1,0:T(8,128)(2,1)} %constant.108.clone.yh_ref) | copy-start | bytes 786436
  47.4 1.0 copy-start.7
  48.4 1.0 copy-start.9
  74.1 3.3 %copy-start.1 = (f32[16384,128]{1,0:T(8,128)}, f32[16384,128]{1,0:T(8,128)S(1)}, u32[]{:S(2)}) copy-start(f32[16384,128]{1,0:T(8,128)S(1)} %get-tuple-element.22.field_hbm) | copy-start | bytes 25165828
  77.3 1.2 collective-permute-start.1
  77.3 3.4 %collective-permute-start = (f32[80,128]{1,0:T(8,128)S(1)}, f32[80,128]{1,0:T(8,128)S(1)}, u32[]{:S(2)}, u32[]{:S(2)}) collective-permute-start(f32[80,128]{1,0:T(8,128)S(1)} %get-tuple-element.18), channel_id=1, source_target_pairs={{1,0},{2,1},{3,2},{4,3},{5,4},{6,5},{7,6},{8,7},{9,8},{10,9},{11,1... | collective-permute-start | bytes 122888 | tf_op jit(solution)/shard_map/ppermute | solution.py:486
  80.8 8.8 %collective-permute-start.3 = (f32[48,128]{1,0:T(8,128)S(1)}, f32[48,128]{1,0:T(8,128)S(1)}, u32[]{:S(2)}, u32[]{:S(2)}) collective-permute-start(f32[48,128]{1,0:T(8,128)S(1)} %get-tuple-element.29), channel_id=1, source_target_pairs={{125,0},{126,1},{127,2},{0,3},{1,4},{2,5},{3,6},{4,7},{5,8},{6,9},... | collective-permute-start | bytes 73736 | tf_op jit(solution)/shard_map/ppermute | solution.py:486
  81.2 14.7 %collective-permute-start.2 = (f32[48,128]{1,0:T(8,128)S(1)}, f32[48,128]{1,0:T(8,128)S(1)}, u32[]{:S(2)}, u32[]{:S(2)}) collective-permute-start(f32[48,128]{1,0:T(8,128)S(1)} %get-tuple-element.30), channel_id=1, source_target_pairs={{3,0},{4,1},{5,2},{6,3},{7,4},{8,5},{9,6},{10,7},{11,8},{12,9},{13... | collective-permute-start | bytes 73736 | tf_op jit(solution)/shard_map/ppermute | solution.py:486
  124.8 48.3 %copy-start.2 = (f32[2,8,128,128]{3,2,1,0:T(8,128)S(1)}, f32[2,8,128,128]{3,2,1,0:T(8,128)}, u32[]{:S(2)}) copy-start(f32[2,8,128,128]{3,2,1,0:T(8,128)} %coef_ref.3) | copy-start | bytes 3145732

commit v6 on v5

--- a/solution.py
+++ b/solution.py
@@ -18,7 +18,7 @@
 WINDOW = 2 * REACH + 1
 F32 = jnp.float32
 BF16 = jnp.bfloat16
-UNROLL = 4
+UNROLL = 8
 BATCH = 16
 CHUNK = 8
 TO_GRID = CUT ** -1.5
@@ -165,7 +165,7 @@
     yh, yl = yh_ref[...], yl_ref[...]
     piece = lax.broadcasted_iota(jnp.int32, (32, 128), 0)
     pick_group = (lane_iota((32, 128)) % 8 == piece % 8).astype(F32).astype(BF16)
-    for zz in range(2):
+    def along_y(zz):
         for b in range(BANDS):
             for r in range(2):
                 part = recv_ref[pl.ds(zz * 16 + r * 8 + b, 128, stride=32), :]
@@ -173,6 +173,8 @@
                 ah_s[b * 128:(b + 1) * 128, r * 128:(r + 1) * 128] = h
                 al_s[b * 128:(b + 1) * 128, r * 128:(r + 1) * 128] = l
         ys_s[zz] = mm_three_right(ah_s[...], al_s[...], yh, yl)
+
+    along_y(0)
 
     def permute(unit, kc):
         zz, half = unit // 2, unit % 2
@@ -212,6 +214,7 @@
     for unit in range(-1, 4):
         if unit == 0:
             pot_copy.wait()
+            along_y(1)
 
         def step(i, carry, unit=unit):
             if unit >= 0:
@@ -421,7 +424,7 @@
 def run_grid(rows, count, recv, pot, value, group, window):
     return pl.pallas_call(
         grid_kernel,
-        out_shape=(jax.ShapeDtypeStruct((ROWS, 128), F32), pltpu.VMEM((WINDOW * 16, 128), F32)),
+        out_shape=(pltpu.HBM((ROWS, 128), F32), pltpu.VMEM((WINDOW * 16, 128), F32)),
         in_specs=[SM, SM, HBM, HBM] + [VM] * 7,
         out_specs=(HBM, VM),
         scratch_shapes=[
@@ -507,7 +510,8 @@
     weights = run_slots(slot_count, proj_value, group, rowf)
     prepared = (recv, rows, group, weights, window, strength, mask, kinetic)
     recv, rows, group, weights, window, strength, mask, kinetic = lax.optimization_barrier(prepared)
-    field, partial = run_grid(rows, slot_count, recv, potential, proj_value, group, window)
+    in_hbm = [pltpu.with_memory_space_constraint(block, pltpu.HBM) for block in (potential, proj_value)]
+    field, partial = run_grid(rows, slot_count, recv, *in_hbm, group, window)
     wide = jnp.pad(partial, ((16, 16), (0, 0)))
     wide = wide + jnp.pad(from_offset(partial, 1), ((32, 0), (0, 0))) + jnp.pad(from_offset(partial, -1), ((0, 32), (0, 0)))
     partials = (wide, from_offset(wide[:48], 3), from_offset(wide[64:], -3))

time: 176 us -> 171 us (0.972); the launches traced: 176 us -> 173 us
  Pallas kernels: 68.1 us -> 45 us
  starting transfers between devices: 19.3 us -> 37 us
  blocking collectives: 48.3 us -> 59.6 us
  local copies, waits for them, and re-layouts: 10.9 us -> 5.56 us
  waiting for transfers between devices: 27.3 us -> 24.2 us
    ppermute x4, starting transfers between devices: 7.76 us -> 25.5 us  [from_offset(): lax.ppermute(block, 'pencil', [((i + delta) % n, i) for i in range(n)])]
    all_to_all x1, blocking collectives: 48.3 us -> 59.6 us  [to_all(): lax.all_to_all(block, 'pencil', split_axis=0, concat_axis=0, tiled=True)]
    pallas_call x1, Pallas kernels: 24.6 us -> 14.1 us  [run_grid(): pl.pallas_call(grid_kernel, out_shape=(pltpu.HBM((ROWS, 128), F32), pltpu...]
    pallas_call x1, Pallas kernels: 28.9 us -> 19.7 us  [run_back(): pl.pallas_call(back_kernel, out_shape=(SEND, jax.ShapeDtypeStruct((16, 12...]
    ppermute x4, waiting for transfers between devices: 10.7 us -> 4.14 us  [from_offset(): lax.ppermute(block, 'pencil', [((i + delta) % n, i) for i in range(n)])]
    unnamed x28 -> x22, local copies, waits for them, and re-layouts: 7.76 us -> 2.43 us
    pallas_call x1, Pallas kernels: 7.46 us -> 4.04 us  [run_slots(): pl.pallas_call(slots_kernel, out_shape=pltpu.HBM((SLOTS, NPTS, 128), BF16...]
    all_to_all x1, waiting for transfers between devices: 16.6 us -> 20 us  [to_all(): lax.all_to_all(block, 'pencil', split_axis=0, concat_axis=0, tiled=True)]
  transfers between devices with their start and end apart: 5 -> 5, of which waited for: 5 -> 5; matrix products, arithmetic and copies ran while one was open for 3% -> 3% of each run, Pallas kernels for 4% -> 2%
where the time goes in v6:
time: 171 us; the launch traced here: 173 us
  blocking collectives  59.6 us (35%)
  Pallas kernels  45 us (26%)
  starting transfers between devices  37 us (22%)
  waiting for transfers between devices  24.2 us (14%)
  local copies, waits for them, and re-layouts  5.56 us (3%)
    all_to_all x1, blocking collectives, to_all(): lax.all_to_all(block, 'pencil', split_axis=0, concat_axis=0, tiled=True)  59.6 us
    ppermute x4, starting transfers between devices, from_offset(): lax.ppermute(block, 'pencil', [((i + delta) % n, i) for i in range(n)])  25.5 us
    all_to_all x1, waiting for transfers between devices, to_all(): lax.all_to_all(block, 'pencil', split_axis=0, concat_axis=0, tiled=True)  20 us
    pallas_call x1, Pallas kernels, run_back(): pl.pallas_call(back_kernel, out_shape=(SEND, jax.ShapeDtypeStruct((16, 12...  19.7 us
    pallas_call x1, Pallas kernels, run_grid(): pl.pallas_call(grid_kernel, out_shape=(pltpu.HBM((ROWS, 128), F32), pltpu...  14.1 us
    all_to_all x1, starting transfers between devices, to_all(): lax.all_to_all(block, 'pencil', split_axis=0, concat_axis=0, tiled=True)  11.5 us
    pallas_call x1, Pallas kernels, run_columns(): pl.pallas_call(columns_kernel, out_shape=jax.ShapeDtypeStruct((4096, 128)...  4.68 us
    ppermute x4, waiting for transfers between devices, from_offset(): lax.ppermute(block, 'pencil', [((i + delta) % n, i) for i in range(n)])  4.14 us
  transfers between devices with their start and end apart: 5, of which 5 were waited for; matrix products, arithmetic and copies ran while one was open for 3% of the time, Pallas kernels for 2%

profile of v6, /device:TPU:1, one launch (start us, length us, event | category | flops | bytes accessed | tf_op | source)
XLA Modules:
  0.0 173.0 jit_solution(1024329009252375785)
XLA Ops:
  0.6 0.0 copy-start
  0.6 4.7 %columns.1 = f32[4096,128]{1,0:T(8,128)} custom-call(f32[2,8,128,128]{3,2,1,0:T(8,128)} %coef_ref.3, bf16[512,256]{1,0:T(8,128)(2,1)} %constant.106.clone.th_ref, bf16[512,256]{1,0:T(8,128)(2,1)} %constant.107.clone.tl_ref), custom_call_target="tpu_custom_call" | custom-call | tf_op jit(solution)/shard_map/columns/pallas_call | solution.py:417
  5.3 0.0 copy-start.8
  5.3 0.0 copy-start.7
  5.3 11.5 %all-to-all-start = ((f32[128,32,128]{2,1,0:T(8,128)}), f32[128,32,128]{2,1,0:T(8,128)S(1)}, u32[]{:S(2)}, u32[]{:S(2)}) async-start(f32[128,32,128]{2,1,0:T(8,128)} %bitcast.18), calls=%async_computation | async-start | bytes 4194304 | tf_op jit(solution)/shard_map/all_to_all | solution.py:483
  16.8 0.0 copy-start.9
  16.9 0.0 copy-done.8
  17.6 0.0 copy-done.7
  17.6 1.3 copy.15
  18.9 0.0 copy-done
  18.9 1.1 gather_fusion.1
  20.1 1.8 %gather_fusion = f32[80,8]{1,0:T(8,128)S(1)} fusion(f32[2048,8]{1,0:T(8,128)} %copy.15, s32[1024]{0:T(1024)S(1)} %pad_clamp_fusion), kind=kCustom, calls=%fused_computation | custom fusion | bytes 5440 | tf_op jit(solution)/shard_map/gather | solution.py:503
  21.9 0.1 copy.16
  22.0 0.0 copy-done.9
  22.0 0.1 compare_convert_fusion.mask_ref
  22.1 0.1 convert_multiply_fusion.kin_ref
  22.2 0.0 copy-start.6
  22.2 1.0 copy-done.6
  23.3 0.0 copy-start.2
  23.3 0.0 copy-start.3
  23.3 0.0 copy-start.4
  23.3 0.0 copy-start.5
  23.3 4.0 %slots.1.weight_hbm = bf16[64,256,128]{2,1,0:T(8,128)(2,1)} custom-call(s32[1]{0:T(128)S(6)} %copy.19.count_sm, f32[64,8,256]{2,1,0:T(8,128)S(1)} %copy-done.6, s32[64,256]{1,0:T(8,128)S(1)} %get-tuple-element.16.group_ref, f32[64,256]{1,0:T(8,128)S(1)} %get-tuple-element.26.rowf_ref), custom_call_target="tpu_custom_call" | custom-call | flops 10000000000 | bytes 5000000 | tf_op jit(solution)/shard_map/slots/pallas_call | solution.py:445
  27.3 20.0 %all-to-all-done = f32[128,32,128]{2,1,0:T(8,128)S(1)} async-done(((f32[128,32,128]{2,1,0:T(8,128)}), f32[128,32,128]{2,1,0:T(8,128)S(1)}, u32[]{:S(2)}, u32[]{:S(2)}) %all-to-all-start) | async-done | bytes 2097184 | tf_op jit(solution)/shard_map/all_to_all | solution.py:483
  47.3 0.0 copy-done.2
  47.3 0.0 copy-done.3
  47.4 0.0 copy-done.4
  47.4 0.0 copy-done.5
  47.4 14.1 %grid.1 = (f32[16384,128]{1,0:T(8,128)}, f32[80,128]{1,0:T(8,128)S(1)}) custom-call(s32[16384]{0:T(1024)S(1)} %bitcast.16, s32[1]{0:T(128)S(6)} %copy.19.count_sm, f32[2,256,256]{2,1,0:T(8,128)} %pot_hbm.1, f32[64,8,256]{2,1,0:T(8,128)} %value_hbm.1, f32[4096,128]{1,0:T(8,128)S(1)} %bitcast.13, s32[64,256]{1,0:T(8,128)S(1)} %get-tuple-element.16.group_ref, ...), custom_call_target="tpu_custom_call" | custom-call | tf_op jit(solution)/shard_map/grid/pallas_call | solution.py:425
  61.5 2.3 %collective-permute-start.1 = (f32[80,128]{1,0:T(8,128)S(1)}, f32[80,128]{1,0:T(8,128)S(1)}, u32[]{:S(2)}, u32[]{:S(2)}) collective-permute-start(f32[80,128]{1,0:T(8,128)S(1)} %get-tuple-element.18), channel_id=1, source_target_pairs={{127,0},{0,1},{1,2},{2,3},{3,4},{4,5},{5,6},{6,7},{7,8},{8,9},{9,1... | collective-permute-start | bytes 122888 | tf_op jit(solution)/shard_map/ppermute | solution.py:489
  63.8 15.9 %collective-permute-start = (f32[80,128]{1,0:T(8,128)S(1)}, f32[80,128]{1,0:T(8,128)S(1)}, u32[]{:S(2)}, u32[]{:S(2)}) collective-permute-start(f32[80,128]{1,0:T(8,128)S(1)} %get-tuple-element.18), channel_id=1, source_target_pairs={{1,0},{2,1},{3,2},{4,3},{5,4},{6,5},{7,6},{8,7},{9,8},{10,9},{11,1... | collective-permute-start | bytes 122888 | tf_op jit(solution)/shard_map/ppermute | solution.py:489
  79.7 0.6 collective-permute-done.1
  80.3 0.2 collective-permute-done
  80.6 0.1 collective-permute-start.3
  80.6 7.2 %collective-permute-start.2 = (f32[48,128]{1,0:T(8,128)S(1)}, f32[48,128]{1,0:T(8,128)S(1)}, u32[]{:S(2)}, u32[]{:S(2)}) collective-permute-start(f32[48,128]{1,0:T(8,128)S(1)} %get-tuple-element.30), channel_id=1, source_target_pairs={{3,0},{4,1},{5,2},{6,3},{7,4},{8,5},{9,6},{10,7},{11,8},{12,9},{13... | collective-permute-start | bytes 73736 | tf_op jit(solution)/shard_map/ppermute | solution.py:489
  87.8 0.1 copy.17.strength_ref
  87.9 1.4 collective-permute-done.3.before_ref
  89.3 1.8 %collective-permute-done.2.after_ref = f32[48,128]{1,0:T(8,128)S(1)} collective-permute-done((f32[48,128]{1,0:T(8,128)S(1)}, f32[48,128]{1,0:T(8,128)S(1)}, u32[]{:S(2)}, u32[]{:S(2)}) %collective-permute-start.2) | collective-permute-done | bytes 24608 | tf_op jit(solution)/shard_map/ppermute | solution.py:489
  91.2 19.7 %back.1 = (f32[4096,128]{1,0:T(8,128)S(1)}, f32[16,128]{1,0:T(8,128)}) custom-call(s32[16384]{0:T(1024)S(1)} %bitcast.17, s32[1]{0:T(128)S(6)} %copy.19.count_sm, f32[112,128]{1,0:T(8,128)S(1)} %pad_add_fusion.near_ref, f32[48,128]{1,0:T(8,128)S(1)} %collective-permute-done.2.after_ref, f32[48,128]{1,0:T(8,128)S(1)} %collective-permute-done.3.before_ref, ...), custom_call_target="tpu_custom_call" | custom-call | tf_op jit(solution)/shard_map/back/pallas_call | solution.py:454
  110.9 0.0 copy-start.1
  110.9 59.6 %all_to_all.10 = f32[128,32,128]{2,1,0:T(8,128)S(1)} all-to-all(f32[128,32,128]{2,1,0:T(8,128)S(1)} %bitcast.15), channel_id=1, replica_groups=mesh['pencil'=128] {'pencil'}, dimensions={0} | all-to-all | bytes 4194304 | tf_op jit(solution)/shard_map/all_to_all | solution.py:483
  170.5 0.0 copy-done.1
  170.5 2.5 %spectrum.1 = f32[2,8,128,128]{3,2,1,0:T(8,128)} custom-call(f32[4096,128]{1,0:T(8,128)S(1)} %bitcast.14, f32[2,8,128,128]{3,2,1,0:T(8,128)S(1)} %copy-done.1, f32[128,128]{1,0:T(8,128)S(1)} %convert_multiply_fusion.kin_ref, bf16[512,256]{1,0:T(8,128)(2,1)S(1)} %copy-done.3, bf16[512,256]{1,0:T(8,128)(2,1)S(1)} %copy-done.2), custom_call_target="tpu_custom_call" | custom-call | tf_op jit(solution)/shard_map/spectrum/pallas_call | solution.py:474
  (10 shorter events, 0.1 us)
Async XLA Ops:
  0.6 18.3 %copy-start = (s32[2048]{0:T(1024)S(1)}, s32[2048]{0:T(1024)}, u32[]{:S(2)}) copy-start(s32[2048]{0:T(1024)} %param.19) | copy-start | bytes 24580
  5.3 11.5 %copy-start.8 = (s32[64,256]{1,0:T(8,128)S(1)}, s32[64,256]{1,0:T(8,128)}, u32[]{:S(2)}) copy-start(s32[64,256]{1,0:T(8,128)} %param.16) | copy-start | bytes 196612
  5.3 12.3 %copy-start.7 = (f32[2048,8]{0,1:T(8,128)S(1)}, f32[2048,8]{0,1:T(8,128)}, u32[]{:S(2)}) copy-start(f32[2048,8]{0,1:T(8,128)} %param.18) | copy-start | bytes 196612
  5.3 42.0 %all-to-all-start = ((f32[128,32,128]{2,1,0:T(8,128)}), f32[128,32,128]{2,1,0:T(8,128)S(1)}, u32[]{:S(2)}, u32[]{:S(2)}) async-start(f32[128,32,128]{2,1,0:T(8,128)} %bitcast.18), calls=%async_computation | async-start | bytes 4194304 | tf_op jit(solution)/shard_map/all_to_all | solution.py:483
  16.8 5.2 %copy-start.9 = (s32[64]{0:T(128)S(1)}, s32[64]{0:T(128)}, u32[]{:S(2)}) copy-start(s32[64]{0:T(128)} %param.14) | copy-start | bytes 772
  22.2 1.0 copy-start.6
  23.3 24.1 %copy-start.2 = (bf16[512,256]{1,0:T(8,128)(2,1)S(1)}, bf16[512,256]{1,0:T(8,128)(2,1)}, u32[]{:S(2)}) copy-start(bf16[512,256]{1,0:T(8,128)(2,1)} %constant.107.clone.tl_ref) | copy-start | bytes 786436
  23.3 24.1 %copy-start.3 = (bf16[512,256]{1,0:T(8,128)(2,1)S(1)}, bf16[512,256]{1,0:T(8,128)(2,1)}, u32[]{:S(2)}) copy-start(bf16[512,256]{1,0:T(8,128)(2,1)} %constant.106.clone.th_ref) | copy-start | bytes 786436
  23.3 24.1 %copy-start.4 = (bf16[256,512]{1,0:T(8,128)(2,1)S(1)}, bf16[256,512]{1,0:T(8,128)(2,1)}, u32[]{:S(2)}) copy-start(bf16[256,512]{1,0:T(8,128)(2,1)} %constant.109.clone.yl_ref) | copy-start | bytes 786436
  23.3 24.1 %copy-start.5 = (bf16[256,512]{1,0:T(8,128)(2,1)S(1)}, bf16[256,512]{1,0:T(8,128)(2,1)}, u32[]{:S(2)}) copy-start(bf16[256,512]{1,0:T(8,128)(2,1)} %constant.108.clone.yh_ref) | copy-start | bytes 786436
  61.5 18.9 %collective-permute-start.1 = (f32[80,128]{1,0:T(8,128)S(1)}, f32[80,128]{1,0:T(8,128)S(1)}, u32[]{:S(2)}, u32[]{:S(2)}) collective-permute-start(f32[80,128]{1,0:T(8,128)S(1)} %get-tuple-element.18), channel_id=1, source_target_pairs={{127,0},{0,1},{1,2},{2,3},{3,4},{4,5},{5,6},{6,7},{7,8},{8,9},{9,1... | collective-permute-start | bytes 122888 | tf_op jit(solution)/shard_map/ppermute | solution.py:489
  63.8 16.8 %collective-permute-start = (f32[80,128]{1,0:T(8,128)S(1)}, f32[80,128]{1,0:T(8,128)S(1)}, u32[]{:S(2)}, u32[]{:S(2)}) collective-permute-start(f32[80,128]{1,0:T(8,128)S(1)} %get-tuple-element.18), channel_id=1, source_target_pairs={{1,0},{2,1},{3,2},{4,3},{5,4},{6,5},{7,6},{8,7},{9,8},{10,9},{11,1... | collective-permute-start | bytes 122888 | tf_op jit(solution)/shard_map/ppermute | solution.py:489
  80.6 8.8 %collective-permute-start.3 = (f32[48,128]{1,0:T(8,128)S(1)}, f32[48,128]{1,0:T(8,128)S(1)}, u32[]{:S(2)}, u32[]{:S(2)}) collective-permute-start(f32[48,128]{1,0:T(8,128)S(1)} %get-tuple-element.29), channel_id=1, source_target_pairs={{125,0},{126,1},{127,2},{0,3},{1,4},{2,5},{3,6},{4,7},{5,8},{6,9},... | collective-permute-start | bytes 73736 | tf_op jit(solution)/shard_map/ppermute | solution.py:489
  80.6 10.5 %collective-permute-start.2 = (f32[48,128]{1,0:T(8,128)S(1)}, f32[48,128]{1,0:T(8,128)S(1)}, u32[]{:S(2)}, u32[]{:S(2)}) collective-permute-start(f32[48,128]{1,0:T(8,128)S(1)} %get-tuple-element.30), channel_id=1, source_target_pairs={{3,0},{4,1},{5,2},{6,3},{7,4},{8,5},{9,6},{10,7},{11,8},{12,9},{13... | collective-permute-start | bytes 73736 | tf_op jit(solution)/shard_map/ppermute | solution.py:489
  110.9 59.6 %copy-start.1 = (f32[2,8,128,128]{3,2,1,0:T(8,128)S(1)}, f32[2,8,128,128]{3,2,1,0:T(8,128)}, u32[]{:S(2)}) copy-start(f32[2,8,128,128]{3,2,1,0:T(8,128)} %coef_ref.3) | copy-start | bytes 3145732

commit v7 on v6

--- a/solution.py
+++ b/solution.py
@@ -152,12 +152,14 @@
 
 
 def grid_kernel(
-    rows_sm, count_sm,
+    rows_hbm, count_sm,
     pot_hbm, value_hbm, recv_ref, group_ref, window_ref,
     yh_ref, yl_ref, th_ref, tl_ref,
     field_hbm, partial_ref,
-    ah_s, al_s, ys_s, inha_s, inla_s, inhb_s, inlb_s, u_s, w_s, ga_s, gb_s, z_s, pot_ref, value_ref, sem, pot_sem, value_sem,
+    ah_s, al_s, ys_s, inha_s, inla_s, inhb_s, inlb_s, u_s, w_s, ga_s, gb_s, z_s, pot_ref, value_ref, sem, pot_sem, value_sem, rows_sm, rows_sem,
 ):
+    rows_copy = pltpu.make_async_copy(rows_hbm, rows_sm, rows_sem)
+    rows_copy.start()
     pot_copy = pltpu.make_async_copy(pot_hbm, pot_ref, pot_sem)
     pot_copy.start()
     value_copy = pltpu.make_async_copy(value_hbm, value_ref, value_sem)
@@ -258,6 +260,7 @@
         return carry
 
     value_copy.wait()
+    rows_copy.wait()
     pick(0, ga_s)
     lax.fori_loop(0, (count + 1) // 2, two_slots, 0)
     spread = exact_times_ones(z_s[...], block_ones())
@@ -270,14 +273,16 @@
 
 
 def back_kernel(
-    rows_sm, count_sm,
+    rows_hbm, count_sm,
     near_ref, after_ref, before_ref,
     mask_ref, strength_ref, window_ref,
     yh_ref, yl_ref,
     weight_hbm, field_hbm,
     out_ref, becp_ref,
-    w_s, weight_ref, tot_s, f_s, ta_s, tb_s, tc_s, td_s, xa_s, xb_s, ah_s, al_s, sem, chunk_sem,
+    w_s, weight_ref, tot_s, f_s, ta_s, tb_s, tc_s, td_s, xa_s, xb_s, ah_s, al_s, sem, chunk_sem, rows_sm, rows_sem,
 ):
+    rows_copy = pltpu.make_async_copy(rows_hbm, rows_sm, rows_sem)
+    rows_copy.start()
     def chunk_copy(c):
         part = pl.ds(c * CHUNK, CHUNK)
         return pltpu.make_async_copy(weight_hbm.at[part], weight_ref.at[part], chunk_sem.at[c])
@@ -340,6 +345,7 @@
     terms_of(0, ta_s)
     terms_of(1, tb_s)
     field_copy.wait()
+    rows_copy.wait()
     lax.fori_loop(0, fours, four_slots, 0)
 
     def drain(c, carry):
@@ -425,7 +431,7 @@
     return pl.pallas_call(
         grid_kernel,
         out_shape=(pltpu.HBM((ROWS, 128), F32), pltpu.VMEM((WINDOW * 16, 128), F32)),
-        in_specs=[SM, SM, HBM, HBM] + [VM] * 7,
+        in_specs=[HBM, SM, HBM, HBM] + [VM] * 7,
         out_specs=(HBM, VM),
         scratch_shapes=[
             pltpu.VMEM((1024, 256), BF16), pltpu.VMEM((1024, 256), BF16),
@@ -436,6 +442,7 @@
             pltpu.VMEM((NPTS, 128), F32), pltpu.VMEM((NPTS, 128), F32), pltpu.VMEM((SLOTS * 8, 128), F32),
             pltpu.VMEM((2, GRID, GRID), F32), pltpu.VMEM((SLOTS, NPROJ, NPTS), F32),
             pltpu.SemaphoreType.DMA(()), pltpu.SemaphoreType.DMA(()), pltpu.SemaphoreType.DMA(()),
+            pltpu.SMEM((SLOTS * NPTS,), jnp.int32), pltpu.SemaphoreType.DMA(()),
         ],
         compiler_params=params(34), name="grid",
     )(rows, count, pot, value, recv, group, window, *TABLES["f"], *TABLES["ft"])
@@ -454,7 +461,7 @@
     return pl.pallas_call(
         back_kernel,
         out_shape=(SEND, jax.ShapeDtypeStruct((16, 128), F32)),
-        in_specs=[SM, SM] + [VM] * 8 + [HBM, HBM],
+        in_specs=[HBM, SM] + [VM] * 8 + [HBM, HBM],
         out_specs=(VM, VM),
         scratch_shapes=[
             pltpu.VMEM((ROWS, 128), F32), pltpu.VMEM((SLOTS, NPTS, 128), BF16),
@@ -465,6 +472,7 @@
             pltpu.VMEM((16, 128, 128), F32), pltpu.VMEM((16, 128, 128), F32),
             pltpu.VMEM((1024, 512), BF16), pltpu.VMEM((1024, 512), BF16),
             pltpu.SemaphoreType.DMA(()), pltpu.SemaphoreType.DMA((SLOTS // CHUNK,)),
+            pltpu.SMEM((SLOTS * NPTS,), jnp.int32), pltpu.SemaphoreType.DMA(()),
         ],
         compiler_params=params(28), name="back",
     )(rows, count, *partials, mask, strength, window, *TABLES["f"], weights, field)
@@ -510,6 +518,7 @@
     weights = run_slots(slot_count, proj_value, group, rowf)
     prepared = (recv, rows, group, weights, window, strength, mask, kinetic)
     recv, rows, group, weights, window, strength, mask, kinetic = lax.optimization_barrier(prepared)
+    rows = pltpu.with_memory_space_constraint(rows, pltpu.HBM)
     in_hbm = [pltpu.with_memory_space_constraint(block, pltpu.HBM) for block in (potential, proj_value)]
     field, partial = run_grid(rows, slot_count, recv, *in_hbm, group, window)
     wide = jnp.pad(partial, ((16, 16), (0, 0)))

time: 171 us -> 163 us (0.953); the launches traced: 173 us -> 162 us
  starting transfers between devices: 37 us -> 24.8 us
  blocking collectives: 59.6 us -> 62.3 us
  Pallas kernels: 45 us -> 42.6 us
    ppermute x4, starting transfers between devices: 25.5 us -> 13.3 us  [from_offset(): lax.ppermute(block, 'pencil', [((i + delta) % n, i) for i in range(n)])]
    all_to_all x1, blocking collectives: 59.6 us -> 62.3 us  [to_all(): lax.all_to_all(block, 'pencil', split_axis=0, concat_axis=0, tiled=True)]
  transfers between devices with their start and end apart: 5 -> 5, of which waited for: 5 -> 4; matrix products, arithmetic and copies ran while one was open for 3% -> 3% of each run, Pallas kernels for 2% -> 2%
where the time goes in v7:
time: 163 us; the launch traced here: 162 us
  blocking collectives  62.3 us (38%)
  Pallas kernels  42.6 us (26%)
  starting transfers between devices  24.8 us (15%)
  waiting for transfers between devices  24.5 us (15%)
  local copies, waits for them, and re-layouts  6.19 us (4%)
    all_to_all x1, blocking collectives, to_all(): lax.all_to_all(block, 'pencil', split_axis=0, concat_axis=0, tiled=True)  62.3 us
    all_to_all x1, waiting for transfers between devices, to_all(): lax.all_to_all(block, 'pencil', split_axis=0, concat_axis=0, tiled=True)  19.4 us
    pallas_call x1, Pallas kernels, run_back(): pl.pallas_call(back_kernel, out_shape=(SEND, jax.ShapeDtypeStruct((16, 12...  18.2 us
    ppermute x4, starting transfers between devices, from_offset(): lax.ppermute(block, 'pencil', [((i + delta) % n, i) for i in range(n)])  13.3 us
    pallas_call x1, Pallas kernels, run_grid(): pl.pallas_call(grid_kernel, out_shape=(pltpu.HBM((ROWS, 128), F32), pltpu...  13.1 us
    all_to_all x1, starting transfers between devices, to_all(): lax.all_to_all(block, 'pencil', split_axis=0, concat_axis=0, tiled=True)  11.5 us
    ppermute x4, waiting for transfers between devices, from_offset(): lax.ppermute(block, 'pencil', [((i + delta) % n, i) for i in range(n)])  5.11 us
    pallas_call x1, Pallas kernels, run_columns(): pl.pallas_call(columns_kernel, out_shape=jax.ShapeDtypeStruct((4096, 128)...  4.68 us
  transfers between devices with their start and end apart: 5, of which 4 were waited for; matrix products, arithmetic and copies ran while one was open for 3% of the time, Pallas kernels for 2%

profile of v7, /device:TPU:1, one launch (start us, length us, event | category | flops | bytes accessed | tf_op | source)
XLA Modules:
  0.0 162.1 jit_solution(15802678309682874561)
XLA Ops:
  0.6 0.0 copy-start
  0.6 4.7 %columns.1 = f32[4096,128]{1,0:T(8,128)} custom-call(f32[2,8,128,128]{3,2,1,0:T(8,128)} %coef_ref.3, bf16[512,256]{1,0:T(8,128)(2,1)} %constant.106.clone.th_ref, bf16[512,256]{1,0:T(8,128)(2,1)} %constant.107.clone.tl_ref), custom_call_target="tpu_custom_call" | custom-call | tf_op jit(solution)/shard_map/columns/pallas_call | solution.py:423
  5.3 0.0 copy-start.8
  5.3 0.0 copy-start.7
  5.3 11.5 %all-to-all-start = ((f32[128,32,128]{2,1,0:T(8,128)}), f32[128,32,128]{2,1,0:T(8,128)S(1)}, u32[]{:S(2)}, u32[]{:S(2)}) async-start(f32[128,32,128]{2,1,0:T(8,128)} %bitcast.16), calls=%async_computation | async-start | bytes 4194304 | tf_op jit(solution)/shard_map/all_to_all | solution.py:491
  16.8 0.0 copy-start.9
  16.9 0.0 copy-done.8
  17.6 0.7 copy.18
  18.2 0.0 copy-done.7
  18.2 1.3 copy.15
  19.6 0.0 copy-done
  19.6 1.1 gather_fusion.1
  20.7 1.8 %gather_fusion = f32[80,8]{1,0:T(8,128)S(1)} fusion(f32[2048,8]{1,0:T(8,128)} %copy.15, s32[1024]{0:T(1024)S(1)} %pad_clamp_fusion), kind=kCustom, calls=%fused_computation | custom fusion | bytes 5440 | tf_op jit(solution)/shard_map/gather | solution.py:511
  22.5 0.1 copy.16
  22.6 0.0 copy-done.9
  22.7 0.1 compare_convert_fusion.mask_ref
  22.7 0.1 convert_multiply_fusion.kin_ref
  22.8 0.0 copy-start.6
  22.9 1.0 copy-done.6
  23.9 0.0 copy-start.2
  23.9 0.0 copy-start.3
  23.9 0.0 copy-start.4
  23.9 0.0 copy-start.5
  23.9 4.0 %slots.1.weight_hbm = bf16[64,256,128]{2,1,0:T(8,128)(2,1)} custom-call(s32[1]{0:T(128)S(6)} %copy.19.count_sm, f32[64,8,256]{2,1,0:T(8,128)S(1)} %copy-done.6, s32[64,256]{1,0:T(8,128)S(1)} %get-tuple-element.16.group_ref, f32[64,256]{1,0:T(8,128)S(1)} %get-tuple-element.26.rowf_ref), custom_call_target="tpu_custom_call" | custom-call | flops 10000000000 | bytes 5000000 | tf_op jit(solution)/shard_map/slots/pallas_call | solution.py:452
  27.9 19.4 %all-to-all-done = f32[128,32,128]{2,1,0:T(8,128)S(1)} async-done(((f32[128,32,128]{2,1,0:T(8,128)}), f32[128,32,128]{2,1,0:T(8,128)S(1)}, u32[]{:S(2)}, u32[]{:S(2)}) %all-to-all-start) | async-done | bytes 2097184 | tf_op jit(solution)/shard_map/all_to_all | solution.py:491
  47.3 0.0 copy-done.2
  47.3 0.0 copy-done.3
  47.4 0.0 copy-done.4
  47.4 0.0 copy-done.5
  47.4 13.1 %grid.1 = (f32[16384,128]{1,0:T(8,128)}, f32[80,128]{1,0:T(8,128)S(1)}) custom-call(s32[16384]{0:T(1024)} %bitcast.17, s32[1]{0:T(128)S(6)} %copy.19.count_sm, f32[2,256,256]{2,1,0:T(8,128)} %pot_hbm.1, f32[64,8,256]{2,1,0:T(8,128)} %value_hbm.1, f32[4096,128]{1,0:T(8,128)S(1)} %bitcast.13, s32[64,256]{1,0:T(8,128)S(1)} %get-tuple-element.16.group_ref, ...), custom_call_target="tpu_custom_call" | custom-call | tf_op jit(solution)/shard_map/grid/pallas_call | solution.py:431
  60.5 6.1 %collective-permute-start.1 = (f32[80,128]{1,0:T(8,128)S(1)}, f32[80,128]{1,0:T(8,128)S(1)}, u32[]{:S(2)}, u32[]{:S(2)}) collective-permute-start(f32[80,128]{1,0:T(8,128)S(1)} %get-tuple-element.18), channel_id=1, source_target_pairs={{127,0},{0,1},{1,2},{2,3},{3,4},{4,5},{5,6},{6,7},{7,8},{8,9},{9,1... | collective-permute-start | bytes 122888 | tf_op jit(solution)/shard_map/ppermute | solution.py:497
  66.6 0.0 collective-permute-start
  66.6 1.1 collective-permute-done.1
  67.7 2.6 %collective-permute-done = f32[80,128]{1,0:T(8,128)S(1)} collective-permute-done((f32[80,128]{1,0:T(8,128)S(1)}, f32[80,128]{1,0:T(8,128)S(1)}, u32[]{:S(2)}, u32[]{:S(2)}) %collective-permute-start) | collective-permute-done | bytes 40992 | tf_op jit(solution)/shard_map/ppermute | solution.py:497
  70.3 0.1 collective-permute-start.3
  70.4 7.2 %collective-permute-start.2 = (f32[48,128]{1,0:T(8,128)S(1)}, f32[48,128]{1,0:T(8,128)S(1)}, u32[]{:S(2)}, u32[]{:S(2)}) collective-permute-start(f32[48,128]{1,0:T(8,128)S(1)} %get-tuple-element.30), channel_id=1, source_target_pairs={{3,0},{4,1},{5,2},{6,3},{7,4},{8,5},{9,6},{10,7},{11,8},{12,9},{13... | collective-permute-start | bytes 73736 | tf_op jit(solution)/shard_map/ppermute | solution.py:497
  77.6 0.1 copy.17.strength_ref
  77.6 1.4 collective-permute-done.3.before_ref
  79.1 0.0 collective-permute-done.2.after_ref
  79.1 18.2 %back.1 = (f32[4096,128]{1,0:T(8,128)S(1)}, f32[16,128]{1,0:T(8,128)}) custom-call(s32[16384]{0:T(1024)} %bitcast.18, s32[1]{0:T(128)S(6)} %copy.19.count_sm, f32[112,128]{1,0:T(8,128)S(1)} %pad_add_fusion.near_ref, f32[48,128]{1,0:T(8,128)S(1)} %collective-permute-done.2.after_ref, f32[48,128]{1,0:T(8,128)S(1)} %collective-permute-done.3.before_ref, ...), custom_call_target="tpu_custom_call" | custom-call | tf_op jit(solution)/shard_map/back/pallas_call | solution.py:461
  97.3 0.0 copy-start.1
  97.3 62.3 %all_to_all.10 = f32[128,32,128]{2,1,0:T(8,128)S(1)} all-to-all(f32[128,32,128]{2,1,0:T(8,128)S(1)} %bitcast.15), channel_id=1, replica_groups=mesh['pencil'=128] {'pencil'}, dimensions={0} | all-to-all | bytes 4194304 | tf_op jit(solution)/shard_map/all_to_all | solution.py:491
  159.6 0.0 copy-done.1
  159.6 2.5 %spectrum.1 = f32[2,8,128,128]{3,2,1,0:T(8,128)} custom-call(f32[4096,128]{1,0:T(8,128)S(1)} %bitcast.14, f32[2,8,128,128]{3,2,1,0:T(8,128)S(1)} %copy-done.1, f32[128,128]{1,0:T(8,128)S(1)} %convert_multiply_fusion.kin_ref, bf16[512,256]{1,0:T(8,128)(2,1)S(1)} %copy-done.3, bf16[512,256]{1,0:T(8,128)(2,1)S(1)} %copy-done.2), custom_call_target="tpu_custom_call" | custom-call | tf_op jit(solution)/shard_map/spectrum/pallas_call | solution.py:482
  (9 shorter events, 0.1 us)
Async XLA Ops:
  0.6 18.9 %copy-start = (s32[2048]{0:T(1024)S(1)}, s32[2048]{0:T(1024)}, u32[]{:S(2)}) copy-start(s32[2048]{0:T(1024)} %param.19) | copy-start | bytes 24580
  5.3 11.5 %copy-start.8 = (s32[64,256]{1,0:T(8,128)S(1)}, s32[64,256]{1,0:T(8,128)}, u32[]{:S(2)}) copy-start(s32[64,256]{1,0:T(8,128)} %param.16) | copy-start | bytes 196612
  5.3 12.9 %copy-start.7 = (f32[2048,8]{0,1:T(8,128)S(1)}, f32[2048,8]{0,1:T(8,128)}, u32[]{:S(2)}) copy-start(f32[2048,8]{0,1:T(8,128)} %param.18) | copy-start | bytes 196612
  5.3 42.0 %all-to-all-start = ((f32[128,32,128]{2,1,0:T(8,128)}), f32[128,32,128]{2,1,0:T(8,128)S(1)}, u32[]{:S(2)}, u32[]{:S(2)}) async-start(f32[128,32,128]{2,1,0:T(8,128)} %bitcast.16), calls=%async_computation | async-start | bytes 4194304 | tf_op jit(solution)/shard_map/all_to_all | solution.py:491
  16.8 5.8 %copy-start.9 = (s32[64]{0:T(128)S(1)}, s32[64]{0:T(128)}, u32[]{:S(2)}) copy-start(s32[64]{0:T(128)} %param.14) | copy-start | bytes 772
  22.8 1.0 copy-start.6
  23.9 23.5 %copy-start.2 = (bf16[512,256]{1,0:T(8,128)(2,1)S(1)}, bf16[512,256]{1,0:T(8,128)(2,1)}, u32[]{:S(2)}) copy-start(bf16[512,256]{1,0:T(8,128)(2,1)} %constant.107.clone.tl_ref) | copy-start | bytes 786436
  23.9 23.5 %copy-start.3 = (bf16[512,256]{1,0:T(8,128)(2,1)S(1)}, bf16[512,256]{1,0:T(8,128)(2,1)}, u32[]{:S(2)}) copy-start(bf16[512,256]{1,0:T(8,128)(2,1)} %constant.106.clone.th_ref) | copy-start | bytes 786436
  23.9 23.5 %copy-start.4 = (bf16[256,512]{1,0:T(8,128)(2,1)S(1)}, bf16[256,512]{1,0:T(8,128)(2,1)}, u32[]{:S(2)}) copy-start(bf16[256,512]{1,0:T(8,128)(2,1)} %constant.109.clone.yl_ref) | copy-start | bytes 786436
  23.9 23.5 %copy-start.5 = (bf16[256,512]{1,0:T(8,128)(2,1)S(1)}, bf16[256,512]{1,0:T(8,128)(2,1)}, u32[]{:S(2)}) copy-start(bf16[256,512]{1,0:T(8,128)(2,1)} %constant.108.clone.yh_ref) | copy-start | bytes 786436
  60.5 7.2 %collective-permute-start.1 = (f32[80,128]{1,0:T(8,128)S(1)}, f32[80,128]{1,0:T(8,128)S(1)}, u32[]{:S(2)}, u32[]{:S(2)}) collective-permute-start(f32[80,128]{1,0:T(8,128)S(1)} %get-tuple-element.18), channel_id=1, source_target_pairs={{127,0},{0,1},{1,2},{2,3},{3,4},{4,5},{5,6},{6,7},{7,8},{8,9},{9,1... | collective-permute-start | bytes 122888 | tf_op jit(solution)/shard_map/ppermute | solution.py:497
  66.6 3.7 %collective-permute-start = (f32[80,128]{1,0:T(8,128)S(1)}, f32[80,128]{1,0:T(8,128)S(1)}, u32[]{:S(2)}, u32[]{:S(2)}) collective-permute-start(f32[80,128]{1,0:T(8,128)S(1)} %get-tuple-element.18), channel_id=1, source_target_pairs={{1,0},{2,1},{3,2},{4,3},{5,4},{6,5},{7,6},{8,7},{9,8},{10,9},{11,1... | collective-permute-start | bytes 122888 | tf_op jit(solution)/shard_map/ppermute | solution.py:497
  70.3 8.8 %collective-permute-start.3 = (f32[48,128]{1,0:T(8,128)S(1)}, f32[48,128]{1,0:T(8,128)S(1)}, u32[]{:S(2)}, u32[]{:S(2)}) collective-permute-start(f32[48,128]{1,0:T(8,128)S(1)} %get-tuple-element.29), channel_id=1, source_target_pairs={{125,0},{126,1},{127,2},{0,3},{1,4},{2,5},{3,6},{4,7},{5,8},{6,9},... | collective-permute-start | bytes 73736 | tf_op jit(solution)/shard_map/ppermute | solution.py:497
  70.4 8.7 %collective-permute-start.2 = (f32[48,128]{1,0:T(8,128)S(1)}, f32[48,128]{1,0:T(8,128)S(1)}, u32[]{:S(2)}, u32[]{:S(2)}) collective-permute-start(f32[48,128]{1,0:T(8,128)S(1)} %get-tuple-element.30), channel_id=1, source_target_pairs={{3,0},{4,1},{5,2},{6,3},{7,4},{8,5},{9,6},{10,7},{11,8},{12,9},{13... | collective-permute-start | bytes 73736 | tf_op jit(solution)/shard_map/ppermute | solution.py:497
  97.3 62.3 %copy-start.1 = (f32[2,8,128,128]{3,2,1,0:T(8,128)S(1)}, f32[2,8,128,128]{3,2,1,0:T(8,128)}, u32[]{:S(2)}) copy-start(f32[2,8,128,128]{3,2,1,0:T(8,128)} %coef_ref.3) | copy-start | bytes 3145732
